TPU v7x, 32 devices: a whole 2x2x4 slice. The times are simulated.
32 devices in a mesh: replica: 4 (over x, core), group: 8 (over z, y).
Axes of the slice: x: 2, y: 2, z: 4, core: 2. Of those that a mesh axis runs over, the one named last changes fastest.
Arguments:
- tokens: bfloat16 [25216, 512], P(('replica', 'group')), may hold values from -6 to 6
- cotangent: bfloat16 [25216, 512], P(('replica', 'group')), may hold values from -6 to 6
- expert_index: int32 [25216, 2], P(('replica', 'group')), may hold values from 0 to 3, all different within a row; in each aligned block of 394 rows (0 to 393, 394 to 787, ...) at most 392 rows name the same one
- qkv_weight: float32 [512, 1536], P('group'), may hold values from -0.25 to 0.25
- out_weight: float32 [512, 512], P('group'), may hold values from -1.5 to 1.5
- router_weight: float32 [512, 4], P('group'), may hold values from -0.1875 to 0.1875
- up_weight: float32 [4, 512, 2048], P(None, 'group'), may hold values from -0.25 to 0.25
- up_bias: float32 [4, 2048], P(None, 'group'), may hold values from -0.5 to 0.5
- down_weight: float32 [4, 2048, 512], P(None, 'group'), may hold values from -0.5 to 0.5
- vectors: float32 [11, 512], P(None, 'group'), may hold values from -0.4 to 1.4, as said below
- qkv_moments: float32 [2, 512, 1536], P(None, 'group'), as said below
- out_moments: float32 [2, 512, 512], P(None, 'group'), as said below
- router_moments: float32 [2, 512, 4], P(None, 'group'), as said below
- up_moments: float32 [2, 4, 512, 2048], P(None, None, 'group'), as said below
- up_bias_moments: float32 [2, 4, 2048], P(None, None, 'group'), as said below
- down_moments: float32 [2, 4, 2048, 512], P(None, None, 'group'), as said below
- vector_moments: float32 [2, 11, 512], P(None, None, 'group'), as said below
Outputs:
- block_out: bfloat16 [25216, 512], P(('replica', 'group'))
- input_grad: float32 [25216, 512], P(('replica', 'group'))
- qkv_grad: float32 [512, 1536], P('group')
- out_grad: float32 [512, 512], P('group')
- router_grad: float32 [512, 4], P('group')
- up_grad: float32 [4, 512, 2048], P(None, 'group')
- up_bias_grad: float32 [4, 2048], P(None, 'group')
- down_grad: float32 [4, 2048, 512], P(None, 'group')
- vectors_grad: float32 [11, 512], P(None, 'group')
- qkv_new: float32 [512, 1536], P('group')
- out_new: float32 [512, 512], P('group')
- router_new: float32 [512, 4], P('group')
- up_new: float32 [4, 512, 2048], P(None, 'group')
- up_bias_new: float32 [4, 2048], P(None, 'group')
- down_new: float32 [4, 2048, 512], P(None, 'group')
- vectors_new: float32 [11, 512], P(None, 'group')
- qkv_moments_new: float32 [2, 512, 1536], P(None, 'group')
- out_moments_new: float32 [2, 512, 512], P(None, 'group')
- router_moments_new: float32 [2, 512, 4], P(None, 'group')
- up_moments_new: float32 [2, 4, 512, 2048], P(None, None, 'group')
- up_bias_moments_new: float32 [2, 4, 2048], P(None, None, 'group')
- down_moments_new: float32 [2, 4, 2048, 512], P(None, None, 'group')
- vector_moments_new: float32 [2, 11, 512], P(None, None, 'group')
Inputs may be any that keep to these rules, and one draw needn't show every extreme that they name: `expert_index`: in each aligned block of 394 rows (one micro-batch of one device) no expert is named by more than 392 rows; a row names two different experts. `vectors`: rows 0 and 5 are gains near one, the others biases near zero. `qkv_moments`: index 1 of the first dimension is positive. `out_moments`: index 1 of the first dimension is positive. `router_moments`: index 1 of the first dimension is positive. `up_moments`: index 1 of the first dimension is positive. `up_bias_moments`: index 1 of the first dimension is positive. `down_moments`: index 1 of the first dimension is positive. `vector_moments`: index 1 of the first dimension is positive.
All inputs are finite; a program needn't handle non-finite values.
Results may differ from a plain program's by a relative error of at most 0.019.
Values may be sent and summed in bfloat16 or wider, within the bound.
A program may use at most 256 MiB of HBM per device.

v0:
```python
import jax
import jax.numpy as jnp
from jax import lax
from jax.sharding import PartitionSpec as P

D = 512
HEADS = 8
HEAD_DIM = 64
F = 2048
E = 4
S = 197
MICRO = 2
IMG_MB = 2
CAP = 392


def layer_norm(value, gain, shift):
    center = value - jnp.mean(value, -1, keepdims=True)
    spread = jnp.mean(center * center, -1, keepdims=True)
    return center * lax.rsqrt(spread + 1e-06) * gain + shift


def gelu_exact(value):
    return jax.nn.gelu(value, approximate=False)


def assign_places(route):
    chosen = jnp.concatenate([route[:, 0], route[:, 1]])
    hits = (chosen[:, None] == jnp.arange(E, dtype=jnp.int32)[None, :]).astype(jnp.int32)
    before = jnp.cumsum(hits, 0) - hits
    slot = jnp.sum(before * hits, 1)
    return chosen * CAP + slot


def fetch_dense(qkv_weight, out_weight, router_weight, vectors):
    return (
        lax.all_gather(qkv_weight.astype(jnp.bfloat16), "group", axis=0, tiled=True),
        lax.all_gather(out_weight.astype(jnp.bfloat16), "group", axis=0, tiled=True),
        lax.all_gather(router_weight.astype(jnp.bfloat16), "group", axis=0, tiled=True),
        lax.all_gather(vectors.astype(jnp.bfloat16), "group", axis=1, tiled=True),
    )


def fetch_experts(up_weight, up_bias, down_weight):
    return (
        lax.all_gather(up_weight.astype(jnp.bfloat16), "group", axis=1, tiled=True),
        lax.all_gather(up_bias.astype(jnp.bfloat16), "group", axis=1, tiled=True),
        lax.all_gather(down_weight.astype(jnp.bfloat16), "group", axis=1, tiled=True),
    )


def split_heads(part):
    return part.reshape(IMG_MB, S, HEADS, HEAD_DIM)


def forward_block(dense, experts, value, route):
    w_qkv, w_out, w_router, table_b = dense
    w_up, b_up, w_down = experts
    table = table_b.astype(jnp.float32)
    rows = value.shape[0]
    scale = HEAD_DIM ** (-0.5)
    first = layer_norm(value, table[0], table[1]).astype(jnp.bfloat16)
    qkv_bias = jnp.concatenate([table[2], jnp.zeros((D,), jnp.float32), table[3]])
    qkv = (jnp.dot(first, w_qkv, preferred_element_type=jnp.float32) + qkv_bias).astype(
        jnp.bfloat16
    )
    query, key_part, val_part = (
        split_heads(qkv[:, :D]),
        split_heads(qkv[:, D : 2 * D]),
        split_heads(qkv[:, 2 * D :]),
    )
    scores = (
        jnp.einsum("bqhd,bkhd->bhqk", query, key_part, preferred_element_type=jnp.float32) * scale
    )
    peak = jnp.max(scores, -1, keepdims=True)
    expo = jnp.exp(scores - peak)
    total = jnp.sum(expo, -1, keepdims=True)
    probs_att = (expo / total).astype(jnp.bfloat16)
    log_total = peak + jnp.log(total)
    attended = jnp.einsum(
        "bhqk,bkhd->bqhd", probs_att, val_part, preferred_element_type=jnp.float32
    )
    attended = attended.reshape(rows, D).astype(jnp.bfloat16)
    resid = value + (jnp.dot(attended, w_out, preferred_element_type=jnp.float32) + table[4])
    second = layer_norm(resid, table[5], table[6]).astype(jnp.bfloat16)
    logits = jnp.dot(second, w_router, preferred_element_type=jnp.float32)
    probs = jax.nn.softmax(logits, -1)
    picked = route[:, :, None] == jnp.arange(E, dtype=jnp.int32)[None, None, :]
    gate = jnp.sum(jnp.where(picked, probs[:, None, :], 0.0), -1)
    places = assign_places(route)
    dispatch = (places[None, :] == jnp.arange(E * CAP, dtype=jnp.int32)[:, None]).astype(
        jnp.bfloat16
    )
    table_in = jnp.dot(
        dispatch, jnp.concatenate([second, second]), preferred_element_type=jnp.float32
    )
    table_in = table_in.astype(jnp.bfloat16).reshape(E, CAP, D)
    hidden_pre = (
        jnp.einsum("ecd,edf->ecf", table_in, w_up, preferred_element_type=jnp.float32)
        + b_up.astype(jnp.float32)[:, None, :]
    )
    hidden = gelu_exact(hidden_pre).astype(jnp.bfloat16)
    expert_out = (
        jnp.einsum("ecf,efd->ecd", hidden, w_down, preferred_element_type=jnp.float32)
        + table[7 : 7 + E][:, None, :]
    )
    expert_out = expert_out.reshape(E * CAP, D)
    out_zero = expert_out[places[:rows]]
    out_one = expert_out[places[rows:]]
    result = resid + (gate[:, 0:1] * out_zero + gate[:, 1:2] * out_one)
    kept = (
        first,
        qkv,
        log_total,
        attended,
        resid,
        second,
        probs,
        picked,
        gate,
        places,
        dispatch,
        table_in,
        hidden_pre,
        hidden,
        out_zero,
        out_one,
    )
    return (kept, result)


def backward_block(dense, experts, value, kept, d_out):
    w_qkv, w_out, w_router, table_b = dense
    w_up, b_up, w_down = experts
    table = table_b.astype(jnp.float32)
    (
        first,
        qkv,
        log_total,
        attended,
        resid,
        second,
        probs,
        picked,
        gate,
        places,
        dispatch,
        table_in,
        hidden_pre,
        hidden,
        out_zero,
        out_one,
    ) = kept
    rows = value.shape[0]
    scale = HEAD_DIM ** (-0.5)
    d_gate = jnp.stack([jnp.sum(d_out * out_zero, -1), jnp.sum(d_out * out_one, -1)], 1)
    weighted = jnp.concatenate([gate[:, 0:1] * d_out, gate[:, 1:2] * d_out]).astype(jnp.bfloat16)
    d_expert = (
        jnp.dot(dispatch, weighted, preferred_element_type=jnp.float32)
        .astype(jnp.bfloat16)
        .reshape(E, CAP, D)
    )
    g_bias_down = jnp.sum(d_expert.astype(jnp.float32), 1)
    g_down = jnp.einsum("ecf,ecd->efd", hidden, d_expert, preferred_element_type=jnp.float32)
    d_hidden = jnp.einsum("ecd,efd->ecf", d_expert, w_down, preferred_element_type=jnp.float32)
    gelu_pull = jax.vjp(gelu_exact, hidden_pre)[1]
    d_pre = gelu_pull(d_hidden)[0].astype(jnp.bfloat16)
    g_up_bias = jnp.sum(d_pre.astype(jnp.float32), 1)
    g_up = jnp.einsum("ecd,ecf->edf", table_in, d_pre, preferred_element_type=jnp.float32)
    d_table = jnp.einsum("ecf,edf->ecd", d_pre, w_up, preferred_element_type=jnp.float32).reshape(
        E * CAP, D
    )
    d_probs = jnp.sum(jnp.where(picked, d_gate[:, :, None], 0.0), 1)
    d_logit = (probs * (d_probs - jnp.sum(d_probs * probs, -1, keepdims=True))).astype(jnp.bfloat16)
    g_router = jnp.dot(second.T, d_logit, preferred_element_type=jnp.float32)
    d_second = (
        d_table[places[:rows]]
        + d_table[places[rows:]]
        + jnp.dot(d_logit, w_router.T, preferred_element_type=jnp.float32)
    )
    norm_pull = jax.vjp(layer_norm, resid, table[5], table[6])[1]
    d_resid, g_gain_two, g_shift_two = norm_pull(d_second)
    d_resid = d_out + d_resid
    d_branch = d_resid.astype(jnp.bfloat16)
    g_bias_out = jnp.sum(d_branch.astype(jnp.float32), 0)
    g_out = jnp.dot(attended.T, d_branch, preferred_element_type=jnp.float32)
    d_att = split_heads(
        jnp.dot(d_branch, w_out.T, preferred_element_type=jnp.float32).astype(jnp.bfloat16)
    )
    query, key_part, val_part = (
        split_heads(qkv[:, :D]),
        split_heads(qkv[:, D : 2 * D]),
        split_heads(qkv[:, 2 * D :]),
    )
    scores = (
        jnp.einsum("bqhd,bkhd->bhqk", query, key_part, preferred_element_type=jnp.float32) * scale
    )
    probs_f = jnp.exp(scores - log_total)
    probs_att = probs_f.astype(jnp.bfloat16)
    d_val = jnp.einsum("bhqk,bqhd->bkhd", probs_att, d_att, preferred_element_type=jnp.float32)
    d_prob = jnp.einsum("bqhd,bkhd->bhqk", d_att, val_part, preferred_element_type=jnp.float32)
    d_score = (probs_f * (d_prob - jnp.sum(d_prob * probs_f, -1, keepdims=True))).astype(
        jnp.bfloat16
    )
    d_query = (
        jnp.einsum("bhqk,bkhd->bqhd", d_score, key_part, preferred_element_type=jnp.float32) * scale
    )
    d_key = (
        jnp.einsum("bhqk,bqhd->bkhd", d_score, query, preferred_element_type=jnp.float32) * scale
    )
    d_qkv = jnp.concatenate(
        [d_query.reshape(rows, D), d_key.reshape(rows, D), d_val.reshape(rows, D)], 1
    ).astype(jnp.bfloat16)
    d_qkv_f = d_qkv.astype(jnp.float32)
    g_bias_q = jnp.sum(d_qkv_f[:, :D], 0)
    g_bias_v = jnp.sum(d_qkv_f[:, 2 * D :], 0)
    g_qkv = jnp.dot(first.T, d_qkv, preferred_element_type=jnp.float32)
    d_first = jnp.dot(d_qkv, w_qkv.T, preferred_element_type=jnp.float32)
    first_pull = jax.vjp(layer_norm, value, table[0], table[1])[1]
    d_input, g_gain_one, g_shift_one = first_pull(d_first)
    g_table = jnp.concatenate(
        [
            jnp.stack(
                [g_gain_one, g_shift_one, g_bias_q, g_bias_v, g_bias_out, g_gain_two, g_shift_two]
            ),
            g_bias_down,
        ],
        0,
    )
    grads = (g_qkv, g_out, g_router, g_up, g_up_bias, g_down, g_table)
    return (grads, d_resid + d_input)


def adamw(weight, moments, grad, rate):
    first = 0.5 * moments[0] + 0.5 * grad
    root = jnp.sqrt(0.5 * moments[1] * moments[1] + 0.5 * grad * grad)
    update = first / (root + 1e-08)
    return (weight - rate * (update + 0.1 * weight), jnp.stack([first, root]))


def shards(
    tokens,
    cotangent,
    expert_index,
    qkv_weight,
    out_weight,
    router_weight,
    up_weight,
    up_bias,
    down_weight,
    vectors,
    qkv_moments,
    out_moments,
    router_moments,
    up_moments,
    up_bias_moments,
    down_moments,
    vector_moments,
):
    rows = IMG_MB * S
    totals = None
    results = []
    input_grads = []
    for micro in range(MICRO):
        value = tokens[micro * rows : (micro + 1) * rows].astype(jnp.float32)
        route = expert_index[micro * rows : (micro + 1) * rows]
        d_out = cotangent[micro * rows : (micro + 1) * rows].astype(jnp.float32)
        dense = fetch_dense(qkv_weight, out_weight, router_weight, vectors)
        experts = fetch_experts(up_weight, up_bias, down_weight)
        kept, result = forward_block(dense, experts, value, route)
        results.append(result.astype(jnp.bfloat16))
        dense = fetch_dense(qkv_weight, out_weight, router_weight, vectors)
        experts = fetch_experts(up_weight, up_bias, down_weight)
        grads, d_input = backward_block(dense, experts, value, kept, d_out)
        input_grads.append(d_input)
        if totals is None:
            totals = grads
        else:
            totals = tuple((old + new for old, new in zip(totals, grads)))
    owned = (
        lax.psum_scatter(
            totals[0].astype(jnp.bfloat16), "group", scatter_dimension=0, tiled=True
        ).astype(jnp.float32),
        lax.psum_scatter(
            totals[1].astype(jnp.bfloat16), "group", scatter_dimension=0, tiled=True
        ).astype(jnp.float32),
        lax.psum_scatter(
            totals[2].astype(jnp.bfloat16), "group", scatter_dimension=0, tiled=True
        ).astype(jnp.float32),
        lax.psum_scatter(
            totals[3].astype(jnp.bfloat16), "group", scatter_dimension=1, tiled=True
        ).astype(jnp.float32),
        lax.psum_scatter(
            totals[4].astype(jnp.bfloat16), "group", scatter_dimension=1, tiled=True
        ).astype(jnp.float32),
        lax.psum_scatter(
            totals[5].astype(jnp.bfloat16), "group", scatter_dimension=1, tiled=True
        ).astype(jnp.float32),
        lax.psum_scatter(
            totals[6].astype(jnp.bfloat16), "group", scatter_dimension=1, tiled=True
        ).astype(jnp.float32),
    )
    reduced = (
        lax.psum(owned[0].astype(jnp.bfloat16), "replica").astype(jnp.float32),
        lax.psum(owned[1].astype(jnp.bfloat16), "replica").astype(jnp.float32),
        lax.psum(owned[2].astype(jnp.bfloat16), "replica").astype(jnp.float32),
        lax.psum(owned[3].astype(jnp.bfloat16), "replica").astype(jnp.float32),
        lax.psum(owned[4].astype(jnp.bfloat16), "replica").astype(jnp.float32),
        lax.psum(owned[5].astype(jnp.bfloat16), "replica").astype(jnp.float32),
        lax.psum(owned[6].astype(jnp.bfloat16), "replica").astype(jnp.float32),
    )
    rates = (
        2.0 * D ** (-0.5),
        2.0 * (D // 32) ** (-0.5),
        2.0 * (2 * D) ** (-0.5),
        2.0 * D ** (-0.5),
        0.2,
        2.0 * (F // 16) ** (-0.5),
        0.2,
    )
    params = (qkv_weight, out_weight, router_weight, up_weight, up_bias, down_weight, vectors)
    moments = (
        qkv_moments,
        out_moments,
        router_moments,
        up_moments,
        up_bias_moments,
        down_moments,
        vector_moments,
    )
    news = []
    states = []
    for weight, state, grad, rate in zip(params, moments, reduced, rates):
        new_weight, new_state = adamw(weight, state, grad, rate)
        news.append(new_weight)
        states.append(new_state)
    return (
        jnp.concatenate(results, 0),
        jnp.concatenate(input_grads, 0),
        reduced[0],
        reduced[1],
        reduced[2],
        reduced[3],
        reduced[4],
        reduced[5],
        reduced[6],
        news[0],
        news[1],
        news[2],
        news[3],
        news[4],
        news[5],
        news[6],
        states[0],
        states[1],
        states[2],
        states[3],
        states[4],
        states[5],
        states[6],
    )


def solution(mesh):
    in_specs = (
        P(("replica", "group"), None),
        P(("replica", "group"), None),
        P(("replica", "group"), None),
        P("group", None),
        P("group", None),
        P("group", None),
        P(None, "group", None),
        P(None, "group"),
        P(None, "group", None),
        P(None, "group"),
        P(None, "group", None),
        P(None, "group", None),
        P(None, "group", None),
        P(None, None, "group", None),
        P(None, None, "group"),
        P(None, None, "group", None),
        P(None, None, "group"),
    )
    out_specs = (
        P(("replica", "group"), None),
        P(("replica", "group"), None),
        P("group", None),
        P("group", None),
        P("group", None),
        P(None, "group", None),
        P(None, "group"),
        P(None, "group", None),
        P(None, "group"),
        P("group", None),
        P("group", None),
        P("group", None),
        P(None, "group", None),
        P(None, "group"),
        P(None, "group", None),
        P(None, "group"),
        P(None, "group", None),
        P(None, "group", None),
        P(None, "group", None),
        P(None, None, "group", None),
        P(None, None, "group"),
        P(None, None, "group", None),
        P(None, None, "group"),
    )
    return jax.shard_map(shards, mesh=mesh, in_specs=in_specs, out_specs=out_specs, check_vma=False)
```

profile of v0, /device:TPU:1, one launch (start us, length us, event | category | flops | bytes accessed | tf_op | source)
XLA Modules:
  0.0 1257.5 jit_solution(3630660267633276419)
XLA Ops:
  9.2 2.8 convert_element_type.273
  13.3 25.5 %all-gather = bf16[8,64,11]{1,2,0:T(8,128)(2,1)S(1)} all-gather(bf16[1,64,11]{1,2,0:T(8,128)(2,1)S(1)} %convert_bitcast_fusion), channel_id=1, replica_groups=mesh['replica'=4,'group'=8] {'group'}, dimensions={0}, use_global_device_ids=true | all-gather | bytes 12672 | tf_op jit(solution)/shard_map/all_gather | solution.py:40
  39.2 16.6 %all-gather.1 = bf16[8,64,4]{1,2,0:T(4,128)(2,1)S(1)} all-gather(bf16[1,64,4]{1,2,0:T(4,128)(2,1)S(1)} %convert_bitcast_fusion.1), channel_id=1, replica_groups=mesh['replica'=4,'group'=8] {'group'}, dimensions={0}, use_global_device_ids=true | all-gather | bytes 4608 | tf_op jit(solution)/shard_map/all_gather | solution.py:39
  59.8 22.3 %all_gather.19 = bf16[4,2048]{1,0:T(4,128)(2,1)S(1)} all-gather(bf16[4,256]{1,0:T(4,128)(2,1)S(1)} %convert_element_type.274), channel_id=1, replica_groups=mesh['replica'=4,'group'=8] {'group'}, dimensions={1}, use_global_device_ids=true | all-gather | bytes 18432 | tf_op jit(solution)/shard_map/all_gather | solution.py:47
  83.9 29.0 %all_gather.16 = bf16[512,512]{1,0:T(8,128)(2,1)} all-gather(bf16[64,512]{1,0:T(8,128)(2,1)S(1)} %convert_element_type.268), channel_id=1, replica_groups=mesh['replica'=4,'group'=8] {'group'}, dimensions={0}, use_global_device_ids=true | all-gather | bytes 589824 | tf_op jit(solution)/shard_map/all_gather | solution.py:38
  112.9 2.8 fusion.28
  121.0 1.9 multiply_reduce_fusion.2
  125.9 2.1 convert_element_type.285
  131.7 3.0 fusion.23
  134.7 53.9 %all-gather.8.cloned.1.call-done = bf16[4,512,2048]{2,1,0:T(8,128)(2,1)} async-done(((bf16[4,64,2048]{2,1,0:T(8,128)(2,1)}), bf16[4,512,2048]{2,1,0:T(8,128)(2,1)}) %all-gather.8.cloned.1.call-update) | async-done | bytes 8388624 | tf_op jit(solution)/shard_map/all_gather | solution.py:46
  188.6 11.4 fusion.19
  200.0 4.6 copy-done.7
  204.6 30.6 %multiply_convert_fusion = (bf16[4,392,2048]{2,1,0:T(8,128)(2,1)}, f32[4,392,2048]{2,1,0:T(8,128)}) fusion(f32[4,392,2048]{2,1,0:T(8,128)S(1)} %get-tuple-element.244, f32[4,2048]{1,0:T(4,128)S(1)} %convert_element_type.275, u8[392,2048]{1,0:T(8,128)(4,1)S(1)} %get-tuple-element.118, u8[392,2048]{1,0:T(8,128)(4,1)S(1)} %get-tuple-element.117), kind=kLoop, calls=%fused_computation.27 | loop fusion | flops 227999744 | bytes 33751040 | tf_op jit(solution)/shard_map/convert_element_type | solution.py:102
  235.2 80.0 %all-gather.10.cloned.1.call-done = bf16[4,2048,512]{2,1,0:T(8,128)(2,1)} async-done(((bf16[4,256,512]{2,1,0:T(8,128)(2,1)}), bf16[4,2048,512]{2,1,0:T(8,128)(2,1)}) %all-gather.10.cloned.1.call-update) | async-done | bytes 8388624 | tf_op jit(solution)/shard_map/all_gather | solution.py:48
  315.2 10.4 convolution_add_fusion.3
  325.6 4.6 gather_fusion.3
  330.2 4.7 gather_fusion.2
  334.9 1.9 fusion.105
  341.9 16.9 %convert_reduce_fusion = (f32[4,2048]{1,0:T(4,128)S(1)}, bf16[4,392,2048]{2,1,0:T(8,128)(2,1)}) fusion(f32[4,392,2048]{2,1,0:T(8,128)} %get-tuple-element.186, f32[4,392,2048]{2,1,0:T(8,128)} %copy-done.7, f32[4,2048]{1,0:T(4,128)S(1)} %convert_element_type.275, bf16[4,392,512]{2,1,0:T(8,128)(2,1)} %bitcast.308, ...), kind=kOutput, calls=%fused_computation.23 | convolution fusion | flops 3342917632 | bytes 42172416 | tf_op jit(solution)/shard_map/ecd,efd->ecf/dot_general | solution.py:165
  358.8 10.4 fusion.194
  369.3 4.5 gather_fusion.7
  373.8 4.6 gather_fusion.6
  378.4 2.3 multiply_reduce_fusion.4
  380.8 2.8 fusion.179
  386.4 2.6 reshape.505
  389.1 2.4 copy.249
  399.2 2.1 convert_element_type.324
  402.1 2.1 fusion.173
  410.5 1.9 multiply_reduce_fusion.3
  415.5 2.2 convert_element_type.267
  422.7 10.8 fusion.18
  433.6 30.7 %multiply_convert_fusion.1 = (bf16[4,392,2048]{2,1,0:T(8,128)(2,1)S(1)}, f32[4,392,2048]{2,1,0:T(8,128)}) fusion(f32[4,392,2048]{2,1,0:T(8,128)S(1)} %get-tuple-element.255, f32[4,2048]{1,0:T(4,128)S(1)} %convert_element_type.275, u8[392,2048]{1,0:T(8,128)(4,1)S(1)} %get-tuple-element.116, u8[392,2048]{1,0:T(8,128)(4,1)S(1)} %get-tuple-element.115), kind=kLoop, calls=%fused_computation.40 | loop fusion | flops 227999744 | bytes 33751040 | tf_op jit(solution)/shard_map/convert_element_type | solution.py:102
  464.3 11.0 convolution_add_fusion.4
  475.3 4.6 gather_fusion.1
  479.8 4.6 gather_fusion
  490.7 17.3 %convert_reduce_fusion.1 = (f32[4,2048]{1,0:T(4,128)S(1)}, bf16[4,392,2048]{2,1,0:T(8,128)(2,1)}) fusion(f32[4,392,2048]{2,1,0:T(8,128)} %get-tuple-element.182, f32[4,392,2048]{2,1,0:T(8,128)} %copy-done.8, f32[4,2048]{1,0:T(4,128)S(1)} %convert_element_type.275, bf16[4,392,512]{2,1,0:T(8,128)(2,1)} %bitcast.311, ...), kind=kOutput, calls=%fused_computation.24 | convolution fusion | flops 3342917632 | bytes 42172416 | tf_op jit(solution)/shard_map/ecd,efd->ecf/dot_general | solution.py:165
  508.0 10.4 fusion.193
  518.5 4.6 gather_fusion.5
  523.0 4.5 gather_fusion.4
  528.9 2.3 multiply_reduce_fusion.5
  535.4 2.3 reshape.504
  537.6 2.4 copy.237
  540.0 2.6 fusion.67
  560.7 2.8 fusion.166
  563.5 2.4 fusion.20
  566.3 12.5 fusion.198
  578.8 13.5 %add_convert_fusion = bf16[4,2048,512]{2,1,0:T(8,128)(2,1)} fusion(f32[4,2048,512]{2,1,0:T(8,128)} %fusion.198, bf16[4,392,2048]{2,1,0:T(8,128)(2,1)} %get-tuple-element.185, bf16[4,392,512]{2,1,0:T(8,128)(2,1)S(1)} %bitcast.309), kind=kOutput, calls=%fused_computation.10 | convolution fusion | flops 3296722944 | bytes 33193984 | tf_op jit(solution)/shard_map/ecf,ecd->efd/dot_general | solution.py:164
  593.8 11.0 fusion.197
  604.8 12.1 add_convert_fusion.1
  617.6 2.4 pad_maximum_fusion.3
  620.1 2.1 add_add_fusion.5
  624.5 44.7 %reduce-scatter.26.cloned.1.call-done = bf16[64,11]{1,0:T(8,128)(2,1)} async-done(((bf16[512,11]{1,0:T(8,128)(2,1)}), bf16[64,11]{1,0:T(8,128)(2,1)}) %reduce-scatter.26.cloned.1.call-update) | async-done | bytes 1424
  669.9 63.5 %reduce-scatter.24.cloned.1.call-done = bf16[256,4]{1,0:T(8,128)(2,1)} async-done(((bf16[2048,4]{1,0:T(8,128)(2,1)}), bf16[256,4]{1,0:T(8,128)(2,1)}) %reduce-scatter.24.cloned.1.call-update) | async-done | bytes 2064
  734.3 7.6 all-reduce.2
  742.7 56.0 %reduce-scatter.16.cloned.1.call-done = bf16[64,512]{1,0:T(8,128)(2,1)} async-done(((bf16[512,512]{1,0:T(8,128)(2,1)}), bf16[64,512]{1,0:T(8,128)(2,1)}) %reduce-scatter.16.cloned.1.call-update) | async-done | bytes 65552 | tf_op jit(solution)/shard_map/reduce_scatter | solution.py:284
  798.7 68.6 %reduce-scatter.14.cloned.1.call-done = bf16[64,1536]{1,0:T(8,128)(2,1)} async-done(((bf16[512,1536]{1,0:T(8,128)(2,1)}), bf16[64,1536]{1,0:T(8,128)(2,1)}) %reduce-scatter.14.cloned.1.call-update) | async-done | bytes 196624 | tf_op jit(solution)/shard_map/reduce_scatter | solution.py:281
  867.3 153.6 %reduce-scatter.20.cloned.1.call-done = bf16[4,256,512]{2,1,0:T(8,128)(2,1)} async-done(((bf16[4,2048,512]{2,1,0:T(8,128)(2,1)}), bf16[4,256,512]{2,1,0:T(8,128)(2,1)}) %reduce-scatter.20.cloned.1.call-update) | async-done | bytes 1048592 | tf_op jit(solution)/shard_map/reduce_scatter | solution.py:296
  1020.9 151.9 %reduce-scatter.18.cloned.1.call-done = bf16[4,64,2048]{2,1,0:T(8,128)(2,1)} async-done(((bf16[4,512,2048]{2,1,0:T(8,128)(2,1)}), bf16[4,64,2048]{2,1,0:T(8,128)(2,1)}) %reduce-scatter.18.cloned.1.call-update) | async-done | bytes 1048592 | tf_op jit(solution)/shard_map/reduce_scatter | solution.py:290
  1175.9 54.8 %all-reduce.6.cloned.1.call-done = (bf16[64,1536]{1,0:T(8,128)(2,1)}, bf16[64,512]{1,0:T(8,128)(2,1)}, bf16[4,64,2048]{2,1,0:T(8,128)(2,1)}, bf16[4,256,512]{2,1,0:T(8,128)(2,1)}) async-done(((bf16[64,1536]{1,0:T(8,128)(2,1)}, bf16[64,512]{1,0:T(8,128)(2,1)}, bf16[4,64,2048]{2,1,0:T(8,128)(2,1)}, bf16[4,256,512]{2,1,0:T(8,128)(2,1)}), (bf16[64,1536]{1,0:T(8,128)(2,1)}, bf16[64,512]{1,0:T(8,128)(2,1)}, ...) | async-done | bytes 2359312 | tf_op jit(solution)/shard_map/psum | solution.py:304
  1234.5 2.0 fusion.119
  1236.6 2.7 fusion.126
  1241.5 2.8 fusion.125
  1245.9 2.3 pad_maximum_fusion
  1248.2 2.5 pad_maximum_fusion.1
  (391 shorter events, 98.6 us)
Async XLA Ops:
  7.2 4.9 copy-start.19
  7.2 105.7 %all-gather.6.cloned.1.call-start = ((), (), s32[]{:S(2)}) async-start(), calls=%async_computation.7 | async-start | bytes 1769472 | tf_op jit(solution)/shard_map/all_gather | solution.py:37
  9.1 4.2 copy-start.71
  9.1 29.8 %copy-start.89 = (f32[64,4]{0,1:T(4,128)S(1)}, f32[64,4]{0,1:T(4,128)}, u32[]{:S(2)}) copy-start(f32[64,4]{0,1:T(4,128)} %param.22) | copy-start | bytes 3076
  9.1 29.8 %copy-start.80 = (f32[4,256]{1,0:T(4,128)S(1)}, f32[4,256]{1,0:T(4,128)}, u32[]{:S(2)}) copy-start(f32[4,256]{1,0:T(4,128)} %param.24) | copy-start | bytes 12292
  9.1 29.8 %copy-start.21 = (bf16[788,512]{1,0:T(8,128)(2,1)S(1)}, bf16[788,512]{1,0:T(8,128)(2,1)}, u32[]{:S(2)}) copy-start(bf16[788,512]{1,0:T(8,128)(2,1)} %param.17) | copy-start | bytes 2420740
  9.2 46.7 %copy-start.68 = (s32[788,2]{0,1:T(2,128)S(1)}, s32[788,2]{0,1:T(2,128)}, u32[]{:S(2)}) copy-start(s32[788,2]{0,1:T(2,128)} %param.19) | copy-start | bytes 18916
  9.2 73.0 %copy-start.66 = (f32[64,512]{1,0:T(8,128)S(1)}, f32[64,512]{1,0:T(8,128)}, u32[]{:S(2)}) copy-start(f32[64,512]{1,0:T(8,128)} %param.21) | copy-start | bytes 393220
  9.2 179.4 %all-gather.8.cloned.1.call-start = ((), (), s32[]{:S(2)}) async-start(), calls=%async_computation.8 | async-start | bytes 9437184 | tf_op jit(solution)/shard_map/all_gather | solution.py:46
  12.0 303.2 %all-gather.10.cloned.1.call-start = ((), (), s32[]{:S(2)}) async-start(), calls=%async_computation.9 | async-start | bytes 9437184 | tf_op jit(solution)/shard_map/all_gather | solution.py:48
  13.2 610.5 %reduce-scatter.22.cloned.1.call-start = ((), (), s32[]{:S(2)}) async-start(), calls=%async_computation.14 | async-start | bytes 147456
  83.2 32.5 %copy-start.75 = (f32[394]{0:T(512)}, f32[394]{0:T(512)S(1)}, u32[]{:S(2)}) copy-start(f32[394]{0:T(512)S(1)} %get-tuple-element.145) | copy-start | bytes 4732
  83.3 32.5 %copy-start.86 = (f32[394]{0:T(512)}, f32[394]{0:T(512)S(1)}, u32[]{:S(2)}) copy-start(f32[394]{0:T(512)S(1)} %get-tuple-element.260) | copy-start | bytes 4732
  200.0 4.6 copy-start.7
  378.4 5.3 copy-start.1
  378.4 6.9 copy-start.35
  383.6 9.7 copy-start.73
  399.2 5.0 copy-start.48
  422.7 10.9 copy-start.58
  433.6 30.7 %copy-start.8 = (f32[4,392,2048]{2,1,0:T(8,128)}, f32[4,392,2048]{2,1,0:T(8,128)S(1)}, u32[]{:S(2)}) copy-start(f32[4,392,2048]{2,1,0:T(8,128)S(1)} %get-tuple-element.255) | copy-start | bytes 38535172
  464.3 11.0 copy-start
  464.3 11.0 copy-start.83
  475.2 4.6 copy-start.82
  479.8 6.4 copy-start.78
  527.6 3.7 copy-start.6
  527.6 3.7 copy-start.29
  527.6 3.7 copy-start.30
  527.6 4.9 copy-start.2
  528.9 5.2 copy-start.36
  544.7 3.4 copy-start.52
  547.9 121.3 %reduce-scatter.26.cloned.1.call-start = ((), (), s32[]{:S(2)}) async-start(), calls=%async_computation.16 | async-start | bytes 147456
  550.9 3.9 copy-start.50
  554.8 4.6 copy-start.40
  554.8 4.6 copy-start.51
  556.7 176.7 %reduce-scatter.24.cloned.1.call-start = ((), (), s32[]{:S(2)}) async-start(), calls=%async_computation.15 | async-start | bytes 589824
  559.3 239.4 %reduce-scatter.16.cloned.1.call-start = ((), (), s32[]{:S(2)}) async-start(), calls=%async_computation.11 | async-start | bytes 589824 | tf_op jit(solution)/shard_map/reduce_scatter | solution.py:284
  560.7 306.6 %reduce-scatter.14.cloned.1.call-start = ((), (), s32[]{:S(2)}) async-start(), calls=%async_computation.10 | async-start | bytes 1769472 | tf_op jit(solution)/shard_map/reduce_scatter | solution.py:281
  566.0 12.8 %copy-start.10 = (bf16[1568,512]{1,0:T(8,128)(2,1)S(1)}, bf16[1568,512]{1,0:T(8,128)(2,1)}, u32[]{:S(2)}) copy-start(bf16[1568,512]{1,0:T(8,128)(2,1)} %copy-done.9) | copy-start | bytes 4816900
  566.0 454.8 %reduce-scatter.20.cloned.1.call-start = ((), (), s32[]{:S(2)}) async-start(), calls=%async_computation.13 | async-start | bytes 9437184 | tf_op jit(solution)/shard_map/reduce_scatter | solution.py:296
  592.4 12.4 copy-start.46
  592.4 580.4 %reduce-scatter.18.cloned.1.call-start = ((), (), s32[]{:S(2)}) async-start(), calls=%async_computation.12 | async-start | bytes 9437184 | tf_op jit(solution)/shard_map/reduce_scatter | solution.py:290
  616.9 3.2 copy-start.3
  616.9 3.2 copy-start.24
  616.9 3.2 copy-start.26
  616.9 3.2 copy-start.28
  616.9 3.2 copy-start.74
  617.0 613.7 %all-reduce.6.cloned.1.call-start = ((), (), s32[]{:S(2)}) async-start(), calls=%async_computation.17 | async-start | bytes 4718592 | tf_op jit(solution)/shard_map/psum | solution.py:304
  620.1 121.9 %copy-start.72 = (f32[11,64]{1,0:T(8,128)S(1)}, f32[11,64]{1,0:T(8,128)}, u32[]{:S(2)}) copy-start(f32[11,64]{1,0:T(8,128)} %param.26) | copy-start | bytes 8452
  622.3 551.2 %copy-start.85 = (f32[2,64,4]{1,2,0:T(4,128)S(1)}, f32[2,64,4]{1,2,0:T(4,128)}, u32[]{:S(2)}) copy-start(f32[2,64,4]{1,2,0:T(4,128)} %param.29) | copy-start | bytes 6148
  622.3 551.2 %copy-start.90 = (f32[64,4]{0,1:T(4,128)S(1)}, f32[64,4]{0,1:T(4,128)}, u32[]{:S(2)}) copy-start(f32[64,4]{0,1:T(4,128)} %param.22) | copy-start | bytes 3076
  622.3 552.4 %copy-start.77 = (f32[2,4,256]{2,1,0:T(4,128)S(1)}, f32[2,4,256]{2,1,0:T(4,128)}, u32[]{:S(2)}) copy-start(f32[2,4,256]{2,1,0:T(4,128)} %param.31) | copy-start | bytes 24580
  622.3 552.4 %copy-start.81 = (f32[4,256]{1,0:T(4,128)S(1)}, f32[4,256]{1,0:T(4,128)}, u32[]{:S(2)}) copy-start(f32[4,256]{1,0:T(4,128)} %param.24) | copy-start | bytes 12292
  622.3 608.3 %copy-start.64 = (f32[2,64,512]{2,1,0:T(8,128)S(1)}, f32[2,64,512]{2,1,0:T(8,128)}, u32[]{:S(2)}) copy-start(f32[2,64,512]{2,1,0:T(8,128)} %param.28) | copy-start | bytes 786436
  622.3 609.4 %copy-start.67 = (f32[64,512]{1,0:T(8,128)S(1)}, f32[64,512]{1,0:T(8,128)}, u32[]{:S(2)}) copy-start(f32[64,512]{1,0:T(8,128)} %param.21) | copy-start | bytes 393220
  622.3 610.1 %copy-start.57 = (f32[2,64,1536]{2,1,0:T(8,128)S(1)}, f32[2,64,1536]{2,1,0:T(8,128)}, u32[]{:S(2)}) copy-start(f32[2,64,1536]{2,1,0:T(8,128)} %param.27) | copy-start | bytes 2359300
  622.3 611.1 %copy-start.60 = (f32[64,1536]{1,0:T(8,128)S(1)}, f32[64,1536]{1,0:T(8,128)}, u32[]{:S(2)}) copy-start(f32[64,1536]{1,0:T(8,128)} %param.20) | copy-start | bytes 1179652
  742.0 494.5 %copy-start.70 = (f32[11,64]{1,0:T(8,128)}, f32[11,64]{1,0:T(8,128)S(1)}, u32[]{:S(2)}) copy-start(f32[11,64]{1,0:T(8,128)S(1)} %get-tuple-element.158) | copy-start | bytes 8452
  1173.4 63.1 %copy-start.88 = (f32[64,4]{0,1:T(4,128)}, f32[64,4]{0,1:T(4,128)S(1)}, u32[]{:S(2)}) copy-start(f32[64,4]{0,1:T(4,128)S(1)} %get-tuple-element.166) | copy-start | bytes 3076
  1174.7 61.9 %copy-start.79 = (f32[4,256]{1,0:T(4,128)}, f32[4,256]{1,0:T(4,128)S(1)}, u32[]{:S(2)}) copy-start(f32[4,256]{1,0:T(4,128)S(1)} %get-tuple-element.162) | copy-start | bytes 12292
  1230.7 3.9 copy-start.13
  1231.7 4.9 copy-start.65
  1233.5 3.1 copy-start.61
  1236.6 3.7 copy-start.14
  1236.6 4.0 copy-start.62
  (40 other events, 72.3 us)
Sparse Core Ops, SparseCore 0:
  10.8 45.8 all-gather.5
  59.4 129.1 all-gather.7
  191.3 123.8 all-gather.9
  548.0 57.4 reduce-scatter.21
  609.3 59.8 reduce-scatter.25
  672.3 61.0 reduce-scatter.23
  737.7 60.9 reduce-scatter.15
  802.7 64.5 reduce-scatter.13
  871.3 149.4 reduce-scatter.19
  1024.3 148.3 reduce-scatter.17
  1175.6 55.0 all-reduce.5
where the time goes:
time: 1260 us
  waiting for transfers between devices  727 us (58%)
  matrix products  199 us (16%)
  other arithmetic  118 us (9%)
  blocking collectives  101 us (8%)
  local copies, waits for them, and re-layouts  95.3 us (8%)
  between operations  15.8 us (1%)
    reduce_scatter x1, waiting for transfers between devices, shards(): lax.psum_scatter(totals[5].astype(jnp.bfloat16), 'group', scatter_dimensi...  154 us
    reduce_scatter x1, waiting for transfers between devices, shards(): lax.psum_scatter(totals[3].astype(jnp.bfloat16), 'group', scatter_dimensi...  152 us
    unnamed x14, waiting for transfers between devices  108 us
    all_gather x1, waiting for transfers between devices, fetch_experts(): lax.all_gather(down_weight.astype(jnp.bfloat16), 'group', axis=1, tiled=T...  80 us
    reduce_scatter x1, waiting for transfers between devices, shards(): lax.psum_scatter(totals[0].astype(jnp.bfloat16), 'group', scatter_dimensi...  68.6 us
    convert_element_type x2, other arithmetic, forward_block(): hidden = gelu_exact(hidden_pre).astype(jnp.bfloat16)  61.2 us
    reduce_scatter x1, waiting for transfers between devices, shards(): lax.psum_scatter(totals[1].astype(jnp.bfloat16), 'group', scatter_dimensi...  56 us
    psum x1, waiting for transfers between devices, shards(): lax.psum(owned[0].astype(jnp.bfloat16), 'replica').astype(jnp.float32)  54.8 us
  transfers between devices with their start and end apart: 11, of which 9 were waited for; matrix products, arithmetic and copies ran while one was open for 12% of the time, Pallas kernels for 0%

commit v1 on v0

v1 whole, which is shorter than its diff:
```python
import jax
import jax.numpy as jnp
import numpy as np
from jax import lax
from jax.sharding import Mesh
from jax.sharding import PartitionSpec as P

D = 512
HEADS = 8
HEAD_DIM = 64
F = 2048
E = 4
S = 197
MB_TOK = 394
CAP = 392
NV = 11
F32 = jnp.float32
BF16 = jnp.bfloat16
TOK = ("rx", "core", "group")


def layer_norm(value, gain, shift):
    center = value - jnp.mean(value, -1, keepdims=True)
    spread = jnp.mean(center * center, -1, keepdims=True)
    return center * lax.rsqrt(spread + 1e-06) * gain + shift


def gelu_exact(value):
    return jax.nn.gelu(value, approximate=False)


def split_heads(part):
    return part.reshape(-1, S, HEADS, HEAD_DIM)


def dot(a, b):
    return jnp.dot(a, b, preferred_element_type=F32)


def assign_places(route):
    chosen = jnp.concatenate([route[:, :, 0], route[:, :, 1]], 1)
    hits = (chosen[:, :, None] == jnp.arange(E, dtype=jnp.int32)).astype(jnp.int32)
    before = jnp.cumsum(hits, 1) - hits
    slot = jnp.sum(before * hits, 2)
    return chosen * CAP + slot


def hi_lo(v):
    hi = v.astype(BF16)
    lo = (v - hi.astype(F32)).astype(BF16)
    return jnp.concatenate([hi, lo], -1)


def pick_rows(onehot, table):
    both = jnp.einsum("mnr,mrd->mnd", onehot, hi_lo(table), preferred_element_type=F32)
    return both[..., :D] + both[..., D:]


def pack_dense(qkv_w, out_w, router_w, vectors, up_bias):
    rows = qkv_w.shape[0]
    ub = up_bias.reshape(E, rows, 4).transpose(1, 0, 2).reshape(rows, E * 4)
    return jnp.concatenate([qkv_w, out_w, router_w, vectors.T, ub], 1)


def unpack_dense(packed):
    rows = packed.shape[0]
    w_qkv = packed[:, : 3 * D]
    w_out = packed[:, 3 * D : 4 * D]
    w_router = packed[:, 4 * D : 4 * D + E]
    table = packed[:, 4 * D + E : 4 * D + E + NV].T
    ub = packed[:, 4 * D + E + NV :].reshape(rows, E, 4).transpose(1, 0, 2).reshape(E, rows * 4)
    return w_qkv, w_out, w_router, table, ub


def attention_fwd(w_qkv, w_out, table, value):
    rows = value.shape[0]
    scale = HEAD_DIM ** (-0.5)
    first = layer_norm(value, table[0], table[1]).astype(BF16)
    qkv_bias = jnp.concatenate([table[2], jnp.zeros((D,), F32), table[3]])
    qkv = (dot(first, w_qkv) + qkv_bias).astype(BF16)
    query, key_part, val_part = (
        split_heads(qkv[:, :D]),
        split_heads(qkv[:, D : 2 * D]),
        split_heads(qkv[:, 2 * D :]),
    )
    scores = jnp.einsum("bqhd,bkhd->bhqk", query, key_part, preferred_element_type=F32) * scale
    peak = jnp.max(scores, -1, keepdims=True)
    expo = jnp.exp(scores - peak)
    total = jnp.sum(expo, -1, keepdims=True)
    probs_att = (expo / total).astype(BF16)
    log_total = peak + jnp.log(total)
    attended = jnp.einsum("bhqk,bkhd->bqhd", probs_att, val_part, preferred_element_type=F32)
    attended = attended.reshape(rows, D).astype(BF16)
    resid = value + (dot(attended, w_out) + table[4])
    return first, qkv, log_total, attended, resid


def attention_bwd(w_qkv, w_out, table, value, first, qkv, log_total, attended, d_resid):
    rows = value.shape[0]
    scale = HEAD_DIM ** (-0.5)
    d_branch = d_resid.astype(BF16)
    g_bias_out = jnp.sum(d_branch.astype(F32), 0)
    g_out = lax.dot_general(attended, d_branch, (((0,), (0,)), ((), ())), preferred_element_type=F32)
    d_att = split_heads(
        lax.dot_general(d_branch, w_out, (((1,), (1,)), ((), ())), preferred_element_type=F32).astype(BF16)
    )
    query, key_part, val_part = (
        split_heads(qkv[:, :D]),
        split_heads(qkv[:, D : 2 * D]),
        split_heads(qkv[:, 2 * D :]),
    )
    scores = jnp.einsum("bqhd,bkhd->bhqk", query, key_part, preferred_element_type=F32) * scale
    probs_f = jnp.exp(scores - log_total)
    probs_att = probs_f.astype(BF16)
    d_val = jnp.einsum("bhqk,bqhd->bkhd", probs_att, d_att, preferred_element_type=F32)
    d_prob = jnp.einsum("bqhd,bkhd->bhqk", d_att, val_part, preferred_element_type=F32)
    d_score = (probs_f * (d_prob - jnp.sum(d_prob * probs_f, -1, keepdims=True))).astype(BF16)
    d_query = jnp.einsum("bhqk,bkhd->bqhd", d_score, key_part, preferred_element_type=F32) * scale
    d_key = jnp.einsum("bhqk,bqhd->bkhd", d_score, query, preferred_element_type=F32) * scale
    d_qkv = jnp.concatenate(
        [d_query.reshape(rows, D), d_key.reshape(rows, D), d_val.reshape(rows, D)], 1
    ).astype(BF16)
    d_qkv_f = d_qkv.astype(F32)
    g_bias_q = jnp.sum(d_qkv_f[:, :D], 0)
    g_bias_v = jnp.sum(d_qkv_f[:, 2 * D :], 0)
    g_qkv = lax.dot_general(first, d_qkv, (((0,), (0,)), ((), ())), preferred_element_type=F32)
    d_first = lax.dot_general(d_qkv, w_qkv, (((1,), (1,)), ((), ())), preferred_element_type=F32)
    first_pull = jax.vjp(layer_norm, value, table[0], table[1])[1]
    d_input, g_gain_one, g_shift_one = first_pull(d_first)
    return (g_qkv, g_out, g_bias_out, g_bias_q, g_bias_v, g_gain_one, g_shift_one), d_input


def adamw(weight, moments, grad, rate):
    first = 0.5 * moments[0] + 0.5 * grad
    root = jnp.sqrt(0.5 * moments[1] * moments[1] + 0.5 * grad * grad)
    update = first / (root + 1e-08)
    return (weight - rate * (update + 0.1 * weight), jnp.stack([first, root]))


def shards(
    tokens,
    cotangent,
    expert_index,
    qkv_weight,
    out_weight,
    router_weight,
    up_weight,
    up_bias,
    down_weight,
    vectors,
    qkv_moments,
    out_moments,
    router_moments,
    up_moments,
    up_bias_moments,
    down_moments,
    vector_moments,
):
    rows = tokens.shape[0]
    micro = rows // MB_TOK
    gs = qkv_weight.shape[0]
    core = lax.axis_index("core")

    dense = lax.all_gather(
        pack_dense(qkv_weight, out_weight, router_weight, vectors, up_bias).astype(BF16),
        "group",
        axis=0,
        tiled=True,
    )
    w_qkv, w_out, w_router, table_b, b_up_b = unpack_dense(dense)
    table = table_b.astype(F32)
    b_up = b_up_b.astype(F32)

    chunk_w = []
    for k in range(2):
        e = 2 * k + core
        up_piece = lax.dynamic_index_in_dim(up_weight, e, 0, keepdims=False)
        down_piece = lax.dynamic_index_in_dim(down_weight, e, 0, keepdims=False).reshape(gs, F)
        piece = jnp.stack([up_piece, down_piece]).astype(BF16)
        piece = lax.all_gather(piece, "group", axis=1, tiled=True)
        piece = lax.all_gather(piece, "core", axis=0, tiled=False)
        chunk_w.append((piece[:, 0], piece[:, 1].reshape(2, F, D)))

    value = tokens.astype(F32)
    d_out = cotangent.astype(F32)
    first, qkv, log_total, attended, resid = attention_fwd(w_qkv, w_out, table, value)
    second = layer_norm(resid, table[5], table[6]).astype(BF16)
    logits = dot(second, w_router)
    probs = jax.nn.softmax(logits, -1)
    picked = expert_index[:, :, None] == jnp.arange(E, dtype=jnp.int32)
    gate = jnp.sum(jnp.where(picked, probs[:, None, :], 0.0), -1)

    route = expert_index.reshape(micro, MB_TOK, 2)
    places = assign_places(route)
    onehot = (places[:, :, None] == jnp.arange(E * CAP, dtype=jnp.int32)).astype(BF16)
    second_m = second.reshape(micro, MB_TOK, D)
    pair = jnp.concatenate([second_m, second_m], 1)
    table_in = jnp.einsum("mnr,mnd->mrd", onehot, pair, preferred_element_type=F32).astype(BF16)
    table_in = table_in.reshape(micro, E, CAP, D).transpose(1, 0, 2, 3).reshape(E, micro * CAP, D)

    hidden_pre, hidden, expert_out = [], [], []
    for k in range(2):
        w_up, w_down = chunk_w[k]
        t_in = table_in[2 * k : 2 * k + 2]
        hp = jnp.einsum("ecd,edf->ecf", t_in, w_up, preferred_element_type=F32) + b_up[2 * k : 2 * k + 2, None, :]
        h = gelu_exact(hp).astype(BF16)
        y = jnp.einsum("ecf,efd->ecd", h, w_down, preferred_element_type=F32) + table[7 + 2 * k : 9 + 2 * k][:, None, :]
        hidden_pre.append(hp)
        hidden.append(h)
        expert_out.append(y)
    y_all = jnp.concatenate(expert_out, 0)
    y_m = y_all.reshape(E, micro, CAP, D).transpose(1, 0, 2, 3).reshape(micro, E * CAP, D)
    picked_rows = pick_rows(onehot, y_m)
    out_zero = picked_rows[:, :MB_TOK].reshape(rows, D)
    out_one = picked_rows[:, MB_TOK:].reshape(rows, D)
    result = resid + (gate[:, 0:1] * out_zero + gate[:, 1:2] * out_one)

    d_gate = jnp.stack([jnp.sum(d_out * out_zero, -1), jnp.sum(d_out * out_one, -1)], 1)
    d_out_m = d_out.reshape(micro, MB_TOK, D)
    gate_m = gate.reshape(micro, MB_TOK, 2)
    weighted = jnp.concatenate([gate_m[:, :, 0:1] * d_out_m, gate_m[:, :, 1:2] * d_out_m], 1).astype(BF16)
    d_expert = jnp.einsum("mnr,mnd->mrd", onehot, weighted, preferred_element_type=F32).astype(BF16)
    d_expert = d_expert.reshape(micro, E, CAP, D).transpose(1, 0, 2, 3).reshape(E, micro * CAP, D)
    g_bias_down = jnp.sum(d_expert.astype(F32), 1)

    d_tables = []
    expert_grads = []
    for k in range(2):
        w_up, w_down = chunk_w[k]
        dy = d_expert[2 * k : 2 * k + 2]
        g_down = jnp.einsum("ecf,ecd->efd", hidden[k], dy, preferred_element_type=F32)
        d_hidden = jnp.einsum("ecd,efd->ecf", dy, w_down, preferred_element_type=F32)
        gelu_pull = jax.vjp(gelu_exact, hidden_pre[k])[1]
        d_pre = gelu_pull(d_hidden)[0].astype(BF16)
        g_up_bias = jnp.sum(d_pre.astype(F32), 1)
        g_up = jnp.einsum("ecd,ecf->edf", table_in[2 * k : 2 * k + 2], d_pre, preferred_element_type=F32)
        d_tables.append(jnp.einsum("ecf,edf->ecd", d_pre, w_up, preferred_element_type=F32))
        expert_grads.append((g_up, g_down, g_up_bias))

    owned_experts = []
    for k in range(2):
        g_up, g_down, _ = expert_grads[k]
        packed = jnp.stack([g_up, g_down.reshape(2, D, F)], 1).astype(BF16)
        packed = lax.psum_scatter(packed, "core", scatter_dimension=0, tiled=True)
        packed = lax.psum_scatter(packed, "group", scatter_dimension=2, tiled=True)
        packed = lax.psum(packed, "rx")
        packed = lax.all_gather(packed, "core", axis=0, tiled=True)
        owned_experts.append(packed)

    d_table = jnp.concatenate(d_tables, 0)
    d_table_m = d_table.reshape(E, micro, CAP, D).transpose(1, 0, 2, 3).reshape(micro, E * CAP, D)
    onehot_sum = onehot[:, :MB_TOK] + onehot[:, MB_TOK:]
    d_picked = pick_rows(onehot_sum, d_table_m).reshape(rows, D)

    d_probs = jnp.sum(jnp.where(picked, d_gate[:, :, None], 0.0), 1)
    d_logit = (probs * (d_probs - jnp.sum(d_probs * probs, -1, keepdims=True))).astype(BF16)
    g_router = lax.dot_general(second, d_logit, (((0,), (0,)), ((), ())), preferred_element_type=F32)
    d_second = d_picked + lax.dot_general(d_logit, w_router, (((1,), (1,)), ((), ())), preferred_element_type=F32)
    norm_pull = jax.vjp(layer_norm, resid, table[5], table[6])[1]
    d_resid, g_gain_two, g_shift_two = norm_pull(d_second)
    d_resid = d_out + d_resid

    att_grads, d_input = attention_bwd(w_qkv, w_out, table, value, first, qkv, log_total, attended, d_resid)
    g_qkv, g_out, g_bias_out, g_bias_q, g_bias_v, g_gain_one, g_shift_one = att_grads
    input_grad = d_resid + d_input

    g_table = jnp.concatenate(
        [
            jnp.stack([g_gain_one, g_shift_one, g_bias_q, g_bias_v, g_bias_out, g_gain_two, g_shift_two]),
            g_bias_down,
        ],
        0,
    )
    g_up_bias_all = jnp.concatenate([expert_grads[0][2], expert_grads[1][2]], 0)
    dense_g = pack_dense(g_qkv, g_out, g_router, g_table, g_up_bias_all)
    dense_g = lax.psum_scatter(dense_g.astype(BF16), "group", scatter_dimension=0, tiled=True)
    dense_g = lax.psum(dense_g, ("rx", "core")).astype(F32)
    r_qkv, r_out, r_router, r_table, r_ub = unpack_dense(dense_g)
    r_up = jnp.concatenate([owned_experts[0][:, 0], owned_experts[1][:, 0]], 0).astype(F32)
    r_down = jnp.concatenate([owned_experts[0][:, 1], owned_experts[1][:, 1]], 0).astype(F32).reshape(E, gs * 4, D)

    reduced = (r_qkv, r_out, r_router, r_up, r_ub, r_down, r_table)
    rates = (
        2.0 * D ** (-0.5),
        2.0 * (D // 32) ** (-0.5),
        2.0 * (2 * D) ** (-0.5),
        2.0 * D ** (-0.5),
        0.2,
        2.0 * (F // 16) ** (-0.5),
        0.2,
    )
    params = (qkv_weight, out_weight, router_weight, up_weight, up_bias, down_weight, vectors)
    moments = (qkv_moments, out_moments, router_moments, up_moments, up_bias_moments, down_moments, vector_moments)
    news = []
    states = []
    for weight, state, grad, rate in zip(params, moments, reduced, rates):
        new_weight, new_state = adamw(weight, state, grad, rate)
        news.append(new_weight)
        states.append(new_state)
    return (result.astype(BF16), input_grad) + reduced + tuple(news) + tuple(states)


def solution(mesh):
    replica, group = mesh.shape["replica"], mesh.shape["group"]
    view = Mesh(np.asarray(mesh.devices).reshape(replica // 2, 2, group), ("rx", "core", "group"))
    in_specs = (
        P(TOK, None),
        P(TOK, None),
        P(TOK, None),
        P("group", None),
        P("group", None),
        P("group", None),
        P(None, "group", None),
        P(None, "group"),
        P(None, "group", None),
        P(None, "group"),
        P(None, "group", None),
        P(None, "group", None),
        P(None, "group", None),
        P(None, None, "group", None),
        P(None, None, "group"),
        P(None, None, "group", None),
        P(None, None, "group"),
    )
    out_specs = (
        P(TOK, None),
        P(TOK, None),
        P("group", None),
        P("group", None),
        P("group", None),
        P(None, "group", None),
        P(None, "group"),
        P(None, "group", None),
        P(None, "group"),
        P("group", None),
        P("group", None),
        P("group", None),
        P(None, "group", None),
        P(None, "group"),
        P(None, "group", None),
        P(None, "group"),
        P(None, "group", None),
        P(None, "group", None),
        P(None, "group", None),
        P(None, None, "group", None),
        P(None, None, "group"),
        P(None, None, "group", None),
        P(None, None, "group"),
    )
    return jax.shard_map(shards, mesh=view, in_specs=in_specs, out_specs=out_specs, check_vma=False)
```

time: 1260 us -> 1000 us (0.79)
  waiting for transfers between devices: 727 us -> 496 us
  blocking collectives: 101 us -> 0 us
  local copies, waits for them, and re-layouts: 95.3 us -> 155 us
  other arithmetic: 118 us -> 141 us
  matrix products: 199 us -> 185 us
    reduce_scatter x4 -> x2, waiting for transfers between devices: 430 us -> 184 us  [shards(): packed = lax.psum_scatter(packed, 'group', scatter_dimension=2, tiled=True)]
    all_gather x4 -> x0, blocking collectives: 93.5 us -> none  [the longest x1 29 us: fetch_dense(): lax.all_gather(out_weight.astype(jnp.bfloat16), 'group', axis=0, tiled=True)]
    all_gather x3 -> x7, waiting for transfers between devices: 134 us -> 197 us  [the longest x2 143 us: shards(): piece = lax.all_gather(piece, 'group', axis=1, tiled=True)]
    unnamed x14 -> x15, waiting for transfers between devices: 108 us -> 69.1 us
    gather x8 -> x0, local copies, waits for them, and re-layouts: 36.7 us -> none  [the longest x2 9.31 us: forward_block(): out_zero = expert_out[places[:rows]]]
    another operation x4 -> x19, local copies, waits for them, and re-layouts: 0.24 us -> 33.9 us  [the longest x2 15.3 us: shards(): packed = jnp.stack([g_up, g_down.reshape(2, D, F)], 1).astype(BF16)]
    slice x9 -> x25, local copies, waits for them, and re-layouts: 1.16 us -> 23.1 us  [the longest x2 9.58 us: shards(): chunk_w.append((piece[:, 0], piece[:, 1].reshape(2, F, D)))]
    unnamed x200 -> x218, local copies, waits for them, and re-layouts: 24.8 us -> 43.9 us
  transfers between devices with their start and end apart: 11 -> 13, of which waited for: 9 -> 10; matrix products, arithmetic and copies ran while one was open for 12% -> 19% of each run, Pallas kernels for 0% -> 0%
where the time goes in v1:
time: 1000 us; the launch traced here: 993 us
  waiting for transfers between devices  496 us (50%)
  matrix products  185 us (18%)
  local copies, waits for them, and re-layouts  155 us (16%)
  other arithmetic  141 us (14%)
  between operations  16 us (2%)
    reduce_scatter x2, waiting for transfers between devices, shards(): packed = lax.psum_scatter(packed, 'group', scatter_dimension=2, tiled=True)  184 us
    all_gather x2, waiting for transfers between devices, shards(): piece = lax.all_gather(piece, 'group', axis=1, tiled=True)  143 us
    unnamed x15, waiting for transfers between devices  69.1 us
    convert_element_type x2, other arithmetic, shards(): h = gelu_exact(hp).astype(BF16)  64.7 us
    all_gather x1, waiting for transfers between devices, shards(): lax.all_gather(pack_dense(qkv_weight, out_weight, router_weight, vectors,...  45.5 us
    unnamed x218, local copies, waits for them, and re-layouts  43.9 us
    psum x1, waiting for transfers between devices, shards(): packed = lax.psum(packed, 'rx')  37.5 us
    dot_general x2, matrix products, shards(): jnp.einsum('ecd,efd->ecf', dy, w_down, preferred_element_type=F32)  29 us
  transfers between devices with their start and end apart: 13, of which 10 were waited for; matrix products, arithmetic and copies ran while one was open for 19% of the time, Pallas kernels for 0%

profile of v1, /device:TPU:1, one launch (start us, length us, event | category | flops | bytes accessed | tf_op | source)
XLA Modules:
  0.0 992.9 jit_solution(9458446906884833733)
XLA Ops:
  13.7 71.7 %all-gather.12.cloned.1.call-done = bf16[2,512,2048]{2,1,0:T(8,128)(2,1)} async-done(((bf16[2,64,2048]{2,1,0:T(8,128)(2,1)}), bf16[2,512,2048]{2,1,0:T(8,128)(2,1)}) %all-gather.12.cloned.1.call-update) | async-done | bytes 4194320 | tf_op jit(solution)/shard_map/all_gather | solution.py:180
  85.8 2.3 reduce-window.6
  88.7 71.2 %all-gather.14.cloned.1.call-done = bf16[2,512,2048]{2,1,0:T(8,128)(2,1)} async-done(((bf16[2,64,2048]{2,1,0:T(8,128)(2,1)}), bf16[2,512,2048]{2,1,0:T(8,128)(2,1)}) %all-gather.14.cloned.1.call-update) | async-done | bytes 4194320 | tf_op jit(solution)/shard_map/all_gather | solution.py:180
  162.8 3.4 fusion.13
  166.1 45.5 %all-gather.10.cloned.1.call-done = bf16[512,2079]{1,0:T(8,128)(2,1)} async-done(((bf16[64,2079]{1,0:T(8,128)(2,1)}), bf16[512,2079]{1,0:T(8,128)(2,1)}) %all-gather.10.cloned.1.call-update) | async-done | bytes 2128912 | tf_op jit(solution)/shard_map/all_gather | solution.py:164
  213.7 3.0 add_convert_fusion.2
  219.7 2.4 copy.352
  224.2 2.2 copy.353
  226.3 3.6 reshape.466
  229.9 2.8 copy.354
  242.9 17.4 %fusion.30 = bf16[2,1568,512]{2,1,0:T(8,128)(2,1)S(1)} fusion(s32[2,788]{1,0:T(2,128)S(1)} %multiply_add_fusion.7, bf16[2,394,512]{2,1,0:T(8,128)(2,1)S(1)} %reshape.429), kind=kOutput, calls=%fused_computation.81 | convolution fusion | flops 2537780480 | bytes 4024480 | tf_op jit(solution)/shard_map/mnr,mnd->mrd/dot_general | solution.py:198
  267.9 4.8 slice.338
  272.7 7.6 reshape_squeeze.6
  280.3 4.8 slice.343
  285.1 7.6 reshape_squeeze.7
  292.7 14.5 %fusion.43 = (u8[784,2048]{1,0:T(8,128)(4,1)}, u8[784,2048]{1,0:T(8,128)(4,1)}, f32[2,784,2048]{2,1,0:T(8,128)}) fusion(f32[2,2048]{1,0:T(2,128)S(1)} %slice.264, bf16[2,784,512]{2,1,0:T(8,128)(2,1)S(1)} %bitcast.282, bf16[2,2,512,2048]{3,2,1,0:T(8,128)(2,1)} %bitcast.276), kind=kOutput, calls=%fused_computation.96 | convolution fusion | flops 3330080768 | bytes 21872640 | tf_op jit(solution)/shard_map/ecd,edf->ecf/dot_general | solution.py:205
  307.2 10.9 %fusion.44 = (u8[784,2048]{1,0:T(8,128)(4,1)}, u8[784,2048]{1,0:T(8,128)(4,1)}, f32[2,784,2048]{2,1,0:T(8,128)S(1)}) fusion(f32[2,2048]{1,0:T(2,128)S(1)} %slice.271, bf16[2,784,512]{2,1,0:T(8,128)(2,1)S(1)} %bitcast.284, bf16[2,2,512,2048]{3,2,1,0:T(8,128)(2,1)} %bitcast.279), kind=kOutput, calls=%fused_computation.97 | convolution fusion | flops 3330080768 | bytes 21872640 | tf_op jit(solution)/shard_map/ecd,edf->ecf/dot_general | solution.py:205
  318.2 33.5 %multiply_convert_fusion.1 = (bf16[2,784,2048]{2,1,0:T(8,128)(2,1)S(1)}, f32[2,784,2048]{2,1,0:T(8,128)}) fusion(f32[2,784,2048]{2,1,0:T(8,128)} %get-tuple-element.268, f32[2,2048]{1,0:T(2,128)S(1)} %slice.264, u8[784,2048]{1,0:T(8,128)(4,1)} %get-tuple-element.162, u8[784,2048]{1,0:T(8,128)(4,1)} %get-tuple-element.161), kind=kLoop, calls=%fused_computation.28 | loop fusion | flops 227999744 | bytes 35340288 | tf_op jit(solution)/shard_map/convert_element_type | solution.py:206
  351.7 5.2 convolution_add_fusion.1
  356.9 31.2 %multiply_convert_fusion = (bf16[2,784,2048]{2,1,0:T(8,128)(2,1)S(1)}, f32[2,784,2048]{2,1,0:T(8,128)}) fusion(f32[2,784,2048]{2,1,0:T(8,128)S(1)} %get-tuple-element.267, f32[2,2048]{1,0:T(2,128)S(1)} %slice.271, u8[784,2048]{1,0:T(8,128)(4,1)S(1)} %copy-done.53, u8[784,2048]{1,0:T(8,128)(4,1)S(1)} %copy-done.52), kind=kLoop, calls=%fused_computation.15 | loop fusion | flops 227999744 | bytes 35340288 | tf_op jit(solution)/shard_map/convert_element_type | solution.py:206
  388.1 2.7 copy-done.26
  390.8 3.5 convolution_add_fusion
  397.2 6.1 fusion.14
  409.4 2.2 multiply_reduce_fusion.5
  413.7 4.7 fusion.31
  422.8 14.4 %fusion.157 = (bf16[2,2048]{1,0:T(2,128)(2,1)S(1)}, bf16[2,784,2048]{2,1,0:T(8,128)(2,1)}) fusion(f32[2,784,2048]{2,1,0:T(8,128)} %get-tuple-element.208, bf16[2,784,512]{2,1,0:T(8,128)(2,1)} %bitcast.288, bf16[2,2048,512]{2,1,0:T(8,128)(2,1)S(1)} %copy-done.32, f32[2,784,2048]{2,1,0:T(8,128)} %get-tuple-element.268, f32[2,2048]{1,0:T(2,128)S(1)} %slice.264), kind=kOutput, calls=%fused_computation.336 | convolution fusion | flops 3339710464 | bytes 37937152 | tf_op jit(solution)/shard_map/ecd,efd->ecf/dot_general | solution.py:232
  437.3 9.4 fusion.32
  446.6 14.6 %fusion.156 = (bf16[2,2048]{1,0:T(2,128)(2,1)S(1)}, bf16[2,784,2048]{2,1,0:T(8,128)(2,1)}) fusion(f32[2,784,2048]{2,1,0:T(8,128)} %get-tuple-element.210, bf16[2,784,512]{2,1,0:T(8,128)(2,1)} %bitcast.286, bf16[2,2048,512]{2,1,0:T(8,128)(2,1)S(1)} %copy-done.30, f32[2,784,2048]{2,1,0:T(8,128)} %copy-done.19, f32[2,2048]{1,0:T(2,128)S(1)} %slice.271), kind=kOutput, calls=%fused_computation.335 | convolution fusion | flops 3339710464 | bytes 37937152 | tf_op jit(solution)/shard_map/ecd,efd->ecf/dot_general | solution.py:232
  461.3 7.1 fusion.34
  470.1 2.9 fusion.23
  473.0 4.9 fusion.19
  479.5 2.8 reshape.440
  482.3 2.6 multiply_reduce_fusion.2
  493.0 4.3 fusion.88
  497.3 7.5 multiply_reduce_fusion
  504.9 4.7 multiply_convert_fusion.2
  520.9 2.8 convert_element_type.198
  523.7 3.5 convolution_convert_fusion.2
  529.8 2.3 slice_reduce_fusion
  532.1 4.2 fusion.139
  538.4 2.3 reduce.2
  541.2 4.4 concatenate.112
  545.7 10.4 %convolution_convert_fusion.1 = bf16[2,2048,512]{2,1,0:T(8,128)(2,1)} fusion(bf16[2,784,2048]{2,1,0:T(8,128)(2,1)} %copy-done.25, bf16[2,784,512]{2,1,0:T(8,128)(2,1)S(1)} %bitcast.289), kind=kOutput, calls=%fused_computation.84 | convolution fusion | flops 3290431488 | bytes 12222464 | tf_op jit(solution)/shard_map/ecf,ecd->efd/dot_general | solution.py:231
  556.1 7.7 stack_reshape.18
  563.8 10.5 %convolution_convert_fusion = bf16[2,2048,512]{2,1,0:T(8,128)(2,1)} fusion(bf16[2,784,2048]{2,1,0:T(8,128)(2,1)} %copy-done.26, bf16[2,784,512]{2,1,0:T(8,128)(2,1)S(1)} %bitcast.287), kind=kOutput, calls=%fused_computation.83 | convolution fusion | flops 3290431488 | bytes 12222464 | tf_op jit(solution)/shard_map/ecf,ecd->efd/dot_general | solution.py:231
  574.3 7.7 stack_reshape.19
  582.0 7.8 convert_bitcast_fusion.1
  589.8 7.8 convert_bitcast_fusion
  597.6 6.2 pad_maximum_fusion
  605.1 7.7 reduce-scatter.16.cloned.1.call-done
  614.8 61.1 %all-reduce.11.cloned.1.call-done = (bf16[2,2,512,2048]{3,2,0,1:T(8,128)(2,1)}, bf16[2,2,512,2048]{3,2,0,1:T(8,128)(2,1)}) async-done(((bf16[2,2,512,2048]{3,2,0,1:T(8,128)(2,1)}, bf16[2,2,512,2048]{3,2,0,1:T(8,128)(2,1)}), (bf16[2,2,512,2048]{3,2,0,1:T(8,128)(2,1)}, bf16[2,2,512,2048]{3,2,0,1:T(8,128)(2,1)})) %all-reduce.11.cloned.1.call-update) | async-done | bytes 16777232
  675.9 5.4 constant_dynamic-slice_fusion.1
  681.7 5.4 constant_dynamic-slice_fusion
  700.1 2.9 add_add_fusion.2
  703.0 8.7 all-reduce.9.cloned.1.call-done
  713.9 91.4 %reduce-scatter.12.cloned.1.call-done = bf16[1,2,64,2048]{3,2,0,1:T(8,128)(2,1)} async-done(((bf16[1,2,512,2048]{3,2,0,1:T(8,128)(2,1)}), bf16[1,2,64,2048]{3,2,0,1:T(8,128)(2,1)}) %reduce-scatter.12.cloned.1.call-update) | async-done | bytes 524304 | tf_op jit(solution)/shard_map/reduce_scatter | solution.py:245
  805.3 92.4 %reduce-scatter.14.cloned.1.call-done = bf16[1,2,64,2048]{3,2,0,1:T(8,128)(2,1)} async-done(((bf16[1,2,512,2048]{3,2,0,1:T(8,128)(2,1)}), bf16[1,2,64,2048]{3,2,0,1:T(8,128)(2,1)}) %reduce-scatter.14.cloned.1.call-update) | async-done | bytes 524304 | tf_op jit(solution)/shard_map/reduce_scatter | solution.py:245
  902.5 37.5 %all-reduce.13.cloned.1.call-done = (bf16[1,2,64,2048]{3,2,0,1:T(8,128)(2,1)}, bf16[1,2,64,2048]{3,2,0,1:T(8,128)(2,1)}) async-done(((bf16[1,2,64,2048]{3,2,0,1:T(8,128)(2,1)}, bf16[1,2,64,2048]{3,2,0,1:T(8,128)(2,1)}), (bf16[1,2,64,2048]{3,2,0,1:T(8,128)(2,1)}, bf16[1,2,64,2048]{3,2,0,1:T(8,128)(2,1)})) %all-reduce.13.cloned.1.call-update) | async-done | bytes 1048592 | tf_op jit(solution)/shard_map/psum | solution.py:246
  954.5 8.3 all-gather.18.cloned.1.call-done
  966.3 3.5 multiply_add_fusion
  969.8 2.7 pad_maximum_fusion.5
  974.6 2.4 pad_maximum_fusion.4
  979.0 3.5 fusion.60
  982.5 3.5 fusion.53
  (404 shorter events, 123.2 us)
Async XLA Ops:
  7.2 5.4 copy-start.61
  7.2 5.4 copy-start.89
  7.2 5.5 copy-start.75
  7.3 78.2 %all-gather.12.cloned.1.call-start = ((), (), s32[]{:S(2)}) async-start(), calls=%async_computation.4 | async-start | bytes 4718592 | tf_op jit(solution)/shard_map/all_gather | solution.py:180
  11.0 74.5 %copy-start.81 = (s32[788,2]{0,1:T(2,128)S(1)}, s32[788,2]{0,1:T(2,128)}, u32[]{:S(2)}) copy-start(s32[788,2]{0,1:T(2,128)} %param.19) | copy-start | bytes 18916
  11.0 148.9 %all-gather.14.cloned.1.call-start = ((), (), s32[]{:S(2)}) async-start(), calls=%async_computation.5 | async-start | bytes 4718592 | tf_op jit(solution)/shard_map/all_gather | solution.py:180
  12.1 199.5 %all-gather.10.cloned.1.call-start = ((), (), s32[]{:S(2)}) async-start(), calls=%async_computation.3 | async-start | bytes 2506752 | tf_op jit(solution)/shard_map/all_gather | solution.py:164
  13.7 254.2 %all-gather.20.cloned.1.call-start = ((), (), s32[]{:S(2)}) async-start(), calls=%async_computation.11 | async-start | bytes 12582912 | tf_op jit(solution)/shard_map/all_gather | solution.py:181
  85.4 74.6 %copy-start.15 = (bf16[788,512]{1,0:T(8,128)(2,1)S(1)}, bf16[788,512]{1,0:T(8,128)(2,1)}, u32[]{:S(2)}) copy-start(bf16[788,512]{1,0:T(8,128)(2,1)} %param.18) | copy-start | bytes 2420740
  85.5 75.9 %copy-start.13 = (bf16[788,512]{1,0:T(8,128)(2,1)S(1)}, bf16[788,512]{1,0:T(8,128)(2,1)}, u32[]{:S(2)}) copy-start(bf16[788,512]{1,0:T(8,128)(2,1)} %param.17) | copy-start | bytes 2420740
  85.5 194.8 %all-gather.22.cloned.1.call-start = ((), (), s32[]{:S(2)}) async-start(), calls=%async_computation.12 | async-start | bytes 12582912 | tf_op jit(solution)/shard_map/all_gather | solution.py:181
  159.9 452.9 %reduce-scatter.16.cloned.1.call-start = ((), (), s32[]{:S(2)}) async-start(), calls=%async_computation.13 | async-start | bytes 2506752
  161.6 52.1 %copy-start.67 = (f32[788]{0:T(1024)}, f32[788]{0:T(1024)S(1)}, u32[]{:S(2)}) copy-start(f32[788]{0:T(1024)S(1)} %broadcast_multiply_fusion.1) | copy-start | bytes 9460
  162.7 51.0 %copy-start.73 = (f32[788]{0:T(1024)}, f32[788]{0:T(1024)S(1)}, u32[]{:S(2)}) copy-start(f32[788]{0:T(1024)S(1)} %fusion.122) | copy-start | bytes 9460
  213.7 28.0 %copy-start.79 = (f32[512]{0:T(512)}, f32[512]{0:T(512)S(1)}, u32[]{:S(2)}) copy-start(f32[512]{0:T(512)S(1)} %get-tuple-element.176) | copy-start | bytes 6148
  222.2 10.6 %copy-start.22 = (bf16[4,197,8,64]{1,3,2,0:T(8,128)(2,1)}, bf16[4,197,8,64]{1,3,2,0:T(8,128)(2,1)S(1)}, u32[]{:S(2)}) copy-start(bf16[4,197,8,64]{1,3,2,0:T(8,128)(2,1)S(1)} %copy.352) | copy-start | bytes 2420740
  226.3 7.5 copy-start.20
  241.3 19.1 %copy-start.63 = (f32[788]{0:T(1024)}, f32[788]{0:T(1024)S(1)}, u32[]{:S(2)}) copy-start(f32[788]{0:T(1024)S(1)} %broadcast_multiply_fusion) | copy-start | bytes 9460
  241.7 18.7 %copy-start.71 = (f32[788]{0:T(1024)}, f32[788]{0:T(1024)S(1)}, u32[]{:S(2)}) copy-start(f32[788]{0:T(1024)S(1)} %multiply_reduce_fusion.6) | copy-start | bytes 9460
  241.7 18.7 %copy-start.65 = (f32[788]{0:T(1024)}, f32[788]{0:T(1024)S(1)}, u32[]{:S(2)}) copy-start(f32[788]{0:T(1024)S(1)} %fusion.123) | copy-start | bytes 9460
  242.7 23.2 %copy-start.11 = (bf16[788,512]{1,0:T(8,128)(2,1)}, bf16[788,512]{1,0:T(8,128)(2,1)S(1)}, u32[]{:S(2)}) copy-start(bf16[788,512]{1,0:T(8,128)(2,1)S(1)} %add_convert_fusion.4) | copy-start | bytes 2420740
  285.1 7.6 copy-start.46
  292.7 14.5 %copy-start.48 = (bf16[2,2,392,512]{3,2,1,0:T(8,128)(2,1)S(1)}, bf16[2,2,392,512]{3,2,1,0:T(8,128)(2,1)}, u32[]{:S(2)}) copy-start(bf16[2,2,392,512]{3,2,1,0:T(8,128)(2,1)} %copy.362) | copy-start | bytes 4816900
  318.2 38.7 %copy-start.19 = (f32[2,784,2048]{2,1,0:T(8,128)}, f32[2,784,2048]{2,1,0:T(8,128)S(1)}, u32[]{:S(2)}) copy-start(f32[2,784,2048]{2,1,0:T(8,128)S(1)} %get-tuple-element.267) | copy-start | bytes 38535172
  318.2 33.5 %copy-start.31 = (bf16[2,2048,512]{2,1,0:T(8,128)(2,1)S(1)}, bf16[2,2048,512]{2,1,0:T(8,128)(2,1)}, u32[]{:S(2)}) copy-start(bf16[2,2048,512]{2,1,0:T(8,128)(2,1)} %reshape_squeeze.6) | copy-start | bytes 12582916
  351.6 5.2 copy-start.25
  351.6 5.2 copy-start.52
  351.7 5.2 copy-start.53
  356.8 34.0 %copy-start.29 = (bf16[2,2048,512]{2,1,0:T(8,128)(2,1)S(1)}, bf16[2,2048,512]{2,1,0:T(8,128)(2,1)}, u32[]{:S(2)}) copy-start(bf16[2,2048,512]{2,1,0:T(8,128)(2,1)} %reshape_squeeze.7) | copy-start | bytes 12582916
  409.3 9.0 copy-start.7
  437.2 9.4 copy-start.30
  461.3 7.1 copy-start.39
  479.5 5.4 copy-start.72
  493.0 11.9 %slice-start = ((s8[6553600]{0:T(1024)(128)(4,1)}), s8[4194304]{0:T(1024)(128)(4,1)S(1)}, s32[]{:S(2)}) async-start(s8[6553600]{0:T(1024)(128)(4,1)} %bitcast.266), calls=%async_computation.16 | async-start | bytes 8388608
  497.3 7.5 slice-start.1
  520.9 6.4 copy-start.27
  545.7 130.3 %all-reduce.11.cloned.1.call-start = ((), (), s32[]{:S(2)}) async-start(), calls=%async_computation.14 | async-start | bytes 33554432
  556.1 7.7 copy-start.50
  574.3 7.7 copy-start.47
  582.0 7.8 copy-start.49
  589.8 7.8 copy-start.5
  589.8 7.8 copy-start.6
  603.8 107.8 %all-reduce.9.cloned.1.call-start = ((), (), s32[]{:S(2)}) async-start(), calls=%async_computation.6 | async-start | bytes 1064960 | tf_op jit(solution)/shard_map/psum | solution.py:277
  614.8 190.5 %reduce-scatter.12.cloned.1.call-start = ((), (), s32[]{:S(2)}) async-start(), calls=%async_computation.7 | async-start | bytes 4718592 | tf_op jit(solution)/shard_map/reduce_scatter | solution.py:245
  681.4 216.3 %reduce-scatter.14.cloned.1.call-start = ((), (), s32[]{:S(2)}) async-start(), calls=%async_computation.9 | async-start | bytes 4718592 | tf_op jit(solution)/shard_map/reduce_scatter | solution.py:245
  687.1 12.9 %copy-start.87 = (f32[2,11,64]{2,0,1:T(2,128)S(1)}, f32[2,11,64]{2,0,1:T(2,128)}, u32[]{:S(2)}) copy-start(f32[2,11,64]{2,0,1:T(2,128)} %param.33) | copy-start | bytes 16900
  687.1 12.9 %copy-start.10 = (f32[788,512]{1,0:T(8,128)S(1)}, f32[788,512]{1,0:T(8,128)}, u32[]{:S(2)}) copy-start(f32[788,512]{1,0:T(8,128)} %copy-done.9) | copy-start | bytes 4841476
  687.2 12.9 %copy-start.17 = (bf16[788,512]{1,0:T(8,128)(2,1)S(1)}, bf16[788,512]{1,0:T(8,128)(2,1)}, u32[]{:S(2)}) copy-start(bf16[788,512]{1,0:T(8,128)(2,1)} %param.18) | copy-start | bytes 2420740
  687.2 252.8 %all-reduce.13.cloned.1.call-start = ((), (), s32[]{:S(2)}) async-start(), calls=%async_computation.15 | async-start | bytes 2097152 | tf_op jit(solution)/shard_map/psum | solution.py:246
  700.1 197.7 %copy-start.76 = (f32[11,64]{1,0:T(8,128)S(1)}, f32[11,64]{1,0:T(8,128)}, u32[]{:S(2)}) copy-start(f32[11,64]{1,0:T(8,128)} %param.26) | copy-start | bytes 8452
  703.0 197.6 %copy-start.41 = (f32[64,1536]{0,1:T(8,128)S(1)}, f32[64,1536]{0,1:T(8,128)}, u32[]{:S(2)}) copy-start(f32[64,1536]{0,1:T(8,128)} %copy.392) | copy-start | bytes 1179652
  703.0 197.6 %copy-start.42 = (f32[1,64,1536]{1,2,0:T(8,128)S(1)}, f32[1,64,1536]{1,2,0:T(8,128)}, u32[]{:S(2)}) copy-start(f32[1,64,1536]{1,2,0:T(8,128)} %copy.430) | copy-start | bytes 1179652
  703.0 197.6 %copy-start.43 = (f32[1,64,1536]{1,2,0:T(8,128)S(1)}, f32[1,64,1536]{1,2,0:T(8,128)}, u32[]{:S(2)}) copy-start(f32[1,64,1536]{1,2,0:T(8,128)} %copy.431) | copy-start | bytes 1179652
  712.7 238.3 %copy-start.84 = (f32[4,256]{1,0:T(4,128)}, f32[4,256]{1,0:T(4,128)S(1)}, u32[]{:S(2)}) copy-start(f32[4,256]{1,0:T(4,128)S(1)} %reshape.452) | copy-start | bytes 12292
  713.9 188.6 %copy-start.78 = (f32[11,64]{1,0:T(8,128)}, f32[11,64]{1,0:T(8,128)S(1)}, u32[]{:S(2)}) copy-start(f32[11,64]{1,0:T(8,128)S(1)} %get-tuple-element.192) | copy-start | bytes 8452
  897.7 54.0 %all-gather.16.cloned.1.call-start = ((), (), s32[]{:S(2)}) async-start(), calls=%async_computation.8 | async-start | bytes 1572864 | tf_op jit(solution)/shard_map/all_gather | solution.py:247
  902.5 42.4 %copy-start.44 = (f32[64,1536]{0,1:T(8,128)S(1)}, f32[64,1536]{0,1:T(8,128)}, u32[]{:S(2)}) copy-start(f32[64,1536]{0,1:T(8,128)} %get-tuple-element.229) | copy-start | bytes 1179652
  940.0 22.7 %all-gather.18.cloned.1.call-start = ((), (), s32[]{:S(2)}) async-start(), calls=%async_computation.10 | async-start | bytes 1572864 | tf_op jit(solution)/shard_map/all_gather | solution.py:247
  940.0 5.9 copy-start.55
  941.2 5.5 copy-start.28
  943.5 5.0 copy-start.88
  943.6 5.6 copy-start.77
  943.6 7.5 copy-start.86
  948.6 16.7 %copy-start.91 = (f32[64,4]{0,1:T(4,128)}, f32[64,4]{0,1:T(4,128)S(1)}, u32[]{:S(2)}) copy-start(f32[64,4]{0,1:T(4,128)S(1)} %get-tuple-element.194) | copy-start | bytes 3076
  (48 other events, 155.8 us)
Sparse Core Ops, SparseCore 0:
  11.1 74.2 all-gather.11
  88.2 71.6 all-gather.13
  162.6 48.9 all-gather.9
  213.0 19.8 all-gather.19
  234.4 21.0 all-gather.21
  545.8 66.9 reduce-scatter.15
  615.3 60.5 all-reduce.10
  679.0 32.6 all-reduce.8
  715.9 89.3 reduce-scatter.11
  809.8 87.8 reduce-scatter.13
  900.0 39.8 all-reduce.12
  941.4 9.4 all-gather.15
  952.5 10.1 all-gather.17

commit v2 on v1

--- a/solution.py
+++ b/solution.py
@@ -1,9 +1,13 @@
+import functools
+
 import jax
 import jax.numpy as jnp
 import numpy as np
 from jax import lax
 from jax.sharding import Mesh
 from jax.sharding import PartitionSpec as P
+from jax.experimental import pallas as pl
+from jax.experimental.pallas import tpu as pltpu
 
 D = 512
 HEADS = 8
@@ -14,9 +18,138 @@
 MB_TOK = 394
 CAP = 392
 NV = 11
+DENSE_PAD = 2304
 F32 = jnp.float32
 BF16 = jnp.bfloat16
 TOK = ("rx", "core", "group")
+
+
+MESH_ID = pl.DeviceIdType.MESH
+
+
+def ring_order(groups):
+    if groups in (4, 8):
+        zs = groups // 2
+
+        def pos_of(g):
+            y = g % 2
+            z = g // 2
+            return z + y * (2 * zs - 1 - 2 * z)
+
+        def dev_at(p):
+            p = p % groups
+            yy = p // zs
+            return 2 * (p + yy * (2 * zs - 1 - 2 * p)) + yy
+
+        return pos_of, dev_at
+    return (lambda g: g), (lambda p: p % groups)
+
+
+def ring_rs_kernel(groups, n_in, *refs):
+    ins = refs[:n_in]
+    outs = refs[n_in : 2 * n_in]
+    rbufs = refs[2 * n_in : 3 * n_in]
+    sbufs = refs[3 * n_in : 4 * n_in]
+    owns = refs[4 * n_in : 5 * n_in]
+    send_sem, recv_sem, load_sem = refs[5 * n_in :]
+    pos_of, dev_at = ring_order(groups)
+    rx = lax.axis_index("rx")
+    core = lax.axis_index("core")
+    g = lax.axis_index("group")
+    pos = pos_of(g)
+    nbr = (dev_at(pos + 1), dev_at(pos + groups - 1))
+
+    barrier = pltpu.get_barrier_semaphore()
+    for n in nbr:
+        pl.semaphore_signal(barrier, inc=1, device_id=(rx, core, n), device_id_type=MESH_ID)
+    pl.semaphore_wait(barrier, 2)
+
+    def block_dev(d, s):
+        if d == 0:
+            return dev_at(pos + 2 * groups - s - 1)
+        return dev_at(pos + s + 1)
+
+    def load(d, s, slot):
+        b = block_dev(d, s)
+        copies = []
+        for i in range(n_in):
+            rows = ins[i].shape[1] // groups
+            half = ins[i].shape[2] // 2
+            src = ins[i].at[:, pl.ds(pl.multiple_of(b * rows, rows), rows), pl.ds(d * half, half)]
+            copies.append(pltpu.make_async_copy(src, owns[i].at[d, slot], load_sem.at[d, slot, i]))
+        return copies
+
+    def remote(d, s, i):
+        return pltpu.make_async_remote_copy(
+            src_ref=sbufs[i].at[d, s],
+            dst_ref=rbufs[i].at[d, s],
+            send_sem=send_sem.at[d, s, i],
+            recv_sem=recv_sem.at[d, s, i],
+            device_id=(rx, core, nbr[d]),
+            device_id_type=MESH_ID,
+        )
+
+    for d in range(2):
+        for c in load(d, 0, 0):
+            c.start()
+    sends = []
+    for s in range(groups):
+        slot = s % 2
+        for d in range(2):
+            for c in load(d, s, slot):
+                c.wait()
+            if s + 1 < groups:
+                for c in load(d, s + 1, 1 - slot):
+                    c.start()
+            for i in range(n_in):
+                if s > 0:
+                    remote(d, s - 1, i).wait_recv()
+                for a in range(ins[i].shape[0]):
+                    mine = owns[i][d, slot, a].astype(F32)
+                    if s > 0:
+                        mine = mine + rbufs[i][d, s - 1, a].astype(F32)
+                    if s < groups - 1:
+                        sbufs[i][d, s, a] = mine.astype(sbufs[i].dtype)
+                    else:
+                        half = ins[i].shape[2] // 2
+                        outs[i][a, :, pl.ds(d * half, half)] = mine.astype(outs[i].dtype)
+                if s < groups - 1:
+                    c = remote(d, s, i)
+                    c.start()
+                    sends.append(c)
+    for c in sends:
+        c.wait_send()
+
+
+def ring_reduce_scatter(xs, groups, collective_id):
+    n_in = len(xs)
+    outs, rb, own = [], [], []
+    flops = 0
+    nbytes = 0
+    for x in xs:
+        a, total, c = x.shape
+        rows = total // groups
+        outs.append(jax.ShapeDtypeStruct((a, rows, c), x.dtype))
+        rb.append(pltpu.VMEM((2, groups - 1, a, rows, c // 2), x.dtype))
+        own.append(pltpu.VMEM((2, 2, a, rows, c // 2), x.dtype))
+        flops += a * total * c
+        nbytes += 3 * x.size * x.dtype.itemsize
+    scratch = rb + rb + own + [
+        pltpu.SemaphoreType.DMA((2, groups - 1, n_in)),
+        pltpu.SemaphoreType.DMA((2, groups - 1, n_in)),
+        pltpu.SemaphoreType.DMA((2, 2, n_in)),
+    ]
+    return pl.pallas_call(
+        functools.partial(ring_rs_kernel, groups, n_in),
+        out_shape=outs,
+        in_specs=[pl.BlockSpec(memory_space=pl.ANY)] * n_in,
+        out_specs=[pl.BlockSpec(memory_space=pltpu.VMEM)] * n_in,
+        scratch_shapes=scratch,
+        compiler_params=pltpu.CompilerParams(
+            collective_id=collective_id, has_side_effects=True, vmem_limit_bytes=60 * 1024 * 1024
+        ),
+        cost_estimate=pl.CostEstimate(flops=flops, bytes_accessed=nbytes, transcendentals=0),
+    )(*xs)
 
 
 def layer_norm(value, gain, shift):
@@ -159,6 +292,7 @@
     rows = tokens.shape[0]
     micro = rows // MB_TOK
     gs = qkv_weight.shape[0]
+    group_size = D // gs
     core = lax.axis_index("core")
 
     dense = lax.all_gather(
@@ -237,16 +371,6 @@
         d_tables.append(jnp.einsum("ecf,edf->ecd", d_pre, w_up, preferred_element_type=F32))
         expert_grads.append((g_up, g_down, g_up_bias))
 
-    owned_experts = []
-    for k in range(2):
-        g_up, g_down, _ = expert_grads[k]
-        packed = jnp.stack([g_up, g_down.reshape(2, D, F)], 1).astype(BF16)
-        packed = lax.psum_scatter(packed, "core", scatter_dimension=0, tiled=True)
-        packed = lax.psum_scatter(packed, "group", scatter_dimension=2, tiled=True)
-        packed = lax.psum(packed, "rx")
-        packed = lax.all_gather(packed, "core", axis=0, tiled=True)
-        owned_experts.append(packed)
-
     d_table = jnp.concatenate(d_tables, 0)
     d_table_m = d_table.reshape(E, micro, CAP, D).transpose(1, 0, 2, 3).reshape(micro, E * CAP, D)
     onehot_sum = onehot[:, :MB_TOK] + onehot[:, MB_TOK:]
@@ -272,12 +396,25 @@
         0,
     )
     g_up_bias_all = jnp.concatenate([expert_grads[0][2], expert_grads[1][2]], 0)
+    mine_list, send_list = [], []
+    for k in range(2):
+        g_up, g_down, _ = expert_grads[k]
+        both = jnp.stack([g_up, g_down.reshape(2, D, F)], 1)
+        mine_list.append(lax.dynamic_index_in_dim(both, core, 0, keepdims=False))
+        send_list.append(lax.dynamic_index_in_dim(both, 1 - core, 0, keepdims=False))
+    sent = jnp.stack(send_list).astype(BF16)
+    got = lax.ppermute(sent, "core", [(0, 1), (1, 0)])
+    expert_sum = (jnp.stack(mine_list) + got.astype(F32)).astype(BF16).reshape(4, D, F)
     dense_g = pack_dense(g_qkv, g_out, g_router, g_table, g_up_bias_all)
-    dense_g = lax.psum_scatter(dense_g.astype(BF16), "group", scatter_dimension=0, tiled=True)
-    dense_g = lax.psum(dense_g, ("rx", "core")).astype(F32)
-    r_qkv, r_out, r_router, r_table, r_ub = unpack_dense(dense_g)
-    r_up = jnp.concatenate([owned_experts[0][:, 0], owned_experts[1][:, 0]], 0).astype(F32)
-    r_down = jnp.concatenate([owned_experts[0][:, 1], owned_experts[1][:, 1]], 0).astype(F32).reshape(E, gs * 4, D)
+    width = dense_g.shape[1]
+    dense_g = jnp.pad(dense_g, ((0, 0), (0, DENSE_PAD - width))).astype(BF16)[None]
+    e_out, d_out_g = ring_reduce_scatter([expert_sum, dense_g], group_size, 0)
+    e_red = lax.psum(e_out, "rx").reshape(2, 2, gs, F)
+    d_red = lax.psum(d_out_g[0, :, :width], ("rx", "core")).astype(F32)
+    r_qkv, r_out, r_router, r_table, r_ub = unpack_dense(d_red)
+    e_all = lax.all_gather(e_red, "core", axis=0, tiled=False).transpose(1, 0, 2, 3, 4).reshape(E, 2, gs, F)
+    r_up = e_all[:, 0].astype(F32)
+    r_down = e_all[:, 1].astype(F32).reshape(E, gs * 4, D)
 
     reduced = (r_qkv, r_out, r_router, r_up, r_ub, r_down, r_table)
     rates = (

time: 1000 us -> 871 us (0.87)
  waiting for transfers between devices: 496 us -> 253 us
  Pallas kernels: 0 us -> 107 us
  other arithmetic: 141 us -> 158 us
  matrix products: 185 us -> 174 us
    reduce_scatter x2 -> x0, waiting for transfers between devices: 184 us -> none  [shards(): packed = lax.psum_scatter(packed, 'group', scatter_dimension=2, tiled=True)]
    pallas_call x0 -> x1, Pallas kernels: none -> 107 us  [ring_reduce_scatter(): pl.pallas_call(functools.partial(ring_rs_kernel, groups, n_in), out_shape...]
    unnamed x15 -> x8, waiting for transfers between devices: 69.1 us -> 0.13 us
    psum x2, waiting for transfers between devices: 46.1 us -> 64.9 us  [the longest x1 36.8 us: shards(): e_red = lax.psum(e_out, 'rx').reshape(2, 2, gs, F)]
    unnamed x218 -> x240, local copies, waits for them, and re-layouts: 43.9 us -> 26.8 us
    another operation x10 -> x12, other arithmetic: 10.9 us -> 26.4 us  [the longest x1 6.23 us: shards(): packed = jnp.stack([g_up, g_down.reshape(2, D, F)], 1).astype(BF16)]
    convert_element_type x0 -> x3, local copies, waits for them, and re-layouts: none -> 11.8 us  [the longest x1 8.35 us: shards(): (jnp.stack(mine_list) + got.astype(F32)).astype(BF16).reshape(4, D, F)]
  transfers between devices with their start and end apart: 13 -> 9, of which waited for: 10 -> 6; matrix products, arithmetic and copies ran while one was open for 19% -> 20% of each run, Pallas kernels for 0% -> 0%
where the time goes in v2:
time: 871 us; the launch traced here: 864 us
  waiting for transfers between devices  253 us (29%)
  matrix products  174 us (20%)
  other arithmetic  158 us (18%)
  local copies, waits for them, and re-layouts  154 us (18%)
  Pallas kernels  107 us (12%)
  between operations  16.2 us (2%)
    all_gather x2, waiting for transfers between devices, shards(): piece = lax.all_gather(piece, 'group', axis=1, tiled=True)  143 us
    pallas_call x1, Pallas kernels, ring_reduce_scatter(): pl.pallas_call(functools.partial(ring_rs_kernel, groups, n_in), out_shape...  107 us
    convert_element_type x2, other arithmetic, shards(): h = gelu_exact(hp).astype(BF16)  64.6 us
    all_gather x1, waiting for transfers between devices, shards(): lax.all_gather(pack_dense(qkv_weight, out_weight, router_weight, vectors,...  42.1 us
    psum x1, waiting for transfers between devices, shards(): e_red = lax.psum(e_out, 'rx').reshape(2, 2, gs, F)  36.8 us
    dot_general x2, matrix products, shards(): jnp.einsum('ecd,efd->ecf', dy, w_down, preferred_element_type=F32)  28.9 us
    psum x1, waiting for transfers between devices, shards(): d_red = lax.psum(d_out_g[0, :, :width], ('rx', 'core')).astype(F32)  28 us
    unnamed x240, local copies, waits for them, and re-layouts  26.8 us
  transfers between devices with their start and end apart: 9, of which 6 were waited for; matrix products, arithmetic and copies ran while one was open for 20% of the time, Pallas kernels for 0%

profile of v2, /device:TPU:1, one launch (start us, length us, event | category | flops | bytes accessed | tf_op | source)
XLA Modules:
  0.0 863.6 jit_solution(9421177419508184522)
XLA Ops:
  13.7 71.7 %all-gather.11.cloned.1.call-done = bf16[2,512,2048]{2,1,0:T(8,128)(2,1)} async-done(((bf16[2,64,2048]{2,1,0:T(8,128)(2,1)}), bf16[2,512,2048]{2,1,0:T(8,128)(2,1)}) %all-gather.11.cloned.1.call-update) | async-done | bytes 4194320 | tf_op jit(solution)/shard_map/all_gather | solution.py:314
  85.7 2.3 reduce-window.6
  88.8 71.1 %all-gather.13.cloned.1.call-done = bf16[2,512,2048]{2,1,0:T(8,128)(2,1)} async-done(((bf16[2,64,2048]{2,1,0:T(8,128)(2,1)}), bf16[2,512,2048]{2,1,0:T(8,128)(2,1)}) %all-gather.13.cloned.1.call-update) | async-done | bytes 4194320 | tf_op jit(solution)/shard_map/all_gather | solution.py:314
  166.2 3.3 fusion.14
  169.5 42.1 %all-gather.9.cloned.1.call-done = bf16[512,2079]{1,0:T(8,128)(2,1)} async-done(((bf16[64,2079]{1,0:T(8,128)(2,1)}), bf16[512,2079]{1,0:T(8,128)(2,1)}) %all-gather.9.cloned.1.call-update) | async-done | bytes 2128912 | tf_op jit(solution)/shard_map/all_gather | solution.py:298
  213.7 3.0 add_convert_fusion.2
  219.7 2.5 copy.433
  224.3 2.2 copy.434
  226.5 3.6 reshape.409
  230.1 2.9 copy.435
  239.3 2.1 fusion.159
  243.1 17.3 %fusion.37 = bf16[2,1568,512]{2,1,0:T(8,128)(2,1)S(1)} fusion(s32[2,788]{1,0:T(2,128)S(1)} %multiply_add_fusion.8, bf16[2,394,512]{2,1,0:T(8,128)(2,1)S(1)} %reshape.374), kind=kOutput, calls=%fused_computation.96 | convolution fusion | flops 2537780480 | bytes 4024480 | tf_op jit(solution)/shard_map/mnr,mnd->mrd/dot_general | solution.py:332
  268.6 4.8 slice.334
  273.4 7.5 reshape_squeeze.6
  280.9 4.8 slice.339
  285.7 7.6 reshape_squeeze.7
  293.3 14.4 %fusion.50 = (u8[784,2048]{1,0:T(8,128)(4,1)}, u8[784,2048]{1,0:T(8,128)(4,1)}, f32[2,784,2048]{2,1,0:T(8,128)}) fusion(f32[2,2048]{1,0:T(2,128)S(1)} %slice.261, bf16[2,784,512]{2,1,0:T(8,128)(2,1)S(1)} %bitcast.278, bf16[2,2,512,2048]{3,2,1,0:T(8,128)(2,1)} %bitcast.272), kind=kOutput, calls=%fused_computation.109 | convolution fusion | flops 3330080768 | bytes 21872640 | tf_op jit(solution)/shard_map/ecd,edf->ecf/dot_general | solution.py:339
  307.8 10.9 %fusion.51 = (u8[784,2048]{1,0:T(8,128)(4,1)}, u8[784,2048]{1,0:T(8,128)(4,1)}, f32[2,784,2048]{2,1,0:T(8,128)S(1)}) fusion(f32[2,2048]{1,0:T(2,128)S(1)} %slice.268, bf16[2,784,512]{2,1,0:T(8,128)(2,1)S(1)} %bitcast.280, bf16[2,2,512,2048]{3,2,1,0:T(8,128)(2,1)} %bitcast.275), kind=kOutput, calls=%fused_computation.110 | convolution fusion | flops 3330080768 | bytes 21872640 | tf_op jit(solution)/shard_map/ecd,edf->ecf/dot_general | solution.py:339
  318.7 33.4 %multiply_convert_fusion.1 = (bf16[2,784,2048]{2,1,0:T(8,128)(2,1)S(1)}, f32[2,784,2048]{2,1,0:T(8,128)}) fusion(f32[2,784,2048]{2,1,0:T(8,128)} %get-tuple-element.281, f32[2,2048]{1,0:T(2,128)S(1)} %slice.261, u8[784,2048]{1,0:T(8,128)(4,1)} %get-tuple-element.189, u8[784,2048]{1,0:T(8,128)(4,1)} %get-tuple-element.188), kind=kLoop, calls=%fused_computation.38 | loop fusion | flops 227999744 | bytes 35340288 | tf_op jit(solution)/shard_map/convert_element_type | solution.py:340
  352.2 3.5 convolution_add_fusion.1
  356.4 31.1 %multiply_convert_fusion = (bf16[2,784,2048]{2,1,0:T(8,128)(2,1)S(1)}, f32[2,784,2048]{2,1,0:T(8,128)}) fusion(f32[2,784,2048]{2,1,0:T(8,128)S(1)} %get-tuple-element.280, f32[2,2048]{1,0:T(2,128)S(1)} %slice.268, u8[784,2048]{1,0:T(8,128)(4,1)S(1)} %copy-done.51, u8[784,2048]{1,0:T(8,128)(4,1)S(1)} %copy-done.50), kind=kLoop, calls=%fused_computation.25 | loop fusion | flops 227999744 | bytes 35340288 | tf_op jit(solution)/shard_map/convert_element_type | solution.py:340
  387.5 2.7 copy-done.30
  390.2 3.5 convolution_add_fusion
  396.6 6.1 fusion.15
  405.3 2.2 reshape.379
  407.5 2.2 multiply_reduce_fusion.5
  411.9 4.7 fusion.38
  418.3 6.9 fusion.163
  425.2 14.6 %fusion.162 = (bf16[2,2048]{1,0:T(2,128)(2,1)S(1)}, bf16[2,784,2048]{2,1,0:T(8,128)(2,1)}) fusion(f32[2,784,2048]{2,1,0:T(8,128)} %get-tuple-element.229, bf16[2,784,512]{2,1,0:T(8,128)(2,1)} %bitcast.283, bf16[2,2048,512]{2,1,0:T(8,128)(2,1)S(1)} %copy-done.36, f32[2,784,2048]{2,1,0:T(8,128)} %get-tuple-element.281, f32[2,2048]{1,0:T(2,128)S(1)} %slice.261), kind=kOutput, calls=%fused_computation.341 | convolution fusion | flops 3339710464 | bytes 37937152 | tf_op jit(solution)/shard_map/ecd,efd->ecf/dot_general | solution.py:366
  439.8 9.4 %fusion.39 = f32[2,784,512]{2,1,0:T(8,128)} fusion(bf16[2,784,2048]{2,1,0:T(8,128)(2,1)} %get-tuple-element.291, bf16[2,2,512,2048]{3,2,1,0:T(8,128)(2,1)} %bitcast.273), kind=kOutput, calls=%fused_computation.98 | convolution fusion | flops 3288334336 | bytes 13828096 | tf_op jit(solution)/shard_map/ecf,edf->ecd/dot_general | solution.py:371
  449.1 6.9 convolution_bitcast_fusion.1
  456.2 6.9 fusion.164
  463.1 14.4 %fusion.161 = (bf16[2,2048]{1,0:T(2,128)(2,1)}, bf16[2,784,2048]{2,1,0:T(8,128)(2,1)}) fusion(f32[2,784,2048]{2,1,0:T(8,128)} %get-tuple-element.231, bf16[2,784,512]{2,1,0:T(8,128)(2,1)S(1)} %bitcast.285, bf16[2,2048,512]{2,1,0:T(8,128)(2,1)S(1)} %copy-done.34, f32[2,784,2048]{2,1,0:T(8,128)} %copy-done.23, f32[2,2048]{1,0:T(2,128)S(1)} %slice.268), kind=kOutput, calls=%fused_computation.340 | convolution fusion | flops 3339710464 | bytes 37937152 | tf_op jit(solution)/shard_map/ecd,efd->ecf/dot_general | solution.py:366
  477.4 7.6 fusion.41
  485.1 7.0 convolution_bitcast_fusion
  496.2 3.4 fusion.26
  501.3 10.5 %stack_reshape.16 = f32[2,1,512,2048]{3,2,0,1:T(8,128)} reshape(f32[2,2048,512]{2,1,0:T(8,128)} %fusion.163) | data formatting | bytes 16777216 | tf_op jit(solution)/shard_map/stack;reshape | solution.py:402
  511.8 10.6 %stack_reshape.17 = f32[2,1,512,2048]{3,2,0,1:T(8,128)} reshape(f32[2,2048,512]{2,1,0:T(8,128)} %fusion.164) | data formatting | bytes 16777216 | tf_op jit(solution)/shard_map/stack;reshape | solution.py:402
  522.4 8.8 %fusion.18 = (bf16[1,2,512,2048]{3,2,0,1:T(8,128)(2,1)S(1)}, bf16[1,2,512,2048]{3,2,0,1:T(8,128)(2,1)}) fusion(s32[]{:T(128)S(6)} %select_n.32, f32[2,1,512,2048]{3,2,0,1:T(8,128)} %convolution_bitcast_fusion, f32[2,1,512,2048]{3,2,0,1:T(8,128)} %stack_reshape.17, f32[2,1,512,2048]{3,2,0,1:T(8,128)} %stack_reshape.16, ...), kind=kLoop, calls=%fused_computation.57 | loop fusion | flops 4194304 | bytes 41943044 | tf_op jit(solution)/shard_map/convert.39
  531.3 6.4 pad_maximum_fusion
  539.4 2.5 multiply_reduce_fusion.2
  549.6 4.2 fusion.95
  555.6 3.3 reshape.389
  558.8 7.7 multiply_reduce_fusion
  566.5 4.5 multiply_convert_fusion.2
  575.7 3.3 reshape.388
  592.1 2.4 reduce.2
  598.0 2.6 convolution_convert_fusion.2
  600.6 4.1 convolution_convert_fusion
  604.7 3.0 concatenate.67
  608.3 3.2 pad_bitcast_fusion.refs_1_
  611.5 6.5 fusion.19
  618.0 8.8 %fusion = bf16[2,2,512,2048]{3,2,0,1:T(8,128)(2,1)} fusion(f32[1,2,512,2048]{3,2,0,1:T(8,128)S(1)} %get-tuple-element.292, f32[1,2,512,2048]{3,2,0,1:T(8,128)S(1)} %get-tuple-element.293, bf16[2,2,512,2048]{3,2,0,1:T(8,128)(2,1)} %collective-permute-done), kind=kLoop, calls=%fused_computation.11 | loop fusion | flops 16777216 | bytes 33554432 | tf_op jit(solution)/shard_map/convert_element_type | solution.py:407
  626.9 8.3 copy.463
  635.2 106.6 %shard_map.344 = (bf16[4,64,2048]{2,1,0:T(8,128)(2,1)}, bf16[1,64,2304]{2,1,0:T(8,128)(2,1)}) custom-call(bf16[4,512,2048]{2,1,0:T(8,128)(2,1)} %bitcast.256, bf16[1,512,2304]{2,1,0:T(8,128)(2,1)} %pad_bitcast_fusion.refs_1_), custom_call_target="tpu_custom_call" | custom-call | flops 5373952 | bytes 32243712 | tf_op jit(solution)/shard_map/pallas_call | solution.py:142
  743.6 3.1 add_add_fusion.2
  746.8 28.0 %all-reduce.5.cloned.1.call-done = bf16[64,2079]{1,0:T(8,128)(2,1)} async-done(((bf16[64,2079]{1,0:T(8,128)(2,1)}), bf16[64,2079]{1,0:T(8,128)(2,1)}) %all-reduce.5.cloned.1.call-update) | async-done | bytes 266128 | tf_op jit(solution)/shard_map/psum | solution.py:413
  781.8 36.8 %all-reduce.7.cloned.1.call-done = bf16[1,2,2,64,2048]{4,3,2,1,0:T(8,128)(2,1)} async-done(((bf16[1,2,2,64,2048]{4,3,2,1,0:T(8,128)(2,1)}), bf16[1,2,2,64,2048]{4,3,2,1,0:T(8,128)(2,1)}) %all-reduce.7.cloned.1.call-update) | async-done | bytes 1048592 | tf_op jit(solution)/shard_map/psum | solution.py:412
  828.0 3.3 all-gather.15.cloned.1.call-done
  838.0 3.7 multiply_add_fusion.1
  843.1 3.5 fusion.60
  849.1 2.7 fusion.67
  851.8 2.5 pad_maximum_fusion.4
  854.3 2.3 pad_maximum_fusion.3
  (428 shorter events, 113.9 us)
Async XLA Ops:
  7.2 78.2 %all-gather.11.cloned.1.call-start = ((), (), s32[]{:S(2)}) async-start(), calls=%async_computation.1 | async-start | bytes 4718592 | tf_op jit(solution)/shard_map/all_gather | solution.py:314
  11.0 74.5 %copy-start.91 = (s32[788,2]{0,1:T(2,128)S(1)}, s32[788,2]{0,1:T(2,128)}, u32[]{:S(2)}) copy-start(s32[788,2]{0,1:T(2,128)} %param.19) | copy-start | bytes 18916
  11.0 148.9 %all-gather.13.cloned.1.call-start = ((), (), s32[]{:S(2)}) async-start(), calls=%async_computation.2 | async-start | bytes 4718592 | tf_op jit(solution)/shard_map/all_gather | solution.py:314
  11.0 77.6 %copy-start.98 = (f32[2,11,64]{2,0,1:T(2,128)S(1)}, f32[2,11,64]{2,0,1:T(2,128)}, u32[]{:S(2)}) copy-start(f32[2,11,64]{2,0,1:T(2,128)} %param.33) | copy-start | bytes 16900
  12.1 199.5 %all-gather.9.cloned.1.call-start = ((), (), s32[]{:S(2)}) async-start(), calls=%async_computation | async-start | bytes 2506752 | tf_op jit(solution)/shard_map/all_gather | solution.py:298
  12.3 73.2 %copy-start.68 = (f32[11,64]{0,1:T(8,128)}, f32[11,64]{0,1:T(8,128)S(1)}, u32[]{:S(2)}) copy-start(f32[11,64]{0,1:T(8,128)S(1)} %copy.426) | copy-start | bytes 8452
  13.7 254.9 %all-gather.17.cloned.1.call-start = ((), (), s32[]{:S(2)}) async-start(), calls=%async_computation.6 | async-start | bytes 12582912 | tf_op jit(solution)/shard_map/all_gather | solution.py:315
  85.4 74.5 %copy-start.101 = (f32[2,64,4]{1,2,0:T(4,128)S(1)}, f32[2,64,4]{1,2,0:T(4,128)}, u32[]{:S(2)}) copy-start(f32[2,64,4]{1,2,0:T(4,128)} %param.29) | copy-start | bytes 6148
  85.4 75.3 %copy-start.19 = (bf16[788,512]{1,0:T(8,128)(2,1)S(1)}, bf16[788,512]{1,0:T(8,128)(2,1)}, u32[]{:S(2)}) copy-start(bf16[788,512]{1,0:T(8,128)(2,1)} %param.18) | copy-start | bytes 2420740
  85.4 79.4 %copy-start.17 = (bf16[788,512]{1,0:T(8,128)(2,1)S(1)}, bf16[788,512]{1,0:T(8,128)(2,1)}, u32[]{:S(2)}) copy-start(bf16[788,512]{1,0:T(8,128)(2,1)} %param.17) | copy-start | bytes 2420740
  85.5 195.5 %all-gather.19.cloned.1.call-start = ((), (), s32[]{:S(2)}) async-start(), calls=%async_computation.7 | async-start | bytes 12582912 | tf_op jit(solution)/shard_map/all_gather | solution.py:315
  159.9 615.0 %all-reduce.5.cloned.1.call-start = ((), (), s32[]{:S(2)}) async-start(), calls=%async_computation.3 | async-start | bytes 557056 | tf_op jit(solution)/shard_map/psum | solution.py:413
  165.1 48.6 %copy-start.80 = (f32[788]{0:T(1024)}, f32[788]{0:T(1024)S(1)}, u32[]{:S(2)}) copy-start(f32[788]{0:T(1024)S(1)} %broadcast_multiply_fusion.1) | copy-start | bytes 9460
  166.1 47.6 %copy-start.86 = (f32[788]{0:T(1024)}, f32[788]{0:T(1024)S(1)}, u32[]{:S(2)}) copy-start(f32[788]{0:T(1024)S(1)} %fusion.134) | copy-start | bytes 9460
  213.6 28.2 %copy-start.89 = (f32[512]{0:T(512)}, f32[512]{0:T(512)S(1)}, u32[]{:S(2)}) copy-start(f32[512]{0:T(512)S(1)} %get-tuple-element.203) | copy-start | bytes 6148
  222.3 10.7 %copy-start.25 = (bf16[4,197,8,64]{1,3,2,0:T(8,128)(2,1)}, bf16[4,197,8,64]{1,3,2,0:T(8,128)(2,1)S(1)}, u32[]{:S(2)}) copy-start(bf16[4,197,8,64]{1,3,2,0:T(8,128)(2,1)S(1)} %copy.433) | copy-start | bytes 2420740
  226.5 7.5 copy-start.24
  241.5 19.0 %copy-start.72 = (f32[788]{0:T(1024)}, f32[788]{0:T(1024)S(1)}, u32[]{:S(2)}) copy-start(f32[788]{0:T(1024)S(1)} %broadcast_multiply_fusion) | copy-start | bytes 9460
  241.8 18.6 %copy-start.84 = (f32[788]{0:T(1024)}, f32[788]{0:T(1024)S(1)}, u32[]{:S(2)}) copy-start(f32[788]{0:T(1024)S(1)} %multiply_reduce_fusion.6) | copy-start | bytes 9460
  241.9 18.6 %copy-start.76 = (f32[788]{0:T(1024)}, f32[788]{0:T(1024)S(1)}, u32[]{:S(2)}) copy-start(f32[788]{0:T(1024)S(1)} %fusion.135) | copy-start | bytes 9460
  242.9 23.2 %copy-start.15 = (bf16[788,512]{1,0:T(8,128)(2,1)}, bf16[788,512]{1,0:T(8,128)(2,1)S(1)}, u32[]{:S(2)}) copy-start(bf16[788,512]{1,0:T(8,128)(2,1)S(1)} %add_convert_fusion.4) | copy-start | bytes 2420740
  285.7 7.6 copy-start.45
  293.3 14.4 %copy-start.47 = (bf16[2,2,392,512]{3,2,1,0:T(8,128)(2,1)S(1)}, bf16[2,2,392,512]{3,2,1,0:T(8,128)(2,1)}, u32[]{:S(2)}) copy-start(bf16[2,2,392,512]{3,2,1,0:T(8,128)(2,1)} %copy.443) | copy-start | bytes 4816900
  318.7 37.0 %copy-start.23 = (f32[2,784,2048]{2,1,0:T(8,128)}, f32[2,784,2048]{2,1,0:T(8,128)S(1)}, u32[]{:S(2)}) copy-start(f32[2,784,2048]{2,1,0:T(8,128)S(1)} %get-tuple-element.280) | copy-start | bytes 38535172
  318.7 33.5 %copy-start.35 = (bf16[2,2048,512]{2,1,0:T(8,128)(2,1)S(1)}, bf16[2,2048,512]{2,1,0:T(8,128)(2,1)}, u32[]{:S(2)}) copy-start(bf16[2,2048,512]{2,1,0:T(8,128)(2,1)} %reshape_squeeze.6) | copy-start | bytes 12582916
  356.4 33.9 %copy-start.33 = (bf16[2,2048,512]{2,1,0:T(8,128)(2,1)S(1)}, bf16[2,2048,512]{2,1,0:T(8,128)(2,1)}, u32[]{:S(2)}) copy-start(bf16[2,2048,512]{2,1,0:T(8,128)(2,1)} %reshape_squeeze.7) | copy-start | bytes 12582916
  407.4 9.2 %copy-start.9 = (f32[788,512]{1,0:T(8,128)}, f32[788,512]{1,0:T(8,128)S(1)}, u32[]{:S(2)}) copy-start(f32[788,512]{1,0:T(8,128)S(1)} %reshape.379) | copy-start | bytes 4841476
  409.9 8.4 slice-start.4
  439.7 9.4 %copy-start.46 = (bf16[2,2,392,512]{3,2,1,0:T(8,128)(2,1)S(1)}, bf16[2,2,392,512]{3,2,1,0:T(8,128)(2,1)}, u32[]{:S(2)}) copy-start(bf16[2,2,392,512]{3,2,1,0:T(8,128)(2,1)} %copy.438) | copy-start | bytes 4816900
  439.7 9.4 %copy-start.104 = (bf16[2,784,2048]{2,1,0:T(8,128)(2,1)S(1)}, bf16[2,784,2048]{2,1,0:T(8,128)(2,1)}, u32[]{:S(2)}) copy-start(bf16[2,784,2048]{2,1,0:T(8,128)(2,1)} %get-tuple-element.291) | copy-start | bytes 19267588
  439.7 16.4 %slice-start.2 = ((s8[6422528]{0:T(1024)(128)(4,1)}), s8[4194304]{0:T(1024)(128)(4,1)S(1)}, s32[]{:S(2)}) async-start(s8[6422528]{0:T(1024)(128)(4,1)} %bitcast.264), calls=%async_computation.10 | async-start | bytes 8388608
  449.1 7.0 slice-start.3
  477.4 7.6 copy-start.48
  477.4 7.6 copy-start.105
  485.1 7.0 copy-start.67
  485.1 7.0 copy-start.75
  485.1 7.0 copy-start.79
  485.1 7.0 copy-start.42
  531.2 8.2 copy-start.4
  531.2 8.2 copy-start.73
  531.2 8.2 copy-start.77
  531.2 8.2 copy-start.90
  537.7 80.3 %collective-permute-start = (bf16[2,2,512,2048]{3,2,0,1:T(8,128)(2,1)}, bf16[2,2,512,2048]{3,2,0,1:T(8,128)(2,1)}, u32[]{:S(2)}, u32[]{:S(2)}) collective-permute-start(bf16[2,2,512,2048]{3,2,0,1:T(8,128)(2,1)} %pad_maximum_fusion), channel_id=1, source_target_pairs={{0,8},{8,0},{1,9},{9,1},{2,10},{10,2},{3,11},{11,3},{4,12},{12,4},... | collective-permute-start | bytes 25165832 | tf_op jit(solution)/shard_map/ppermute | solution.py:406
  555.6 11.0 %slice-start = ((s8[6553600]{0:T(1024)(128)(4,1)}), s8[2359296]{0:T(1024)(128)(4,1)S(1)}, s32[]{:S(2)}) async-start(s8[6553600]{0:T(1024)(128)(4,1)} %bitcast.254), calls=%async_computation.8 | async-start | bytes 4718592
  558.8 7.7 slice-start.1
  590.0 6.9 copy-start.16
  590.0 8.0 copy-start.56
  592.1 8.5 copy-start.103
  635.2 108.4 %copy-start.12 = (f32[788,512]{1,0:T(8,128)S(1)}, f32[788,512]{1,0:T(8,128)}, u32[]{:S(2)}) copy-start(f32[788,512]{1,0:T(8,128)} %copy-done.11) | copy-start | bytes 4841476
  635.2 108.4 %copy-start.21 = (bf16[788,512]{1,0:T(8,128)(2,1)S(1)}, bf16[788,512]{1,0:T(8,128)(2,1)}, u32[]{:S(2)}) copy-start(bf16[788,512]{1,0:T(8,128)(2,1)} %param.18) | copy-start | bytes 2420740
  743.5 32.4 %copy-start.69 = (f32[11,64]{0,1:T(8,128)S(1)}, f32[11,64]{0,1:T(8,128)}, u32[]{:S(2)}) copy-start(f32[11,64]{0,1:T(8,128)} %copy-done.68) | copy-start | bytes 8452
  743.5 79.4 %copy-start.58 = (f32[2,64,512]{2,1,0:T(8,128)S(1)}, f32[2,64,512]{2,1,0:T(8,128)}, u32[]{:S(2)}) copy-start(f32[2,64,512]{2,1,0:T(8,128)} %param.28) | copy-start | bytes 786436
  743.5 75.1 %all-reduce.7.cloned.1.call-start = ((), (), s32[]{:S(2)}) async-start(), calls=%async_computation.4 | async-start | bytes 2097152 | tf_op jit(solution)/shard_map/psum | solution.py:412
  746.7 72.8 %copy-start.70 = (f32[64,4]{1,0:T(8,128)S(1)}, f32[64,4]{1,0:T(8,128)}, u32[]{:S(2)}) copy-start(f32[64,4]{1,0:T(8,128)} %copy.475) | copy-start | bytes 3076
  746.7 77.1 %copy-start.64 = (f32[64,512]{1,0:T(8,128)S(1)}, f32[64,512]{1,0:T(8,128)}, u32[]{:S(2)}) copy-start(f32[64,512]{1,0:T(8,128)} %param.21) | copy-start | bytes 393220
  746.7 78.6 %copy-start.88 = (f32[2,4,256]{2,1,0:T(4,128)S(1)}, f32[2,4,256]{2,1,0:T(4,128)}, u32[]{:S(2)}) copy-start(f32[2,4,256]{2,1,0:T(4,128)} %param.31) | copy-start | bytes 24580
  746.7 78.6 %copy-start.97 = (f32[4,256]{1,0:T(4,128)S(1)}, f32[4,256]{1,0:T(4,128)}, u32[]{:S(2)}) copy-start(f32[4,256]{1,0:T(4,128)} %param.24) | copy-start | bytes 12292
  746.7 79.2 %copy-start.44 = (f32[2,64,1536]{2,1,0:T(8,128)S(1)}, f32[2,64,1536]{2,1,0:T(8,128)}, u32[]{:S(2)}) copy-start(f32[2,64,1536]{2,1,0:T(8,128)} %param.27) | copy-start | bytes 2359300
  746.7 79.3 %copy-start.53 = (f32[64,1536]{1,0:T(8,128)S(1)}, f32[64,1536]{1,0:T(8,128)}, u32[]{:S(2)}) copy-start(f32[64,1536]{1,0:T(8,128)} %param.20) | copy-start | bytes 1179652
  746.8 84.5 %all-gather.15.cloned.1.call-start = ((), (), s32[]{:S(2)}) async-start(), calls=%async_computation.5 | async-start | bytes 3145728 | tf_op jit(solution)/shard_map/all_gather | solution.py:415
  774.8 51.1 %copy-start.43 = (bf16[64,2079]{1,0:T(8,128)(2,1)S(1)}, bf16[64,2079]{1,0:T(8,128)(2,1)}, u32[]{:S(2)}) copy-start(bf16[64,2079]{1,0:T(8,128)(2,1)} %all-reduce.5.cloned.1.call-done) | copy-start | bytes 798340
  819.4 13.6 %copy-start.95 = (f32[4,256]{1,0:T(4,128)}, f32[4,256]{1,0:T(4,128)S(1)}, u32[]{:S(2)}) copy-start(f32[4,256]{1,0:T(4,128)S(1)} %reshape.399) | copy-start | bytes 12292
  823.8 9.2 %copy-start.65 = (f32[64,512]{1,0:T(8,128)}, f32[64,512]{1,0:T(8,128)S(1)}, u32[]{:S(2)}) copy-start(f32[64,512]{1,0:T(8,128)S(1)} %get-tuple-element.215) | copy-start | bytes 393220
  826.0 8.6 copy-start.54
  (59 other events, 212.9 us)
Sparse Core Ops, SparseCore 0:
  11.1 74.2 all-gather.10
  88.2 71.6 all-gather.12
  162.6 48.9 all-gather.8
  213.0 19.8 all-gather.16
  234.3 21.0 all-gather.18
  743.6 31.1 all-reduce.4
  777.1 41.5 all-reduce.6
  820.3 10.9 all-gather.14

commit v3 on v2

--- a/solution.py
+++ b/solution.py
@@ -18,6 +18,7 @@
 MB_TOK = 394
 CAP = 392
 NV = 11
+DENSE_AG = 2560
 DENSE_PAD = 2304
 F32 = jnp.float32
 BF16 = jnp.bfloat16
@@ -152,6 +153,138 @@
     )(*xs)
 
 
+def ring_ag_kernel(groups, *refs):
+    in_up, in_down, in_dense, out_up, out_down, out_dense = refs[:6]
+    ring_send, ring_recv, part_send, part_recv, local_sem = refs[6:]
+    pos_of, dev_at = ring_order(groups)
+    rx = lax.axis_index("rx")
+    core = lax.axis_index("core")
+    g = lax.axis_index("group")
+    other = 1 - core
+    pos = pos_of(g)
+    nbr = (dev_at(pos + 1), dev_at(pos + groups - 1))
+    gs = in_up.shape[1]
+    fs = in_down.shape[1]
+    width = in_dense.shape[1] // 2
+
+    barrier = pltpu.get_barrier_semaphore()
+    for n in nbr:
+        pl.semaphore_signal(barrier, inc=1, device_id=(rx, core, n), device_id_type=MESH_ID)
+    pl.semaphore_signal(barrier, inc=1, device_id=(rx, other, g), device_id_type=MESH_ID)
+    pl.semaphore_wait(barrier, 3)
+
+    def items(owner):
+        found = []
+        for k in range(2):
+            e = 2 * k + owner
+            found.append((in_up.at[e], lambda b, e=e: out_up.at[e, pl.ds(pl.multiple_of(b * gs, gs), gs)], F // 2))
+            found.append((in_down.at[e], lambda b, e=e: out_down.at[e, pl.ds(pl.multiple_of(b * fs, fs), fs)], D // 2))
+        dense_in = in_dense.at[:, pl.ds(owner * width, width)]
+        found.append(
+            (dense_in, lambda b: out_dense.at[pl.ds(pl.multiple_of(b * gs, gs), gs), pl.ds(owner * width, width)], width // 2)
+        )
+        return found
+
+    mine = items(core)
+    theirs = items(other)
+    n_items = len(mine)
+
+    locals_ = [pltpu.make_async_copy(in_up.at[e], out_up.at[e, pl.ds(pl.multiple_of(g * gs, gs), gs)], local_sem.at[e]) for e in range(E)]
+    locals_ += [
+        pltpu.make_async_copy(in_down.at[e], out_down.at[e, pl.ds(pl.multiple_of(g * fs, fs), fs)], local_sem.at[E + e])
+        for e in range(E)
+    ]
+    locals_.append(pltpu.make_async_copy(in_dense, out_dense.at[pl.ds(pl.multiple_of(g * gs, gs), gs)], local_sem.at[2 * E]))
+    for c in locals_:
+        c.start()
+
+    def block_at(d, s):
+        if d == 0:
+            return dev_at(pos + 2 * groups - 1 - s)
+        return dev_at(pos + 1 + s)
+
+    def ring_copy(d, s, j, src_block):
+        src_in, dst_of, half = mine[j]
+        cols = pl.ds(d * half, half)
+        if src_block is None:
+            src = src_in.at[:, cols]
+            dst = dst_of(g).at[:, cols]
+        else:
+            src = dst_of(src_block).at[:, cols]
+            dst = src
+        return pltpu.make_async_remote_copy(
+            src_ref=src, dst_ref=dst, send_sem=ring_send.at[d, s, j], recv_sem=ring_recv.at[d, s, j],
+            device_id=(rx, core, nbr[d]), device_id_type=MESH_ID,
+        )
+
+    def part_copy(d, s, j, table, block):
+        _, dst_of, half = table[j]
+        view = dst_of(block).at[:, pl.ds(d * half, half)]
+        return pltpu.make_async_remote_copy(
+            src_ref=view, dst_ref=view, send_sem=part_send.at[d, s, j], recv_sem=part_recv.at[d, s, j],
+            device_id=(rx, other, g), device_id_type=MESH_ID,
+        )
+
+    sends = []
+    for d in range(2):
+        for j in range(n_items):
+            c = ring_copy(d, 0, j, None)
+            c.start()
+            sends.append(c)
+    for s in range(groups - 1):
+        for d in range(2):
+            b = block_at(d, s)
+            for j in range(n_items):
+                pltpu.make_async_remote_copy(
+                    src_ref=mine[j][1](b).at[:, pl.ds(d * mine[j][2], mine[j][2])],
+                    dst_ref=mine[j][1](b).at[:, pl.ds(d * mine[j][2], mine[j][2])],
+                    send_sem=ring_send.at[d, s, j], recv_sem=ring_recv.at[d, s, j],
+                    device_id=(rx, core, nbr[d]), device_id_type=MESH_ID,
+                ).wait_recv()
+                if s + 1 < groups - 1:
+                    c = ring_copy(d, s + 1, j, b)
+                    c.start()
+                    sends.append(c)
+                c = part_copy(d, s, j, mine, b)
+                c.start()
+                sends.append(c)
+    for s in range(groups - 1):
+        for d in range(2):
+            b = block_at(d, s)
+            for j in range(n_items):
+                part_copy(d, s, j, theirs, b).wait_recv()
+    for c in sends:
+        c.wait_send()
+    for c in locals_:
+        c.wait()
+
+
+def ring_all_gather(up_b, down_b, dense_b, groups, collective_id):
+    n_items = 5
+    gs = up_b.shape[1]
+    shapes = [
+        jax.ShapeDtypeStruct((E, gs * groups, F), BF16),
+        jax.ShapeDtypeStruct((E, down_b.shape[1] * groups, D), BF16),
+        jax.ShapeDtypeStruct((gs * groups, dense_b.shape[1]), BF16),
+    ]
+    nbytes = sum(int(np.prod(s.shape)) * 2 for s in shapes)
+    return pl.pallas_call(
+        functools.partial(ring_ag_kernel, groups),
+        out_shape=shapes,
+        in_specs=[pl.BlockSpec(memory_space=pl.ANY)] * 3,
+        out_specs=[pl.BlockSpec(memory_space=pl.ANY)] * 3,
+        scratch_shapes=[
+            pltpu.SemaphoreType.DMA((2, groups - 1, n_items)),
+            pltpu.SemaphoreType.DMA((2, groups - 1, n_items)),
+            pltpu.SemaphoreType.DMA((2, groups - 1, n_items)),
+            pltpu.SemaphoreType.DMA((2, groups - 1, n_items)),
+            pltpu.SemaphoreType.DMA((2 * E + 1,)),
+        ],
+        compiler_params=pltpu.CompilerParams(collective_id=collective_id, has_side_effects=True),
+        cost_estimate=pl.CostEstimate(flops=0, bytes_accessed=nbytes, transcendentals=0),
+    )(up_b, down_b, dense_b)
+
+
 def layer_norm(value, gain, shift):
     center = value - jnp.mean(value, -1, keepdims=True)
     spread = jnp.mean(center * center, -1, keepdims=True)
@@ -295,25 +428,15 @@
     group_size = D // gs
     core = lax.axis_index("core")
 
-    dense = lax.all_gather(
-        pack_dense(qkv_weight, out_weight, router_weight, vectors, up_bias).astype(BF16),
-        "group",
-        axis=0,
-        tiled=True,
-    )
-    w_qkv, w_out, w_router, table_b, b_up_b = unpack_dense(dense)
+    dense_in = pack_dense(qkv_weight, out_weight, router_weight, vectors, up_bias)
+    width = dense_in.shape[1]
+    dense_in = jnp.pad(dense_in, ((0, 0), (0, DENSE_AG - width))).astype(BF16)
+    w_up_all, w_down_all, dense = ring_all_gather(
+        up_weight.astype(BF16), down_weight.astype(BF16), dense_in, group_size, 1
+    )
+    w_qkv, w_out, w_router, table_b, b_up_b = unpack_dense(dense[:, :width])
     table = table_b.astype(F32)
     b_up = b_up_b.astype(F32)
-
-    chunk_w = []
-    for k in range(2):
-        e = 2 * k + core
-        up_piece = lax.dynamic_index_in_dim(up_weight, e, 0, keepdims=False)
-        down_piece = lax.dynamic_index_in_dim(down_weight, e, 0, keepdims=False).reshape(gs, F)
-        piece = jnp.stack([up_piece, down_piece]).astype(BF16)
-        piece = lax.all_gather(piece, "group", axis=1, tiled=True)
-        piece = lax.all_gather(piece, "core", axis=0, tiled=False)
-        chunk_w.append((piece[:, 0], piece[:, 1].reshape(2, F, D)))
 
     value = tokens.astype(F32)
     d_out = cotangent.astype(F32)
@@ -332,17 +455,9 @@
     table_in = jnp.einsum("mnr,mnd->mrd", onehot, pair, preferred_element_type=F32).astype(BF16)
     table_in = table_in.reshape(micro, E, CAP, D).transpose(1, 0, 2, 3).reshape(E, micro * CAP, D)
 
-    hidden_pre, hidden, expert_out = [], [], []
-    for k in range(2):
-        w_up, w_down = chunk_w[k]
-        t_in = table_in[2 * k : 2 * k + 2]
-        hp = jnp.einsum("ecd,edf->ecf", t_in, w_up, preferred_element_type=F32) + b_up[2 * k : 2 * k + 2, None, :]
-        h = gelu_exact(hp).astype(BF16)
-        y = jnp.einsum("ecf,efd->ecd", h, w_down, preferred_element_type=F32) + table[7 + 2 * k : 9 + 2 * k][:, None, :]
-        hidden_pre.append(hp)
-        hidden.append(h)
-        expert_out.append(y)
-    y_all = jnp.concatenate(expert_out, 0)
+    hidden_pre = jnp.einsum("ecd,edf->ecf", table_in, w_up_all, preferred_element_type=F32) + b_up[:, None, :]
+    hidden = gelu_exact(hidden_pre).astype(BF16)
+    y_all = jnp.einsum("ecf,efd->ecd", hidden, w_down_all, preferred_element_type=F32) + table[7 : 7 + E][:, None, :]
     y_m = y_all.reshape(E, micro, CAP, D).transpose(1, 0, 2, 3).reshape(micro, E * CAP, D)
     picked_rows = pick_rows(onehot, y_m)
     out_zero = picked_rows[:, :MB_TOK].reshape(rows, D)
@@ -357,21 +472,14 @@
     d_expert = d_expert.reshape(micro, E, CAP, D).transpose(1, 0, 2, 3).reshape(E, micro * CAP, D)
     g_bias_down = jnp.sum(d_expert.astype(F32), 1)
 
-    d_tables = []
-    expert_grads = []
-    for k in range(2):
-        w_up, w_down = chunk_w[k]
-        dy = d_expert[2 * k : 2 * k + 2]
-        g_down = jnp.einsum("ecf,ecd->efd", hidden[k], dy, preferred_element_type=F32)
-        d_hidden = jnp.einsum("ecd,efd->ecf", dy, w_down, preferred_element_type=F32)
-        gelu_pull = jax.vjp(gelu_exact, hidden_pre[k])[1]
-        d_pre = gelu_pull(d_hidden)[0].astype(BF16)
-        g_up_bias = jnp.sum(d_pre.astype(F32), 1)
-        g_up = jnp.einsum("ecd,ecf->edf", table_in[2 * k : 2 * k + 2], d_pre, preferred_element_type=F32)
-        d_tables.append(jnp.einsum("ecf,edf->ecd", d_pre, w_up, preferred_element_type=F32))
-        expert_grads.append((g_up, g_down, g_up_bias))
-
-    d_table = jnp.concatenate(d_tables, 0)
+    g_down = jnp.einsum("ecf,ecd->efd", hidden, d_expert, preferred_element_type=F32)
+    d_hidden = jnp.einsum("ecd,efd->ecf", d_expert, w_down_all, preferred_element_type=F32)
+    gelu_pull = jax.vjp(gelu_exact, hidden_pre)[1]
+    d_pre = gelu_pull(d_hidden)[0].astype(BF16)
+    g_up_bias_all = jnp.sum(d_pre.astype(F32), 1)
+    g_up = jnp.einsum("ecd,ecf->edf", table_in, d_pre, preferred_element_type=F32)
+    d_table = jnp.einsum("ecf,edf->ecd", d_pre, w_up_all, preferred_element_type=F32)
+
     d_table_m = d_table.reshape(E, micro, CAP, D).transpose(1, 0, 2, 3).reshape(micro, E * CAP, D)
     onehot_sum = onehot[:, :MB_TOK] + onehot[:, MB_TOK:]
     d_picked = pick_rows(onehot_sum, d_table_m).reshape(rows, D)
@@ -395,16 +503,11 @@
         ],
         0,
     )
-    g_up_bias_all = jnp.concatenate([expert_grads[0][2], expert_grads[1][2]], 0)
-    mine_list, send_list = [], []
-    for k in range(2):
-        g_up, g_down, _ = expert_grads[k]
-        both = jnp.stack([g_up, g_down.reshape(2, D, F)], 1)
-        mine_list.append(lax.dynamic_index_in_dim(both, core, 0, keepdims=False))
-        send_list.append(lax.dynamic_index_in_dim(both, 1 - core, 0, keepdims=False))
-    sent = jnp.stack(send_list).astype(BF16)
+    both = jnp.stack([g_up, g_down.reshape(E, D, F)], 1).reshape(2, 2, 2, D, F)
+    sent = lax.dynamic_index_in_dim(both, 1 - core, 1, keepdims=False).astype(BF16)
     got = lax.ppermute(sent, "core", [(0, 1), (1, 0)])
-    expert_sum = (jnp.stack(mine_list) + got.astype(F32)).astype(BF16).reshape(4, D, F)
+    mine = lax.dynamic_index_in_dim(both, core, 1, keepdims=False)
+    expert_sum = (mine + got.astype(F32)).astype(BF16).reshape(4, D, F)
     dense_g = pack_dense(g_qkv, g_out, g_router, g_table, g_up_bias_all)
     width = dense_g.shape[1]
     dense_g = jnp.pad(dense_g, ((0, 0), (0, DENSE_PAD - width))).astype(BF16)[None]

time: 871 us -> 729 us (0.84)
  waiting for transfers between devices: 253 us -> 76.2 us
  Pallas kernels: 107 us -> 208 us
  local copies, waits for them, and re-layouts: 154 us -> 114 us
  other arithmetic: 158 us -> 141 us
    all_gather x5 -> x0, waiting for transfers between devices: 185 us -> none  [the longest x2 143 us: shards(): piece = lax.all_gather(piece, 'group', axis=1, tiled=True)]
    pallas_call x0 -> x1, Pallas kernels: none -> 101 us  [ring_all_gather(): pl.pallas_call(functools.partial(ring_ag_kernel, groups), out_shape=shape...]
    another operation x14 -> x10, other arithmetic: 28.1 us -> 4.49 us
    another operation x12 -> x6, local copies, waits for them, and re-layouts: 40.2 us -> 21.4 us  [the longest x1 20.4 us: shards(): both = jnp.stack([g_up, g_down.reshape(E, D, F)], 1).reshape(2, 2, 2, D, F)]
    slice x17 -> x3, local copies, waits for them, and re-layouts: 14.9 us -> 0.52 us  [the longest x2 9.58 us: shards(): chunk_w.append((piece[:, 0], piece[:, 1].reshape(2, F, D)))]
    convert_element_type x3 -> x6, other arithmetic: 73.4 us -> 87.7 us  [the longest x1 61.5 us: shards(): hidden = gelu_exact(hidden_pre).astype(BF16)]
    dot_general x1, matrix products: 17.3 us -> 5.05 us  [shards(): jnp.einsum('mnr,mnd->mrd', onehot, pair, preferred_element_type=F32)]
    dot_general x12 -> x6, matrix products: 106 us -> 111 us  [the longest x1 28.2 us: shards(): jnp.einsum('ecd,efd->ecf', d_expert, w_down_all, preferred_element_type=F32)]
  transfers between devices with their start and end apart: 9 -> 4, of which waited for: 6 -> 3; matrix products, arithmetic and copies ran while one was open for 20% -> 15% of each run, Pallas kernels for 0% -> 0%
where the time goes in v3:
time: 729 us; the launch traced here: 722 us
  Pallas kernels  208 us (29%)
  matrix products  167 us (23%)
  other arithmetic  141 us (19%)
  local copies, waits for them, and re-layouts  114 us (16%)
  waiting for transfers between devices  76.2 us (10%)
  between operations  15.6 us (2%)
    pallas_call x1, Pallas kernels, ring_reduce_scatter(): pl.pallas_call(functools.partial(ring_rs_kernel, groups, n_in), out_shape...  107 us
    pallas_call x1, Pallas kernels, ring_all_gather(): pl.pallas_call(functools.partial(ring_ag_kernel, groups), out_shape=shape...  101 us
    convert_element_type x1, other arithmetic, shards(): hidden = gelu_exact(hidden_pre).astype(BF16)  61.5 us
    psum x1, waiting for transfers between devices, shards(): e_red = lax.psum(e_out, 'rx').reshape(2, 2, gs, F)  39.8 us
    psum x1, waiting for transfers between devices, shards(): d_red = lax.psum(d_out_g[0, :, :width], ('rx', 'core')).astype(F32)  31 us
    dot_general x1, matrix products, shards(): jnp.einsum('ecd,efd->ecf', d_expert, w_down_all, preferred_element_type=F32)  28.2 us
    dot_general x1, matrix products, shards(): jnp.einsum('ecd,edf->ecf', table_in, w_up_all, preferred_element_type=F32)  23.9 us
    unnamed x215, local copies, waits for them, and re-layouts  22.1 us
  transfers between devices with their start and end apart: 4, of which 3 were waited for; matrix products, arithmetic and copies ran while one was open for 15% of the time, Pallas kernels for 0%

profile of v3, /device:TPU:1, one launch (start us, length us, event | category | flops | bytes accessed | tf_op | source)
XLA Modules:
  0.0 721.7 jit_solution(4220967705174987719)
XLA Ops:
  7.3 2.9 convert_element_type.192.refs_0_
  12.9 101.1 %shard_map.344 = (bf16[4,512,2048]{2,1,0:T(8,128)(2,1)}, bf16[4,2048,512]{2,1,0:T(8,128)(2,1)}, bf16[512,2560]{1,0:T(8,128)(2,1)}) custom-call(bf16[4,64,2048]{2,1,0:T(8,128)(2,1)} %convert_element_type.192.refs_0_, bf16[4,256,512]{2,1,0:T(8,128)(2,1)} %convert_element_type.193.refs_1_, bf16[64,2560]{1,0:T(8,128)(2,1)} %pad.14.refs_2_), custom_call_target="tpu_custom_call" | custom-call | bytes 19398656 | tf_op jit(solution)/shard_map/pallas_call | solution.py:271
  120.1 2.0 reshape.416
  122.0 2.2 copy.350
  124.3 2.0 reshape.417
  126.3 2.0 copy.351
  128.3 3.5 reshape.415
  131.8 2.8 copy.352
  141.8 2.1 fusion.140
  148.5 2.3 reduce-window.6
  151.7 5.0 fusion.31
  156.8 2.0 copy.355
  160.0 23.9 %fusion.25 = (u8[784,2048]{1,0:T(8,128)(4,1)S(1)}, u8[784,2048]{1,0:T(8,128)(4,1)S(1)}, f32[4,784,2048]{2,1,0:T(8,128)}) fusion(f32[4,2048]{1,0:T(4,128)S(1)} %reshape.409, bf16[4,784,512]{2,1,0:T(8,128)(2,1)} %bitcast.240, bf16[4,512,2048]{2,1,0:T(8,128)(2,1)} %get-tuple-element.29), kind=kOutput, calls=%fused_computation.56 | convolution fusion | flops 6663372800 | bytes 40534016 | tf_op jit(solution)/shard_map/ecd,edf->ecf/dot_general | solution.py:458
  183.9 61.5 %multiply_convert_fusion = (bf16[4,784,2048]{2,1,0:T(8,128)(2,1)S(1)}, f32[4,784,2048]{2,1,0:T(8,128)}) fusion(f32[4,784,2048]{2,1,0:T(8,128)} %get-tuple-element.247, f32[4,2048]{1,0:T(4,128)S(1)} %reshape.409, u8[784,2048]{1,0:T(8,128)(4,1)S(1)} %get-tuple-element.172, u8[784,2048]{1,0:T(8,128)(4,1)S(1)} %get-tuple-element.171), kind=kLoop, calls=%fused_computation.12 | loop fusion | flops 455999488 | bytes 67469312 | tf_op jit(solution)/shard_map/convert_element_type | solution.py:459
  245.4 12.5 %broadcast_add_fusion = f32[4,784,512]{2,1,0:T(8,128)S(1)} fusion(f32[4,512]{1,0:T(4,128)S(1)} %copy.358, bf16[4,784,2048]{2,1,0:T(8,128)(2,1)S(1)} %get-tuple-element.209, bf16[4,2048,512]{2,1,0:T(8,128)(2,1)} %get-tuple-element.30), kind=kOutput, calls=%fused_computation.73 | convolution fusion | flops 6578274304 | bytes 27664384 | tf_op jit(solution)/shard_map/ecf,efd->ecd/dot_general | solution.py:460
  259.8 6.1 fusion.12
  266.7 2.1 fusion.136
  268.8 1.6 reshape.384
  270.4 1.6 reshape.385
  272.0 3.0 reshape.387
  275.0 1.6 multiply_reduce_fusion.5
  276.8 1.7 multiply_convert_fusion.5
  278.5 4.7 fusion.32
  284.9 16.4 %fusion.145 = f32[4,2048,512]{2,1,0:T(8,128)} fusion(bf16[4,784,2048]{2,1,0:T(8,128)(2,1)} %copy-done.19, bf16[4,784,512]{2,1,0:T(8,128)(2,1)S(1)} %bitcast.242), kind=kOutput, calls=%fused_computation.293 | convolution fusion | flops 6576668672 | bytes 32833536 | tf_op jit(solution)/shard_map/ecf,ecd->efd/dot_general | solution.py:475
  301.3 28.2 %fusion.142 = (bf16[4,2048]{1,0:T(4,128)(2,1)}, bf16[4,784,2048]{2,1,0:T(8,128)(2,1)}) fusion(f32[4,784,2048]{2,1,0:T(8,128)} %get-tuple-element.210, bf16[4,784,512]{2,1,0:T(8,128)(2,1)} %bitcast.243, bf16[4,2048,512]{2,1,0:T(8,128)(2,1)} %get-tuple-element.30, f32[4,784,2048]{2,1,0:T(8,128)} %get-tuple-element.247, f32[4,2048]{1,0:T(4,128)S(1)} %reshape.409), kind=kOutput, calls=%fused_computation.290 | convolution fusion | flops 6679420928 | bytes 75874304 | tf_op jit(solution)/shard_map/ecd,efd->ecf/dot_general | solution.py:476
  329.5 20.4 %stack.92 = f32[2,2,1,512,2048]{4,3,1,0,2:T(8,128)} reshape(f32[4,2048,512]{2,1,0:T(8,128)} %fusion.145) | data formatting | bytes 33554432 | tf_op jit(solution)/shard_map/stack | solution.py:506
  349.8 17.8 %fusion.144 = f32[4,512,2048]{2,1,0:T(8,128)} fusion(bf16[4,784,512]{2,1,0:T(8,128)(2,1)} %bitcast.241, bf16[4,784,2048]{2,1,0:T(8,128)(2,1)} %get-tuple-element.255), kind=kOutput, calls=%fused_computation.292 | convolution fusion | flops 6576668672 | bytes 32833536 | tf_op jit(solution)/shard_map/ecd,ecf->edf/dot_general | solution.py:480
  367.7 9.1 %fusion.14 = bf16[2,2,512,2048]{3,2,1,0:T(8,128)(2,1)} fusion(s32[]{:T(128)S(6)} %select_n.18, f32[2,2,1,512,2048]{4,3,1,0,2:T(8,128)} %bitcast.230, f32[2,2,1,512,2048]{4,3,1,0,2:T(8,128)} %stack.92), kind=kLoop, calls=%fused_computation.36 | loop fusion | flops 4194304 | bytes 41943044 | tf_op jit(solution)/shard_map/convert_element_type | solution.py:507
  376.8 12.3 %fusion.143 = f32[4,784,512]{2,1,0:T(8,128)S(1)} fusion(bf16[4,784,2048]{2,1,0:T(8,128)(2,1)} %get-tuple-element.255, bf16[4,512,2048]{2,1,0:T(8,128)(2,1)} %get-tuple-element.29), kind=kOutput, calls=%fused_computation.291 | convolution fusion | flops 6576668672 | bytes 27656192 | tf_op jit(solution)/shard_map/ecf,edf->ecd/dot_general | solution.py:481
  392.3 3.6 fusion.18
  398.4 2.7 reshape.392
  401.2 3.1 multiply_reduce_fusion.2
  404.3 1.7 fusion.134
  409.0 1.7 convolution_convert_fusion.1
  412.6 4.2 fusion.81
  416.7 1.8 copy.373
  418.5 3.3 reshape.396
  421.8 7.7 %multiply_reduce_fusion = (f32[4,8,197]{2,1,0:T(8,128)S(1)}, f32[4,8,197,197]{2,3,1,0:T(8,128)}) fusion(f32[4,8,197,197]{2,3,1,0:T(8,128)} %copy-done, f32[4,8,197]{2,1,0:T(8,128)S(1)} %log_add_fusion, bf16[4,197,8,64]{1,3,2,0:T(8,128)(2,1)S(1)} %copy.363, bf16[4,197,8,64]{1,3,2,0:T(8,128)(2,1)} %copy.352), kind=kOutput, calls=%fused_computation.38 | convolution fusion | flops 163922912 | bytes 11599360 | tf_op jit(solution)/shard_map/bqhd,bkhd->bhqk/dot_general | solution.py:382
  429.5 4.5 multiply_convert_fusion.1
  434.0 1.7 copy-done.1
  436.8 1.8 copy.370
  438.6 3.5 reshape.395
  442.1 2.0 fusion.85
  444.9 1.8 reshape.394
  451.3 2.0 fusion.131
  456.0 2.5 reduce.2
  459.8 1.8 reshape.402
  466.3 5.1 convolution_convert_fusion
  471.5 4.7 concatenate.55
  476.3 3.1 add_add_fusion.2
  480.9 12.1 %fusion.9 = bf16[2,2,512,2048]{3,2,1,0:T(8,128)(2,1)} fusion(bf16[2,2,512,2048]{3,2,1,0:T(8,128)(2,1)} %collective-permute-done, s32[]{:T(128)S(6)} %select_n.17, f32[2,2,1,512,2048]{4,3,1,0,2:T(8,128)} %bitcast.231, f32[2,2,1,512,2048]{4,3,1,0,2:T(8,128)} %stack.92), kind=kLoop, calls=%fused_computation.30 | loop fusion | flops 16777216 | bytes 50331652 | tf_op jit(solution)/shard_map/convert_element_type | solution.py:510
  493.1 106.7 %shard_map.345 = (bf16[4,64,2048]{2,1,0:T(8,128)(2,1)}, bf16[1,64,2304]{2,1,0:T(8,128)(2,1)}) custom-call(bf16[4,512,2048]{2,1,0:T(8,128)(2,1)} %bitcast.232, bf16[1,512,2304]{2,1,0:T(8,128)(2,1)} %pad_bitcast_fusion.refs_1_), custom_call_target="tpu_custom_call" | custom-call | flops 5373952 | bytes 32243712 | tf_op jit(solution)/shard_map/pallas_call | solution.py:143
  599.9 1.7 slice_bitcast_fusion
  602.4 31.0 %all-reduce.6.cloned.1.call-done = bf16[64,2079]{1,0:T(8,128)(2,1)} async-done(((bf16[64,2079]{1,0:T(8,128)(2,1)}), bf16[64,2079]{1,0:T(8,128)(2,1)}) %all-reduce.6.cloned.1.call-update) | async-done | bytes 266128 | tf_op jit(solution)/shard_map/psum | solution.py:516
  637.6 39.8 %all-reduce.8.cloned.1.call-done = bf16[1,2,2,64,2048]{4,3,2,1,0:T(8,128)(2,1)} async-done(((bf16[1,2,2,64,2048]{4,3,2,1,0:T(8,128)(2,1)}), bf16[1,2,2,64,2048]{4,3,2,1,0:T(8,128)(2,1)}) %all-reduce.8.cloned.1.call-update) | async-done | bytes 1048592 | tf_op jit(solution)/shard_map/psum | solution.py:515
  685.1 4.9 all-gather.2.cloned.1.call-done
  689.9 1.7 copy.382
  693.2 1.6 reshape.413
  694.9 1.6 reshape.411
  696.5 3.7 multiply_add_fusion.1
  701.5 3.5 fusion.46
  707.5 2.7 fusion.53
  710.3 2.5 pad_maximum_fusion.1
  712.7 2.3 pad_maximum_fusion
  (359 shorter events, 71.8 us)
Async XLA Ops:
  7.2 4.1 copy-start.38
  7.2 4.1 copy-start.93
  7.2 4.5 copy-start.46
  7.2 4.5 copy-start.78
  7.3 4.6 copy-start.84
  7.3 626.2 %all-reduce.6.cloned.1.call-start = ((), (), s32[]{:S(2)}) async-start(), calls=%async_computation | async-start | bytes 557056 | tf_op jit(solution)/shard_map/psum | solution.py:516
  11.3 104.8 %copy-start.15 = (bf16[788,512]{1,0:T(8,128)(2,1)S(1)}, bf16[788,512]{1,0:T(8,128)(2,1)}, u32[]{:S(2)}) copy-start(bf16[788,512]{1,0:T(8,128)(2,1)} %param.17) | copy-start | bytes 2420740
  116.1 28.9 %copy-start.81 = (f32[512]{0:T(512)}, f32[512]{0:T(512)S(1)}, u32[]{:S(2)}) copy-start(f32[512]{0:T(512)S(1)} %get-tuple-element.184) | copy-start | bytes 6148
  124.2 10.4 %copy-start.22 = (bf16[4,197,8,64]{1,3,2,0:T(8,128)(2,1)}, bf16[4,197,8,64]{1,3,2,0:T(8,128)(2,1)S(1)}, u32[]{:S(2)}) copy-start(bf16[4,197,8,64]{1,3,2,0:T(8,128)(2,1)S(1)} %copy.350) | copy-start | bytes 2420740
  128.3 7.5 %copy-start.21 = (bf16[4,197,8,64]{1,3,2,0:T(8,128)(2,1)}, bf16[4,197,8,64]{1,3,2,0:T(8,128)(2,1)S(1)}, u32[]{:S(2)}) copy-start(bf16[4,197,8,64]{1,3,2,0:T(8,128)(2,1)S(1)} %copy.351) | copy-start | bytes 2420740
  141.8 3.6 copy-start.41
  144.3 3.9 copy-start.83
  145.4 11.3 %copy-start.13 = (bf16[788,512]{1,0:T(8,128)(2,1)}, bf16[788,512]{1,0:T(8,128)(2,1)S(1)}, u32[]{:S(2)}) copy-start(bf16[788,512]{1,0:T(8,128)(2,1)S(1)} %add_convert_fusion.3) | copy-start | bytes 2420740
  146.9 9.9 %copy-start.49 = (f32[788,4]{0,1:T(4,128)}, f32[788,4]{0,1:T(4,128)S(1)}, u32[]{:S(2)}) copy-start(f32[788,4]{0,1:T(4,128)S(1)} %get-tuple-element.249) | copy-start | bytes 37828
  146.9 9.9 %copy-start.62 = (f32[788]{0:T(1024)}, f32[788]{0:T(1024)S(1)}, u32[]{:S(2)}) copy-start(f32[788]{0:T(1024)S(1)} %get-tuple-element.248) | copy-start | bytes 9460
  148.2 8.5 %copy-start.66 = (f32[788]{0:T(1024)}, f32[788]{0:T(1024)S(1)}, u32[]{:S(2)}) copy-start(f32[788]{0:T(1024)S(1)} %fusion.108) | copy-start | bytes 9460
  245.4 12.5 %copy-start.19 = (bf16[4,784,2048]{2,1,0:T(8,128)(2,1)}, bf16[4,784,2048]{2,1,0:T(8,128)(2,1)S(1)}, u32[]{:S(2)}) copy-start(bf16[4,784,2048]{2,1,0:T(8,128)(2,1)S(1)} %get-tuple-element.209) | copy-start | bytes 38535172
  272.0 4.7 copy-start.7
  284.9 16.4 %copy-start.35 = (bf16[2,4,392,512]{3,2,0,1:T(8,128)(2,1)}, bf16[2,4,392,512]{3,2,0,1:T(8,128)(2,1)S(1)}, u32[]{:S(2)}) copy-start(bf16[2,4,392,512]{3,2,0,1:T(8,128)(2,1)S(1)} %copy.360) | copy-start | bytes 9633796
  376.8 104.2 %collective-permute-start = (bf16[2,2,512,2048]{3,2,1,0:T(8,128)(2,1)}, bf16[2,2,512,2048]{3,2,1,0:T(8,128)(2,1)}, u32[]{:S(2)}, u32[]{:S(2)}) collective-permute-start(bf16[2,2,512,2048]{3,2,1,0:T(8,128)(2,1)} %fusion.14), channel_id=1, source_target_pairs={{0,8},{8,0},{1,9},{9,1},{2,10},{10,2},{3,11},{11,3},{4,12},{12,4},... | collective-permute-start | bytes 25165832 | tf_op jit(solution)/shard_map/ppermute | solution.py:508
  396.0 5.2 copy-start.4
  396.0 5.2 copy-start.61
  396.0 5.1 copy-start.65
  396.0 5.1 copy-start.82
  409.0 3.5 copy-start.52
  409.0 3.5 copy-start.54
  418.5 11.0 %slice-start = ((s8[6553600]{0:T(1024)(128)(4,1)}), s8[2359296]{0:T(1024)(128)(4,1)S(1)}, s32[]{:S(2)}) async-start(s8[6553600]{0:T(1024)(128)(4,1)} %bitcast.228), calls=%async_computation.3 | async-start | bytes 4718592
  421.8 7.7 %slice-start.1 = ((s8[6553600]{0:T(1024)(128)(4,1)}), s8[4194304]{0:T(1024)(128)(4,1)S(1)}, s32[]{:S(2)}) async-start(s8[6553600]{0:T(1024)(128)(4,1)} %bitcast.228), calls=%async_computation.4 | async-start | bytes 8388608
  429.5 6.2 copy-start.23
  436.8 5.3 copy-start.2
  444.1 3.9 copy-start.34
  451.3 4.7 copy-start.97
  451.3 4.7 copy-start.96
  451.3 4.7 copy-start.95
  453.3 5.5 copy-start.14
  455.9 8.9 %copy-start.42 = (bf16[788,512]{0,1:T(8,128)(2,1)S(1)}, bf16[788,512]{0,1:T(8,128)(2,1)}, u32[]{:S(2)}) copy-start(bf16[788,512]{0,1:T(8,128)(2,1)} %copy-done.41) | copy-start | bytes 2420740
  455.9 8.9 %copy-start.44 = (bf16[788,512]{1,0:T(8,128)(2,1)S(1)}, bf16[788,512]{1,0:T(8,128)(2,1)}, u32[]{:S(2)}) copy-start(bf16[788,512]{1,0:T(8,128)(2,1)} %copy-done.43) | copy-start | bytes 2420740
  458.4 7.9 %copy-start.89 = (f32[512]{0:T(512)S(1)}, f32[512]{0:T(512)}, u32[]{:S(2)}) copy-start(f32[512]{0:T(512)} %copy-done.87) | copy-start | bytes 6148
  471.5 4.7 copy-start.91
  471.5 4.8 copy-start.10
  471.5 4.8 copy-start.18
  471.5 4.8 copy-start.77
  471.5 4.8 copy-start.90
  493.1 108.6 %copy-start.98 = (f32[2,64,4]{1,2,0:T(4,128)S(1)}, f32[2,64,4]{1,2,0:T(4,128)}, u32[]{:S(2)}) copy-start(f32[2,64,4]{1,2,0:T(4,128)} %param.29) | copy-start | bytes 6148
  493.1 141.5 %copy-start.56 = (f32[1,11,64]{1,2,0:T(8,128)S(1)}, f32[1,11,64]{1,2,0:T(8,128)}, u32[]{:S(2)}) copy-start(f32[1,11,64]{1,2,0:T(8,128)} %copy.421) | copy-start | bytes 8452
  493.1 141.5 %copy-start.57 = (f32[1,11,64]{1,2,0:T(8,128)S(1)}, f32[1,11,64]{1,2,0:T(8,128)}, u32[]{:S(2)}) copy-start(f32[1,11,64]{1,2,0:T(8,128)} %copy.422) | copy-start | bytes 8452
  599.8 36.4 %copy-start.80 = (f32[2,4,256]{2,1,0:T(4,128)S(1)}, f32[2,4,256]{2,1,0:T(4,128)}, u32[]{:S(2)}) copy-start(f32[2,4,256]{2,1,0:T(4,128)} %param.31) | copy-start | bytes 24580
  599.8 37.7 %copy-start.86 = (f32[64,4]{0,1:T(4,128)S(1)}, f32[64,4]{0,1:T(4,128)}, u32[]{:S(2)}) copy-start(f32[64,4]{0,1:T(4,128)} %param.22) | copy-start | bytes 3076
  599.8 78.3 %copy-start.55 = (f32[64,4]{1,0:T(8,128)S(1)}, f32[64,4]{1,0:T(8,128)}, u32[]{:S(2)}) copy-start(f32[64,4]{1,0:T(8,128)} %copy.388) | copy-start | bytes 3076
  599.8 81.0 %copy-start.45 = (f32[2,64,512]{2,1,0:T(8,128)S(1)}, f32[2,64,512]{2,1,0:T(8,128)}, u32[]{:S(2)}) copy-start(f32[2,64,512]{2,1,0:T(8,128)} %param.28) | copy-start | bytes 786436
  599.9 81.0 %copy-start.47 = (f32[64,512]{1,0:T(8,128)S(1)}, f32[64,512]{1,0:T(8,128)}, u32[]{:S(2)}) copy-start(f32[64,512]{1,0:T(8,128)} %param.21) | copy-start | bytes 393220
  601.6 75.7 %all-reduce.8.cloned.1.call-start = ((), (), s32[]{:S(2)}) async-start(), calls=%async_computation.1 | async-start | bytes 2097152 | tf_op jit(solution)/shard_map/psum | solution.py:515
  601.9 80.5 %copy-start.94 = (f32[4,256]{1,0:T(4,128)S(1)}, f32[4,256]{1,0:T(4,128)}, u32[]{:S(2)}) copy-start(f32[4,256]{1,0:T(4,128)} %param.24) | copy-start | bytes 12292
  601.9 81.1 %copy-start.37 = (f32[2,64,1536]{2,1,0:T(8,128)S(1)}, f32[2,64,1536]{2,1,0:T(8,128)}, u32[]{:S(2)}) copy-start(f32[2,64,1536]{2,1,0:T(8,128)} %param.27) | copy-start | bytes 2359300
  602.4 87.6 %all-gather.2.cloned.1.call-start = ((), (), s32[]{:S(2)}) async-start(), calls=%async_computation.2 | async-start | bytes 3145728 | tf_op jit(solution)/shard_map/all_gather | solution.py:518
  633.5 46.7 %copy-start.36 = (bf16[64,2079]{1,0:T(8,128)(2,1)S(1)}, bf16[64,2079]{1,0:T(8,128)(2,1)}, u32[]{:S(2)}) copy-start(bf16[64,2079]{1,0:T(8,128)(2,1)} %all-reduce.6.cloned.1.call-done) | copy-start | bytes 798340
  634.6 48.5 %copy-start.39 = (f32[64,1536]{1,0:T(8,128)S(1)}, f32[64,1536]{1,0:T(8,128)}, u32[]{:S(2)}) copy-start(f32[64,1536]{1,0:T(8,128)} %param.20) | copy-start | bytes 1179652
  678.1 7.0 copy-start.92
  680.9 4.2 copy-start.48
  683.1 8.6 %copy-start.40 = (f32[64,1536]{1,0:T(8,128)}, f32[64,1536]{1,0:T(8,128)S(1)}, u32[]{:S(2)}) copy-start(f32[64,1536]{1,0:T(8,128)S(1)} %get-tuple-element.198) | copy-start | bytes 1179652
  696.5 3.8 copy-start.6
  696.5 4.4 copy-start.12
  696.5 5.0 copy-start.29
  701.5 3.8 copy-start.28
  (42 other events, 86.7 us)
Sparse Core Ops, SparseCore 0:
  601.8 31.6 all-reduce.5
  635.7 41.5 all-reduce.7
  679.0 10.9 all-gather.1

commit v4 on v3

--- a/solution.py
+++ b/solution.py
@@ -283,6 +283,193 @@
         compiler_params=pltpu.CompilerParams(collective_id=collective_id, has_side_effects=True),
         cost_estimate=pl.CostEstimate(flops=0, bytes_accessed=nbytes, transcendentals=0),
     )(up_b, down_b, dense_b)
+
+
+def grad_items(gu, gd, gdense, owner, gs, fs, width):
+    found = []
+    for k in range(2):
+        e = 2 * k + owner
+        found.append((lambda b, e=e: gu.at[e, pl.ds(pl.multiple_of(b * gs, gs), gs)], F // 2))
+        found.append((lambda b, e=e: gd.at[e, pl.ds(pl.multiple_of(b * fs, fs), fs)], D // 2))
+    found.append((lambda b: gdense.at[pl.ds(pl.multiple_of(b * gs, gs), gs), pl.ds(owner * width, width)], width // 2))
+    return found
+
+
+def ring_rs2_kernel(groups, x_pair, *refs):
+    gu, gd, gdense, out_up, out_down, out_dense = refs[:6]
+    n_items = 5
+    scr = refs[6:]
+    rbuf, sbuf, pbuf, own, fin, xr, cr = (scr[i * n_items : (i + 1) * n_items] for i in range(7))
+    ring_send, ring_recv, part_send, part_recv, load_sem, x_send, x_recv, c_send, c_recv = scr[7 * n_items :]
+    pos_of, dev_at = ring_order(groups)
+    rx = lax.axis_index("rx")
+    core = lax.axis_index("core")
+    g = lax.axis_index("group")
+    other = 1 - core
+    pos = pos_of(g)
+    nbr = (dev_at(pos + 1), dev_at(pos + groups - 1))
+    gs = gu.shape[1] // groups
+    fs = gd.shape[1] // groups
+    width = gdense.shape[1] // 2
+    mine = grad_items(gu, gd, gdense, core, gs, fs, width)
+    theirs = grad_items(gu, gd, gdense, other, gs, fs, width)
+
+    barrier = pltpu.get_barrier_semaphore()
+    for n in nbr:
+        pl.semaphore_signal(barrier, inc=1, device_id=(rx, core, n), device_id_type=MESH_ID)
+    pl.semaphore_signal(barrier, inc=1, device_id=(rx, other, g), device_id_type=MESH_ID)
+    count = 3
+    if x_pair:
+        pl.semaphore_signal(barrier, inc=1, device_id=(1 - rx, core, g), device_id_type=MESH_ID)
+        count = 4
+    pl.semaphore_wait(barrier, count)
+
+    def block_at(d, s):
+        if d == 0:
+            return dev_at(pos + 2 * groups - 1 - s)
+        return dev_at(pos + 1 + s)
+
+    def cols(j, d):
+        half = mine[j][1]
+        return pl.ds(d * half, half)
+
+    def load(d, s, slot, j):
+        return pltpu.make_async_copy(mine[j][0](block_at(d, s)).at[:, cols(j, d)], own[j].at[d, slot], load_sem.at[d, slot, j])
+
+    def part(d, s, j):
+        return pltpu.make_async_remote_copy(
+            src_ref=theirs[j][0](block_at(d, s)).at[:, cols(j, d)], dst_ref=pbuf[j].at[d, s],
+            send_sem=part_send.at[d, s, j], recv_sem=part_recv.at[d, s, j],
+            device_id=(rx, other, g), device_id_type=MESH_ID,
+        )
+
+    def ring(d, s, j):
+        return pltpu.make_async_remote_copy(
+            src_ref=sbuf[j].at[d, s], dst_ref=rbuf[j].at[d, s],
+            send_sem=ring_send.at[d, s, j], recv_sem=ring_recv.at[d, s, j],
+            device_id=(rx, core, nbr[d]), device_id_type=MESH_ID,
+        )
+
+    sends = []
+    for d in range(2):
+        for j in range(n_items):
+            load(d, 0, 0, j).start()
+            c = part(d, 0, j)
+            c.start()
+            sends.append(c)
+    for s in range(groups):
+        slot = s % 2
+        for d in range(2):
+            for j in range(n_items):
+                load(d, s, slot, j).wait()
+                if s + 1 < groups:
+                    load(d, s + 1, 1 - slot, j).start()
+                    c = part(d, s + 1, j)
+                    c.start()
+                    sends.append(c)
+                part(d, s, j).wait_recv()
+                val = own[j][d, slot].astype(F32) + pbuf[j][d, s].astype(F32)
+                if s > 0:
+                    ring(d, s - 1, j).wait_recv()
+                    val = val + rbuf[j][d, s - 1].astype(F32)
+                if s < groups - 1:
+                    sbuf[j][d, s] = val.astype(BF16)
+                    c = ring(d, s, j)
+                    c.start()
+                    sends.append(c)
+                else:
+                    fin[j][d] = val
+
+    for c in sends:
+        c.wait_send()
+    sends = []
+    if x_pair:
+        x_copies = []
+        for d in range(2):
+            for j in range(n_items):
+                sbuf[j][d, 0] = fin[j][d].astype(BF16)
+                c = pltpu.make_async_remote_copy(
+                    src_ref=sbuf[j].at[d, 0], dst_ref=xr[j].at[d], send_sem=x_send.at[d, j], recv_sem=x_recv.at[d, j],
+                    device_id=(1 - rx, core, g), device_id_type=MESH_ID,
+                )
+                c.start()
+                x_copies.append(c)
+        for c in x_copies:
+            c.wait_recv()
+        for d in range(2):
+            for j in range(n_items):
+                fin[j][d] = sbuf[j][d, 0].astype(F32) + xr[j][d].astype(F32)
+        sends += x_copies
+
+    c_copies = []
+    for d in range(2):
+        for j in range(n_items):
+            c = pltpu.make_async_remote_copy(
+                src_ref=fin[j].at[d], dst_ref=cr[j].at[d], send_sem=c_send.at[d, j], recv_sem=c_recv.at[d, j],
+                device_id=(rx, other, g), device_id_type=MESH_ID,
+            )
+            c.start()
+            c_copies.append(c)
+
+    def out_items(owner):
+        found = []
+        for k in range(2):
+            e = 2 * k + owner
+            found.append(lambda d, e=e: out_up.at[e, :, pl.ds(d * (F // 2), F // 2)])
+            found.append(lambda d, e=e: out_down.at[e, :, pl.ds(d * (D // 2), D // 2)])
+        found.append(lambda d: out_dense.at[:, pl.ds(owner * width + d * (width // 2), width // 2)])
+        return found
+
+    mine_out = out_items(core)
+    theirs_out = out_items(other)
+    for d in range(2):
+        for j in range(n_items):
+            mine_out[j](d)[...] = fin[j][d]
+    for c in c_copies:
+        c.wait_recv()
+    for d in range(2):
+        for j in range(n_items):
+            theirs_out[j](d)[...] = cr[j][d]
+    for c in sends + c_copies:
+        c.wait_send()
+
+
+def grad_reduce(gu, gd, gdense, groups, x_pair, collective_id):
+    gs = gu.shape[1] // groups
+    fs = gd.shape[1] // groups
+    width = gdense.shape[1] // 2
+    item_shapes = [(gs, F // 2), (fs, D // 2), (gs, F // 2), (fs, D // 2), (gs, width // 2)]
+    scratch = []
+    for lead, dtype in (((2, groups - 1), BF16), ((2, groups - 1), BF16), ((2, groups), BF16), ((2, 2), BF16), ((2,), F32), ((2,), BF16), ((2,), F32)):
+        scratch += [pltpu.VMEM(lead + shp, dtype) for shp in item_shapes]
+    scratch += [
+        pltpu.SemaphoreType.DMA((2, groups - 1, 5)),
+        pltpu.SemaphoreType.DMA((2, groups - 1, 5)),
+        pltpu.SemaphoreType.DMA((2, groups, 5)),
+        pltpu.SemaphoreType.DMA((2, groups, 5)),
+        pltpu.SemaphoreType.DMA((2, 2, 5)),
+        pltpu.SemaphoreType.DMA((2, 5)),
+        pltpu.SemaphoreType.DMA((2, 5)),
+        pltpu.SemaphoreType.DMA((2, 5)),
+        pltpu.SemaphoreType.DMA((2, 5)),
+    ]
+    outs = [
+        jax.ShapeDtypeStruct((E, gs, F), F32),
+        jax.ShapeDtypeStruct((E, fs, D), F32),
+        jax.ShapeDtypeStruct((gs, gdense.shape[1]), F32),
+    ]
+    nbytes = 2 * (gu.size + gd.size + gdense.size)
+    return pl.pallas_call(
+        functools.partial(ring_rs2_kernel, groups, x_pair),
+        out_shape=outs,
+        in_specs=[pl.BlockSpec(memory_space=pl.ANY)] * 3,
+        out_specs=[pl.BlockSpec(memory_space=pltpu.VMEM)] * 3,
+        scratch_shapes=scratch,
+        compiler_params=pltpu.CompilerParams(
+            collective_id=collective_id, has_side_effects=True, vmem_limit_bytes=62 * 1024 * 1024
+        ),
+        cost_estimate=pl.CostEstimate(flops=gu.size + gd.size + gdense.size, bytes_accessed=nbytes, transcendentals=0),
+    )(gu, gd, gdense)
 
 
 def layer_norm(value, gain, shift):
@@ -503,21 +690,14 @@
         ],
         0,
     )
-    both = jnp.stack([g_up, g_down.reshape(E, D, F)], 1).reshape(2, 2, 2, D, F)
-    sent = lax.dynamic_index_in_dim(both, 1 - core, 1, keepdims=False).astype(BF16)
-    got = lax.ppermute(sent, "core", [(0, 1), (1, 0)])
-    mine = lax.dynamic_index_in_dim(both, core, 1, keepdims=False)
-    expert_sum = (mine + got.astype(F32)).astype(BF16).reshape(4, D, F)
     dense_g = pack_dense(g_qkv, g_out, g_router, g_table, g_up_bias_all)
     width = dense_g.shape[1]
-    dense_g = jnp.pad(dense_g, ((0, 0), (0, DENSE_PAD - width))).astype(BF16)[None]
-    e_out, d_out_g = ring_reduce_scatter([expert_sum, dense_g], group_size, 0)
-    e_red = lax.psum(e_out, "rx").reshape(2, 2, gs, F)
-    d_red = lax.psum(d_out_g[0, :, :width], ("rx", "core")).astype(F32)
-    r_qkv, r_out, r_router, r_table, r_ub = unpack_dense(d_red)
-    e_all = lax.all_gather(e_red, "core", axis=0, tiled=False).transpose(1, 0, 2, 3, 4).reshape(E, 2, gs, F)
-    r_up = e_all[:, 0].astype(F32)
-    r_down = e_all[:, 1].astype(F32).reshape(E, gs * 4, D)
+    dense_g = jnp.pad(dense_g, ((0, 0), (0, DENSE_AG - width))).astype(BF16)
+    x_pair = lax.axis_size("rx") == 2
+    r_up, r_down, r_dense = grad_reduce(g_up.astype(BF16), g_down.astype(BF16), dense_g, group_size, x_pair, 0)
+    if not x_pair:
+        r_up, r_down, r_dense = lax.psum((r_up, r_down, r_dense), "rx")
+    r_qkv, r_out, r_router, r_table, r_ub = unpack_dense(r_dense[:, :width])
 
     reduced = (r_qkv, r_out, r_router, r_up, r_ub, r_down, r_table)
     rates = (

time: 729 us -> 623 us (0.85)
  waiting for transfers between devices: 76.2 us -> 0 us
  local copies, waits for them, and re-layouts: 114 us -> 82.4 us
  Pallas kernels: 208 us -> 236 us
  between operations: 15.6 us -> 2.22 us
  other arithmetic: 141 us -> 130 us
    psum x2 -> x0, waiting for transfers between devices: 70.8 us -> none  [the longest x1 39.8 us: shards(): e_red = lax.psum(e_out, 'rx').reshape(2, 2, gs, F)]
    pallas_call x1, Pallas kernels: 107 us -> 135 us  [grad_reduce(): pl.pallas_call(functools.partial(ring_rs2_kernel, groups, x_pair), out_sh...]
    convert_element_type x4 -> x0, other arithmetic: 22.5 us -> none  [the longest x1 12.1 us: shards(): expert_sum = (mine + got.astype(F32)).astype(BF16).reshape(4, D, F)]
    another operation x6 -> x5, local copies, waits for them, and re-layouts: 21.4 us -> 0.44 us  [the longest x1 20.4 us: shards(): both = jnp.stack([g_up, g_down.reshape(E, D, F)], 1).reshape(2, 2, 2, D, F)]
    another operation x13 -> x15, other arithmetic: 10.2 us -> 28.7 us  [adamw(): return (weight - rate * (update + 0.1 * weight), jnp.stack([first, root]))]
    unnamed x215 -> x163, local copies, waits for them, and re-layouts: 22.1 us -> 19.7 us
  transfers between devices with their start and end apart: 4 -> 0, of which waited for: 3 -> 0; matrix products, arithmetic and copies ran while one was open for 15% -> 0% of each run, Pallas kernels for 0% -> 0%
where the time goes in v4:
time: 623 us; the launch traced here: 616 us
  Pallas kernels  236 us (38%)
  matrix products  166 us (27%)
  other arithmetic  130 us (21%)
  local copies, waits for them, and re-layouts  82.4 us (13%)
    pallas_call x1, Pallas kernels, grad_reduce(): pl.pallas_call(functools.partial(ring_rs2_kernel, groups, x_pair), out_sh...  135 us
    pallas_call x1, Pallas kernels, ring_all_gather(): pl.pallas_call(functools.partial(ring_ag_kernel, groups), out_shape=shape...  101 us
    convert_element_type x1, other arithmetic, shards(): hidden = gelu_exact(hidden_pre).astype(BF16)  61.9 us
    dot_general x1, matrix products, shards(): jnp.einsum('ecd,efd->ecf', d_expert, w_down_all, preferred_element_type=F32)  28.8 us
    another operation x15, other arithmetic, adamw(): return (weight - rate * (update + 0.1 * weight), jnp.stack([first, root]))  28.7 us
    dot_general x1, matrix products, shards(): jnp.einsum('ecd,edf->ecf', table_in, w_up_all, preferred_element_type=F32)  23.9 us
    unnamed x163, local copies, waits for them, and re-layouts  19.7 us
    dot_general x1, matrix products, shards(): jnp.einsum('ecd,ecf->edf', table_in, d_pre, preferred_element_type=F32)  15.9 us

profile of v4, /device:TPU:1, one launch (start us, length us, event | category | flops | bytes accessed | tf_op | source)
XLA Modules:
  0.0 616.3 jit_solution(17897927062121439933)
XLA Ops:
  0.7 2.9 convert_element_type.138.refs_0_
  6.3 101.1 %shard_map.344 = (bf16[4,512,2048]{2,1,0:T(8,128)(2,1)}, bf16[4,2048,512]{2,1,0:T(8,128)(2,1)}, bf16[512,2560]{1,0:T(8,128)(2,1)}) custom-call(bf16[4,64,2048]{2,1,0:T(8,128)(2,1)} %convert_element_type.138.refs_0_, bf16[4,256,512]{2,1,0:T(8,128)(2,1)} %convert_element_type.139.refs_1_, bf16[64,2560]{1,0:T(8,128)(2,1)} %pad.14.refs_2_), custom_call_target="tpu_custom_call" | custom-call | bytes 19398656 | tf_op jit(solution)/shard_map/pallas_call | solution.py:271
  110.9 1.6 add_convert_fusion.1
  113.5 2.0 reshape.348
  115.5 2.2 copy.336
  117.7 2.0 reshape.349
  119.7 2.0 copy.337
  122.9 2.6 fusion.21
  126.5 1.8 copy.338
  128.3 4.7 fusion.65
  134.7 2.1 fusion.125
  138.3 1.4 fusion.126
  140.2 2.3 reduce-window.6
  143.3 5.0 fusion.26
  148.4 2.0 copy.341
  152.6 23.9 %fusion.20 = (u8[784,2048]{1,0:T(8,128)(4,1)S(1)}, u8[784,2048]{1,0:T(8,128)(4,1)S(1)}, f32[4,784,2048]{2,1,0:T(8,128)}) fusion(f32[4,2048]{1,0:T(4,128)S(1)} %reshape.345, bf16[4,784,512]{2,1,0:T(8,128)(2,1)} %bitcast.223, bf16[4,512,2048]{2,1,0:T(8,128)(2,1)} %get-tuple-element.30), kind=kOutput, calls=%fused_computation.45 | convolution fusion | flops 6663372800 | bytes 40534016 | tf_op jit(solution)/shard_map/ecd,edf->ecf/dot_general | solution.py:645
  176.4 61.9 %multiply_convert_fusion = (bf16[4,784,2048]{2,1,0:T(8,128)(2,1)}, f32[4,784,2048]{2,1,0:T(8,128)}) fusion(f32[4,784,2048]{2,1,0:T(8,128)} %get-tuple-element.250, f32[4,2048]{1,0:T(4,128)S(1)} %reshape.345, u8[784,2048]{1,0:T(8,128)(4,1)S(1)} %get-tuple-element.174, u8[784,2048]{1,0:T(8,128)(4,1)S(1)} %get-tuple-element.173), kind=kLoop, calls=%fused_computation.8 | loop fusion | flops 455999488 | bytes 67469312 | tf_op jit(solution)/shard_map/convert_element_type | solution.py:646
  238.6 12.5 %broadcast_add_fusion = f32[4,784,512]{2,1,0:T(8,128)S(1)} fusion(f32[4,512]{1,0:T(4,128)S(1)} %copy.344, bf16[4,784,2048]{2,1,0:T(8,128)(2,1)} %get-tuple-element.209, bf16[4,2048,512]{2,1,0:T(8,128)(2,1)} %get-tuple-element.31), kind=kOutput, calls=%fused_computation.64 | convolution fusion | flops 6578274304 | bytes 27664384 | tf_op jit(solution)/shard_map/ecf,efd->ecd/dot_general | solution.py:647
  253.2 6.1 fusion.8
  260.1 2.1 fusion.121
  262.2 1.6 reshape.322
  263.8 1.6 reshape.323
  265.4 2.2 multiply_reduce_fusion.5
  267.9 2.5 reshape.325
  270.3 1.7 multiply_convert_fusion.5
  272.0 4.7 fusion.27
  276.7 2.2 copy.346
  279.4 28.8 %fusion.127 = (bf16[4,2048]{1,0:T(4,128)(2,1)}, bf16[4,784,2048]{2,1,0:T(8,128)(2,1)}) fusion(f32[4,784,2048]{2,1,0:T(8,128)} %get-tuple-element.210, bf16[4,784,512]{2,1,0:T(8,128)(2,1)} %bitcast.225, bf16[4,2048,512]{2,1,0:T(8,128)(2,1)} %get-tuple-element.31, f32[4,784,2048]{2,1,0:T(8,128)} %get-tuple-element.250, f32[4,2048]{1,0:T(4,128)S(1)} %reshape.345), kind=kOutput, calls=%fused_computation.260 | convolution fusion | flops 6679420928 | bytes 75874304 | tf_op jit(solution)/shard_map/ecd,efd->ecf/dot_general | solution.py:663
  308.1 12.4 %fusion.128 = f32[4,784,512]{2,1,0:T(8,128)S(1)} fusion(bf16[4,784,2048]{2,1,0:T(8,128)(2,1)} %get-tuple-element.258, bf16[4,512,2048]{2,1,0:T(8,128)(2,1)} %get-tuple-element.30), kind=kOutput, calls=%fused_computation.261 | convolution fusion | flops 6576668672 | bytes 27656192 | tf_op jit(solution)/shard_map/ecf,edf->ecd/dot_general | solution.py:668
  323.6 3.6 fusion.13
  327.2 1.5 slice_add_fusion.3
  328.8 2.7 reshape.330
  331.6 2.6 multiply_reduce_fusion.2
  334.2 1.7 fusion.119
  338.3 1.7 convolution_convert_fusion.3
  341.9 4.2 fusion.62
  346.1 1.8 copy.359
  347.9 3.3 reshape.334
  351.1 7.8 %multiply_reduce_fusion = (f32[4,8,197]{2,1,0:T(8,128)S(1)}, f32[4,8,197,197]{2,3,1,0:T(8,128)}) fusion(f32[4,8,197,197]{2,3,1,0:T(8,128)} %copy-done, f32[4,8,197]{2,1,0:T(8,128)S(1)} %log_add_fusion, bf16[4,197,8,64]{1,3,2,0:T(8,128)(2,1)S(1)} %copy.349, bf16[4,197,8,64]{1,3,2,0:T(8,128)(2,1)} %copy.338), kind=kOutput, calls=%fused_computation.27 | convolution fusion | flops 163922912 | bytes 11599360 | tf_op jit(solution)/shard_map/bqhd,bkhd->bhqk/dot_general | solution.py:569
  358.9 4.5 multiply_convert_fusion.1
  363.4 1.7 copy-done.1
  366.3 1.8 copy.356
  368.1 3.3 reshape.333
  371.4 2.0 fusion.66
  374.2 1.8 reshape.332
  380.5 2.0 fusion.116
  383.6 1.5 fusion.46
  385.1 2.3 reduce.2
  387.8 5.3 convolution_convert_fusion.2
  395.7 4.4 concatenate.54
  400.2 3.5 pad.16.refs_2_
  403.6 14.6 %convolution_convert_fusion.refs_1_ = bf16[4,2048,512]{2,1,0:T(8,128)(2,1)} fusion(bf16[4,784,2048]{2,1,0:T(8,128)(2,1)} %get-tuple-element.209, bf16[4,784,512]{2,1,0:T(8,128)(2,1)S(1)} %bitcast.226), kind=kOutput, calls=%fused_computation.48 | convolution fusion | flops 6580862976 | bytes 24444928 | tf_op jit(solution)/shard_map/ecf,ecd->efd/dot_general | solution.py:662
  418.2 15.9 %convolution_convert_fusion.1.refs_0_ = bf16[4,512,2048]{2,1,0:T(8,128)(2,1)} fusion(bf16[4,784,512]{2,1,0:T(8,128)(2,1)S(1)} %bitcast.224, bf16[4,784,2048]{2,1,0:T(8,128)(2,1)} %get-tuple-element.258), kind=kOutput, calls=%fused_computation.49 | convolution fusion | flops 6580862976 | bytes 24444928 | tf_op jit(solution)/shard_map/ecd,ecf->edf/dot_general | solution.py:667
  434.1 135.0 %shard_map.345 = (f32[4,64,2048]{2,1,0:T(8,128)}, f32[4,256,512]{2,1,0:T(8,128)}, f32[64,2560]{1,0:T(8,128)}) custom-call(bf16[4,512,2048]{2,1,0:T(8,128)(2,1)} %convolution_convert_fusion.1.refs_0_, bf16[4,2048,512]{2,1,0:T(8,128)(2,1)} %convolution_convert_fusion.refs_1_, bf16[512,2560]{1,0:T(8,128)(2,1)} %pad.16.refs_2_), custom_call_target="tpu_custom_call" | custom-call | flops 9699328 | bytes 19398656 | tf_op jit(solution)/shard_map/pallas_call | solution.py:462
  571.1 6.2 %fusion.70 = (f32[1,4,256,512]{3,2,1,0:T(8,128)S(1)}, f32[1,4,256,512]{3,2,1,0:T(8,128)S(1)}, f32[4,256,512]{2,1,0:T(8,128)}) fusion(f32[4,256,512]{2,1,0:T(8,128)} %get-tuple-element.289, f32[2,4,256,512]{3,2,1,0:T(8,128)} %param.32, f32[4,256,512]{2,1,0:T(8,128)} %param.25), kind=kLoop, calls=%fused_computation.137 | loop fusion | flops 6815744 | bytes 14680064 | tf_op jit(solution)/shard_map/stack | solution.py:590
  577.3 2.5 pad_maximum_fusion.1
  581.5 6.5 %fusion.69 = (f32[1,4,64,2048]{3,2,1,0:T(8,128)S(1)}, f32[1,4,64,2048]{3,2,1,0:T(8,128)S(1)}, f32[4,64,2048]{2,1,0:T(8,128)}) fusion(f32[4,64,2048]{2,1,0:T(8,128)} %get-tuple-element.287, f32[2,4,64,2048]{3,2,1,0:T(8,128)} %param.30, f32[4,64,2048]{2,1,0:T(8,128)} %param.23), kind=kLoop, calls=%fused_computation.136 | loop fusion | flops 6815744 | bytes 14680064 | tf_op jit(solution)/shard_map/stack | solution.py:590
  588.1 2.5 pad_maximum_fusion
  590.8 1.4 fusion.94
  597.4 2.3 fusion.84
  604.3 1.4 copy.382
  605.9 1.3 multiply_subtract_fusion.5
  609.4 3.1 add_add_fusion.2
  612.5 1.3 copy.407
  (284 shorter events, 55.7 us)
Async XLA Ops:
  0.7 2.9 copy-start.19
  0.7 4.0 copy-start.29
  0.7 4.1 copy-start.68
  0.7 4.5 copy-start.36
  0.7 4.5 copy-start.56
  0.7 4.6 copy-start.63
  4.7 104.8 %copy-start.11 = (bf16[788,512]{1,0:T(8,128)(2,1)S(1)}, bf16[788,512]{1,0:T(8,128)(2,1)}, u32[]{:S(2)}) copy-start(bf16[788,512]{1,0:T(8,128)(2,1)} %param.17) | copy-start | bytes 2420740
  107.3 3.5 copy-start.42
  109.5 28.4 %copy-start.59 = (f32[512]{0:T(512)}, f32[512]{0:T(512)S(1)}, u32[]{:S(2)}) copy-start(f32[512]{0:T(512)S(1)} %get-tuple-element.186) | copy-start | bytes 6148
  109.8 2.7 copy-start.48
  110.9 1.6 copy-start.54
  117.7 5.2 copy-start.17
  122.9 2.8 copy-start
  122.9 5.4 copy-start.39
  122.9 2.7 copy-start.26
  134.7 3.6 copy-start.31
  136.8 2.9 copy-start.44
  136.8 3.1 copy-start.61
  137.2 2.5 copy-start.46
  138.3 10.1 %copy-start.9 = (bf16[788,512]{1,0:T(8,128)(2,1)}, bf16[788,512]{1,0:T(8,128)(2,1)S(1)}, u32[]{:S(2)}) copy-start(bf16[788,512]{1,0:T(8,128)(2,1)S(1)} %add_convert_fusion.3) | copy-start | bytes 2420740
  263.8 3.9 copy-start.62
  265.4 4.9 copy-start.5
  276.7 2.7 copy-start.15
  327.2 4.3 copy-start.4
  327.2 4.3 copy-start.45
  327.2 4.3 copy-start.47
  327.2 4.3 copy-start.60
  331.5 2.6 copy-start.53
  331.5 2.6 copy-start.6
  334.2 2.9 copy-start.13
  338.3 3.5 copy-start.40
  338.3 3.5 copy-start.41
  347.9 11.0 %slice-start = ((s8[6553600]{0:T(1024)(128)(4,1)}), s8[2359296]{0:T(1024)(128)(4,1)S(1)}, s32[]{:S(2)}) async-start(s8[6553600]{0:T(1024)(128)(4,1)} %bitcast.217), calls=%async_computation | async-start | bytes 4718592
  351.1 7.8 %slice-start.1 = ((s8[6553600]{0:T(1024)(128)(4,1)}), s8[4194304]{0:T(1024)(128)(4,1)S(1)}, s32[]{:S(2)}) async-start(s8[6553600]{0:T(1024)(128)(4,1)} %bitcast.217), calls=%async_computation.1 | async-start | bytes 8388608
  358.9 6.2 %copy-start.18 = (bf16[4,197,8,64]{1,3,2,0:T(8,128)(2,1)S(1)}, bf16[4,197,8,64]{1,3,2,0:T(8,128)(2,1)}, u32[]{:S(2)}) copy-start(bf16[4,197,8,64]{1,3,2,0:T(8,128)(2,1)} %copy-done.17) | copy-start | bytes 2420740
  363.4 1.7 copy-start.1
  366.3 5.1 copy-start.2
  373.3 3.9 copy-start.25
  374.2 3.2 copy-start.24
  377.5 1.5 copy-start.23
  377.9 1.7 copy-start.12
  377.9 2.6 copy-start.43
  377.9 2.6 copy-start.49
  377.9 2.6 copy-start.65
  380.5 2.0 copy-start.51
  380.5 3.1 copy-start.55
  382.5 5.3 copy-start.72
  387.8 5.3 copy-start.32
  387.8 5.3 copy-start.34
  387.8 6.0 copy-start.10
  400.2 3.5 copy-start.28
  403.6 14.6 %copy-start.27 = (bf16[4,2,392,512]{3,2,1,0:T(8,128)(2,1)S(1)}, bf16[4,2,392,512]{3,2,1,0:T(8,128)(2,1)}, u32[]{:S(2)}) copy-start(bf16[4,2,392,512]{3,2,1,0:T(8,128)(2,1)} %copy.341) | copy-start | bytes 9633796
  434.0 135.1 %copy-start.69 = (f32[2,11,64]{2,0,1:T(2,128)S(1)}, f32[2,11,64]{2,0,1:T(2,128)}, u32[]{:S(2)}) copy-start(f32[2,11,64]{2,0,1:T(2,128)} %param.33) | copy-start | bytes 16900
  434.1 135.3 %copy-start.57 = (f32[11,64]{1,0:T(8,128)S(1)}, f32[11,64]{1,0:T(8,128)}, u32[]{:S(2)}) copy-start(f32[11,64]{1,0:T(8,128)} %param.26) | copy-start | bytes 8452
  577.3 3.6 copy-start.58
  588.1 2.5 copy-start.70
  588.1 4.9 copy-start.35
  588.1 5.8 copy-start.37
  593.9 6.7 %copy-start.38 = (f32[64,512]{1,0:T(8,128)}, f32[64,512]{1,0:T(8,128)S(1)}, u32[]{:S(2)}) copy-start(f32[64,512]{1,0:T(8,128)S(1)} %get-tuple-element.285) | copy-start | bytes 393220
  594.6 14.7 %copy-start.8 = (f32[788,512]{1,0:T(8,128)S(1)}, f32[788,512]{1,0:T(8,128)}, u32[]{:S(2)}) copy-start(f32[788,512]{1,0:T(8,128)} %copy-done.7) | copy-start | bytes 4841476
  594.7 14.7 %copy-start.14 = (bf16[788,512]{1,0:T(8,128)(2,1)S(1)}, bf16[788,512]{1,0:T(8,128)(2,1)}, u32[]{:S(2)}) copy-start(bf16[788,512]{1,0:T(8,128)(2,1)} %param.18) | copy-start | bytes 2420740
  605.9 6.6 %copy-start.67 = (f32[4,256]{1,0:T(4,128)}, f32[4,256]{1,0:T(4,128)S(1)}, u32[]{:S(2)}) copy-start(f32[4,256]{1,0:T(4,128)S(1)} %reshape.342) | copy-start | bytes 12292
  609.4 3.1 copy-start.21
  612.5 2.3 copy-start.20
  (11 other events, 11.4 us)

commit v5 on v4

--- a/solution.py
+++ b/solution.py
@@ -472,6 +472,133 @@
     )(gu, gd, gdense)
 
 
+TILE = 128
+CAPP = 512
+SQRT_HALF = float(np.sqrt(0.5))
+INV_SQRT_2PI = float(1.0 / np.sqrt(2.0 * np.pi))
+
+
+def ffn_fwd_kernel(micro, counts, x_ref, w1_ref, b1_ref, w2_ref, b2_ref, hp_ref, h_ref, y_ref):
+    e, m, t = pl.program_id(0), pl.program_id(1), pl.program_id(2)
+    active = t * TILE < counts[e * micro + m]
+
+    @pl.when(active)
+    def _():
+        hp = jnp.dot(x_ref[0], w1_ref[0], preferred_element_type=F32) + b1_ref[0]
+        h = (0.5 * hp * (1.0 + lax.erf(hp * SQRT_HALF))).astype(BF16)
+        hp_ref[0] = hp
+        h_ref[0] = h
+        y_ref[0] = jnp.dot(h, w2_ref[0], preferred_element_type=F32) + b2_ref[0]
+
+    @pl.when(jnp.logical_not(active))
+    def _():
+        y_ref[0] = jnp.zeros(y_ref.shape[1:], F32)
+
+
+def ffn_forward(counts, table_in, w1, b1, w2, b2, micro):
+    tiles = CAPP // TILE
+    rows = table_in.shape[1]
+    row_map = lambda e, m, t, c: (e, m * tiles + t, 0)
+    w_map = lambda e, m, t, c: (e, 0, 0)
+    grid_spec = pltpu.PrefetchScalarGridSpec(
+        num_scalar_prefetch=1,
+        grid=(E, micro, tiles),
+        in_specs=[
+            pl.BlockSpec((1, TILE, D), row_map),
+            pl.BlockSpec((1, D, F), w_map),
+            pl.BlockSpec((1, 1, F), w_map),
+            pl.BlockSpec((1, F, D), w_map),
+            pl.BlockSpec((1, 1, D), w_map),
+        ],
+        out_specs=[
+            pl.BlockSpec((1, TILE, F), row_map),
+            pl.BlockSpec((1, TILE, F), row_map),
+            pl.BlockSpec((1, TILE, D), row_map),
+        ],
+    )
+    work = E * rows
+    return pl.pallas_call(
+        functools.partial(ffn_fwd_kernel, micro),
+        grid_spec=grid_spec,
+        out_shape=[
+            jax.ShapeDtypeStruct((E, rows, F), F32),
+            jax.ShapeDtypeStruct((E, rows, F), BF16),
+            jax.ShapeDtypeStruct((E, rows, D), F32),
+        ],
+        compiler_params=pltpu.CompilerParams(vmem_limit_bytes=48 * 1024 * 1024),
+        cost_estimate=pl.CostEstimate(
+            flops=4 * work * D * F // 2, bytes_accessed=work * (2 * D + 6 * F + 4 * D) // 2, transcendentals=work * F // 2
+        ),
+    )(counts, table_in, w1, b1, w2, b2)
+
+
+def ffn_bwd_kernel(micro, counts, dy_ref, x_ref, hp_ref, h_ref, w1_ref, w2_ref, dt_ref, gu_ref, gd_ref, gb_ref):
+    e, m, t = pl.program_id(0), pl.program_id(1), pl.program_id(2)
+    active = t * TILE < counts[e * micro + m]
+
+    @pl.when((m == 0) & (t == 0))
+    def _():
+        gu_ref[...] = jnp.zeros(gu_ref.shape, F32)
+        gd_ref[...] = jnp.zeros(gd_ref.shape, F32)
+        gb_ref[...] = jnp.zeros(gb_ref.shape, F32)
+
+    @pl.when(active)
+    def _():
+        dy = dy_ref[0]
+        hp = hp_ref[0]
+        d_hidden = lax.dot_general(dy, w2_ref[0], (((1,), (1,)), ((), ())), preferred_element_type=F32)
+        slope = 0.5 * (1.0 + lax.erf(hp * SQRT_HALF)) + hp * jnp.exp(-0.5 * hp * hp) * INV_SQRT_2PI
+        d_pre = (d_hidden * slope).astype(BF16)
+        dt_ref[0] = lax.dot_general(d_pre, w1_ref[0], (((1,), (1,)), ((), ())), preferred_element_type=F32)
+        gu_ref[0] += lax.dot_general(x_ref[0], d_pre, (((0,), (0,)), ((), ())), preferred_element_type=F32)
+        gd_ref[0] += lax.dot_general(h_ref[0], dy, (((0,), (0,)), ((), ())), preferred_element_type=F32)
+        gb_ref[0] += jnp.sum(d_pre.astype(F32), 0, keepdims=True)
+
+    @pl.when(jnp.logical_not(active))
+    def _():
+        dt_ref[0] = jnp.zeros(dt_ref.shape[1:], F32)
+
+
+def ffn_backward(counts, d_expert, table_in, hp, h, w1, w2, micro):
+    tiles = CAPP // TILE
+    rows = table_in.shape[1]
+    row_map = lambda e, m, t, c: (e, m * tiles + t, 0)
+    w_map = lambda e, m, t, c: (e, 0, 0)
+    grid_spec = pltpu.PrefetchScalarGridSpec(
+        num_scalar_prefetch=1,
+        grid=(E, micro, tiles),
+        in_specs=[
+            pl.BlockSpec((1, TILE, D), row_map),
+            pl.BlockSpec((1, TILE, D), row_map),
+            pl.BlockSpec((1, TILE, F), row_map),
+            pl.BlockSpec((1, TILE, F), row_map),
+            pl.BlockSpec((1, D, F), w_map),
+            pl.BlockSpec((1, F, D), w_map),
+        ],
+        out_specs=[
+            pl.BlockSpec((1, TILE, D), row_map),
+            pl.BlockSpec((1, D, F), w_map),
+            pl.BlockSpec((1, F, D), w_map),
+            pl.BlockSpec((1, 1, F), w_map),
+        ],
+    )
+    work = E * rows
+    return pl.pallas_call(
+        functools.partial(ffn_bwd_kernel, micro),
+        grid_spec=grid_spec,
+        out_shape=[
+            jax.ShapeDtypeStruct((E, rows, D), F32),
+            jax.ShapeDtypeStruct((E, D, F), F32),
+            jax.ShapeDtypeStruct((E, F, D), F32),
+            jax.ShapeDtypeStruct((E, 1, F), F32),
+        ],
+        compiler_params=pltpu.CompilerParams(vmem_limit_bytes=56 * 1024 * 1024),
+        cost_estimate=pl.CostEstimate(
+            flops=8 * work * D * F // 2, bytes_accessed=work * (8 * D + 6 * F) // 2 + 32 * E * D * F, transcendentals=2 * work * F // 2
+        ),
+    )(counts, d_expert, table_in, hp, h, w1, w2)
+
+
 def layer_norm(value, gain, shift):
     center = value - jnp.mean(value, -1, keepdims=True)
     spread = jnp.mean(center * center, -1, keepdims=True)
@@ -495,7 +622,7 @@
     hits = (chosen[:, :, None] == jnp.arange(E, dtype=jnp.int32)).astype(jnp.int32)
     before = jnp.cumsum(hits, 1) - hits
     slot = jnp.sum(before * hits, 2)
-    return chosen * CAP + slot
+    return chosen * CAPP + slot, jnp.sum(hits, 1)
 
 
 def hi_lo(v):
@@ -635,17 +762,18 @@
     gate = jnp.sum(jnp.where(picked, probs[:, None, :], 0.0), -1)
 
     route = expert_index.reshape(micro, MB_TOK, 2)
-    places = assign_places(route)
-    onehot = (places[:, :, None] == jnp.arange(E * CAP, dtype=jnp.int32)).astype(BF16)
+    places, counts = assign_places(route)
+    counts = counts.T.reshape(E * micro)
+    onehot = (places[:, :, None] == jnp.arange(E * CAPP, dtype=jnp.int32)).astype(BF16)
     second_m = second.reshape(micro, MB_TOK, D)
     pair = jnp.concatenate([second_m, second_m], 1)
     table_in = jnp.einsum("mnr,mnd->mrd", onehot, pair, preferred_element_type=F32).astype(BF16)
-    table_in = table_in.reshape(micro, E, CAP, D).transpose(1, 0, 2, 3).reshape(E, micro * CAP, D)
-
-    hidden_pre = jnp.einsum("ecd,edf->ecf", table_in, w_up_all, preferred_element_type=F32) + b_up[:, None, :]
-    hidden = gelu_exact(hidden_pre).astype(BF16)
-    y_all = jnp.einsum("ecf,efd->ecd", hidden, w_down_all, preferred_element_type=F32) + table[7 : 7 + E][:, None, :]
-    y_m = y_all.reshape(E, micro, CAP, D).transpose(1, 0, 2, 3).reshape(micro, E * CAP, D)
+    table_in = table_in.reshape(micro, E, CAPP, D).transpose(1, 0, 2, 3).reshape(E, micro * CAPP, D)
+
+    hidden_pre, hidden, y_all = ffn_forward(
+        counts, table_in, w_up_all, b_up[:, None, :], w_down_all, table[7 : 7 + E][:, None, :], micro
+    )
+    y_m = y_all.reshape(E, micro, CAPP, D).transpose(1, 0, 2, 3).reshape(micro, E * CAPP, D)
     picked_rows = pick_rows(onehot, y_m)
     out_zero = picked_rows[:, :MB_TOK].reshape(rows, D)
     out_one = picked_rows[:, MB_TOK:].reshape(rows, D)
@@ -656,18 +784,13 @@
     gate_m = gate.reshape(micro, MB_TOK, 2)
     weighted = jnp.concatenate([gate_m[:, :, 0:1] * d_out_m, gate_m[:, :, 1:2] * d_out_m], 1).astype(BF16)
     d_expert = jnp.einsum("mnr,mnd->mrd", onehot, weighted, preferred_element_type=F32).astype(BF16)
-    d_expert = d_expert.reshape(micro, E, CAP, D).transpose(1, 0, 2, 3).reshape(E, micro * CAP, D)
+    d_expert = d_expert.reshape(micro, E, CAPP, D).transpose(1, 0, 2, 3).reshape(E, micro * CAPP, D)
     g_bias_down = jnp.sum(d_expert.astype(F32), 1)
 
-    g_down = jnp.einsum("ecf,ecd->efd", hidden, d_expert, preferred_element_type=F32)
-    d_hidden = jnp.einsum("ecd,efd->ecf", d_expert, w_down_all, preferred_element_type=F32)
-    gelu_pull = jax.vjp(gelu_exact, hidden_pre)[1]
-    d_pre = gelu_pull(d_hidden)[0].astype(BF16)
-    g_up_bias_all = jnp.sum(d_pre.astype(F32), 1)
-    g_up = jnp.einsum("ecd,ecf->edf", table_in, d_pre, preferred_element_type=F32)
-    d_table = jnp.einsum("ecf,edf->ecd", d_pre, w_up_all, preferred_element_type=F32)
-
-    d_table_m = d_table.reshape(E, micro, CAP, D).transpose(1, 0, 2, 3).reshape(micro, E * CAP, D)
+    d_table, g_up, g_down, g_b1 = ffn_backward(counts, d_expert, table_in, hidden_pre, hidden, w_up_all, w_down_all, micro)
+    g_up_bias_all = g_b1[:, 0, :]
+
+    d_table_m = d_table.reshape(E, micro, CAPP, D).transpose(1, 0, 2, 3).reshape(micro, E * CAPP, D)
     onehot_sum = onehot[:, :MB_TOK] + onehot[:, MB_TOK:]
     d_picked = pick_rows(onehot_sum, d_table_m).reshape(rows, D)
 

time: 623 us -> 628 us (level)
  Pallas kernels: 236 us -> 358 us
  matrix products: 166 us -> 69 us
  other arithmetic: 130 us -> 92.1 us
  local copies, waits for them, and re-layouts: 82.4 us -> 95 us
    pallas_call x0 -> x2, Pallas kernels: none -> 120 us  [the longest x1 80.6 us: ffn_backward(): pl.pallas_call(functools.partial(ffn_bwd_kernel, micro), grid_spec=grid_s...]
    dot_general x6 -> x0, matrix products: 108 us -> none  [the longest x1 28.8 us: shards(): jnp.einsum('ecd,efd->ecf', d_expert, w_down_all, preferred_element_type=F32)]
    convert_element_type x2 -> x3, other arithmetic: 62.8 us -> 19.1 us  [the longest x1 9.08 us: shards(): g_up.astype(BF16)]
    convert_element_type x2, other arithmetic: 2.28 us -> 12 us  [hi_lo(): lo = (v - hi.astype(F32)).astype(BF16)]
    unnamed x163 -> x145, local copies, waits for them, and re-layouts: 19.7 us -> 23.1 us
where the time goes in v5:
time: 628 us; the launch traced here: 616 us
  Pallas kernels  358 us (57%)
  local copies, waits for them, and re-layouts  95 us (15%)
  other arithmetic  92.1 us (15%)
  matrix products  69 us (11%)
    pallas_call x1, Pallas kernels, grad_reduce(): pl.pallas_call(functools.partial(ring_rs2_kernel, groups, x_pair), out_sh...  137 us
    pallas_call x1, Pallas kernels, ring_all_gather(): pl.pallas_call(functools.partial(ring_ag_kernel, groups), out_shape=shape...  101 us
    pallas_call x1, Pallas kernels, ffn_backward(): pl.pallas_call(functools.partial(ffn_bwd_kernel, micro), grid_spec=grid_s...  80.6 us
    pallas_call x1, Pallas kernels, ffn_forward(): pl.pallas_call(functools.partial(ffn_fwd_kernel, micro), grid_spec=grid_s...  39.5 us
    another operation x15, other arithmetic, adamw(): return (weight - rate * (update + 0.1 * weight), jnp.stack([first, root]))  26 us
    unnamed x145, local copies, waits for them, and re-layouts  23.1 us
    dot_general x2, matrix products, pick_rows(): jnp.einsum('mnr,mrd->mnd', onehot, hi_lo(table), preferred_element_type=F32)  16 us

profile of v5, /device:TPU:1, one launch (start us, length us, event | category | flops | bytes accessed | tf_op | source)
XLA Modules:
  0.0 616.5 jit_solution(1559747955028110843)
XLA Ops:
  0.7 2.9 convert_element_type.132.refs_0_
  6.2 101.1 %shard_map.344 = (bf16[4,512,2048]{2,1,0:T(8,128)(2,1)}, bf16[4,2048,512]{2,1,0:T(8,128)(2,1)}, bf16[512,2560]{1,0:T(8,128)(2,1)}) custom-call(bf16[4,64,2048]{2,1,0:T(8,128)(2,1)} %convert_element_type.132.refs_0_, bf16[4,256,512]{2,1,0:T(8,128)(2,1)} %convert_element_type.133.refs_1_, bf16[64,2560]{1,0:T(8,128)(2,1)} %pad.14.refs_2_), custom_call_target="tpu_custom_call" | custom-call | bytes 19398656 | tf_op jit(solution)/shard_map/pallas_call | solution.py:271
  107.3 4.5 copy.278
  115.0 3.0 add_convert_fusion
  118.0 1.3 fusion.113
  121.2 3.5 reshape.353
  124.7 2.0 copy.283
  128.0 1.3 fusion.16
  129.3 1.5 copy-done.2
  131.6 1.2 copy.284
  132.8 4.8 fusion.57
  139.3 2.1 fusion.117
  142.1 1.4 fusion.118
  144.0 2.3 reduce-window.6
  147.3 5.9 fusion.18
  153.2 2.5 copy.288
  158.9 2.2 copy-done
  161.1 39.5 %shard_map.345 = (f32[4,1024,2048]{2,1,0:T(8,128)}, bf16[4,1024,2048]{2,1,0:T(8,128)(2,1)}, f32[4,1024,512]{2,1,0:T(8,128)}) custom-call(s32[8]{0:T(128)S(1)} %reshape.320.counts, bf16[4,1024,512]{2,1,0:T(8,128)(2,1)S(1)} %bitcast.213, bf16[4,512,2048]{2,1,0:T(8,128)(2,1)} %get-tuple-element.37.w1_ref, f32[4,1,2048]{2,1,0:T(1,128)S(1)} %reshape.350.b1_ref, ...), custom_call_target="tpu_custom_call" | custom-call | flops 8589934592 | bytes 31457280 | tf_op jit(solution)/shard_map/pallas_call | solution.py:520
  200.6 5.1 copy.292
  205.7 6.2 %fusion.12 = (bf16[2,2048,512]{2,1,0:T(8,128)(2,1)}, bf16[2,2048,512]{2,1,0:T(8,128)(2,1)}) fusion(f32[2,4,512,512]{3,2,1,0:T(8,128)S(1)} %copy.292), kind=kLoop, calls=%fused_computation.17 | loop fusion | flops 8388608 | bytes 16777216 | tf_op jit(solution)/shard_map/convert_element_type | solution.py:630
  211.9 9.4 %fusion.2 = f32[2,788,1024]{2,1,0:T(8,128)S(1)} fusion(bf16[2,2048,512]{2,1,0:T(8,128)(2,1)} %get-tuple-element.191, bf16[2,2048,512]{2,1,0:T(8,128)(2,1)} %get-tuple-element.192, s32[2,788]{1,0:T(2,128)S(1)} %multiply_add_fusion.6), kind=kOutput, calls=%fused_computation.3 | convolution fusion | flops 6630227968 | bytes 14850208 | tf_op jit(solution)/shard_map/mnr,mrd->mnd/dot_general | solution.py:635
  222.1 2.1 fusion.112
  224.2 1.6 reshape.326
  225.8 2.7 reshape.327
  228.5 2.1 multiply_reduce_fusion.5
  230.9 2.5 reshape.329
  233.4 1.7 multiply_convert_fusion.4
  235.1 5.9 fusion.19
  241.1 2.8 copy.293
  244.3 80.6 %shard_map.346 = (f32[4,1024,512]{2,1,0:T(8,128)}, f32[4,512,2048]{2,1,0:T(8,128)}, f32[4,2048,512]{2,1,0:T(8,128)}, f32[4,1,2048]{2,1,0:T(1,128)}) custom-call(s32[8]{0:T(128)} %copy-done.1, bf16[4,1024,512]{2,1,0:T(8,128)(2,1)} %bitcast.216, bf16[4,1024,512]{2,1,0:T(8,128)(2,1)} %bitcast.212, f32[4,1024,2048]{2,1,0:T(8,128)} %get-tuple-element.40.hp_ref, ...), custom_call_target="tpu_custom_call" | custom-call | flops 17179869184 | bytes 167772160 | tf_op jit(solution)/shard_map/pallas_call | solution.py:586
  324.9 5.1 copy.294
  330.0 5.8 fusion.11
  338.0 6.6 %fusion.7 = f32[2,394,1024]{2,1,0:T(8,128)} fusion(bf16[2,2048,512]{2,1,0:T(8,128)(2,1)S(1)} %copy-done.24, bf16[2,2048,512]{2,1,0:T(8,128)(2,1)} %get-tuple-element.190, bf16[2,788,2048]{2,1,0:T(8,128)(2,1)S(1)} %fusion.1), kind=kOutput, calls=%fused_computation.8 | convolution fusion | flops 3323502592 | bytes 18169856 | tf_op jit(solution)/shard_map/mnr,mrd->mnd/dot_general | solution.py:635
  344.6 3.4 slice_add_fusion.3
  348.0 2.7 reshape.334
  350.8 3.1 multiply_reduce_fusion.2
  354.0 1.7 fusion.111
  355.7 1.2 copy-done.7
  358.1 1.7 convolution_convert_fusion.1
  361.6 4.2 fusion.54
  365.8 1.8 copy.306
  367.6 3.6 reshape.338
  371.2 7.8 %multiply_reduce_fusion = (f32[4,8,197]{2,1,0:T(8,128)S(1)}, f32[4,8,197,197]{2,3,1,0:T(8,128)}) fusion(f32[4,8,197,197]{2,3,1,0:T(8,128)} %copy-done.2, f32[4,8,197]{2,1,0:T(8,128)S(1)} %log_add_fusion, bf16[4,197,8,64]{1,3,2,0:T(8,128)(2,1)S(1)} %copy.296, bf16[4,197,8,64]{1,3,2,0:T(8,128)(2,1)} %copy-done.25), kind=kOutput, calls=%fused_computation.19 | convolution fusion | flops 163922912 | bytes 11599360 | tf_op jit(solution)/shard_map/bqhd,bkhd->bhqk/dot_general | solution.py:696
  379.0 4.5 multiply_convert_fusion
  383.5 1.2 fusion.59
  386.9 2.7 fusion.58
  395.5 2.0 fusion.108
  398.7 1.5 fusion.38
  401.3 5.3 convolution_convert_fusion
  409.7 4.4 concatenate.54
  414.1 3.3 pad.16.refs_2_
  417.4 9.1 %convert_element_type.164.refs_0_ = bf16[4,512,2048]{2,1,0:T(8,128)(2,1)} convert(f32[4,512,2048]{2,1,0:T(8,128)} %get-tuple-element.43) | non-fusion elementwise | flops 4194304 | bytes 25165824 | tf_op jit(solution)/shard_map/convert_element_type | solution.py:820
  426.5 9.0 %convert_element_type.165.refs_1_ = bf16[4,2048,512]{2,1,0:T(8,128)(2,1)} convert(f32[4,2048,512]{2,1,0:T(8,128)} %get-tuple-element.44) | non-fusion elementwise | flops 4194304 | bytes 25165824 | tf_op jit(solution)/shard_map/convert_element_type | solution.py:820
  435.5 137.3 %shard_map.347 = (f32[4,64,2048]{2,1,0:T(8,128)}, f32[4,256,512]{2,1,0:T(8,128)}, f32[64,2560]{1,0:T(8,128)}) custom-call(bf16[4,512,2048]{2,1,0:T(8,128)(2,1)} %convert_element_type.164.refs_0_, bf16[4,2048,512]{2,1,0:T(8,128)(2,1)} %convert_element_type.165.refs_1_, bf16[512,2560]{1,0:T(8,128)(2,1)} %pad.16.refs_2_), custom_call_target="tpu_custom_call" | custom-call | flops 9699328 | bytes 19398656 | tf_op jit(solution)/shard_map/pallas_call | solution.py:462
  574.7 6.2 %fusion.62 = (f32[1,4,256,512]{3,2,1,0:T(8,128)S(1)}, f32[1,4,256,512]{3,2,1,0:T(8,128)S(1)}, f32[4,256,512]{2,1,0:T(8,128)}) fusion(f32[4,256,512]{2,1,0:T(8,128)} %get-tuple-element.275, f32[2,4,256,512]{3,2,1,0:T(8,128)} %param.32, f32[4,256,512]{2,1,0:T(8,128)} %param.25), kind=kLoop, calls=%fused_computation.112 | loop fusion | flops 6815744 | bytes 14680064 | tf_op jit(solution)/shard_map/stack | solution.py:717
  580.9 2.5 pad_maximum_fusion.1
  584.4 6.5 %fusion.61 = (f32[1,4,64,2048]{3,2,1,0:T(8,128)S(1)}, f32[1,4,64,2048]{3,2,1,0:T(8,128)S(1)}, f32[4,64,2048]{2,1,0:T(8,128)}) fusion(f32[4,64,2048]{2,1,0:T(8,128)} %get-tuple-element.273, f32[2,4,64,2048]{3,2,1,0:T(8,128)} %param.30, f32[4,64,2048]{2,1,0:T(8,128)} %param.23), kind=kLoop, calls=%fused_computation.111 | loop fusion | flops 6815744 | bytes 14680064 | tf_op jit(solution)/shard_map/stack | solution.py:717
  590.9 2.5 pad_maximum_fusion
  597.4 2.4 fusion.76
  604.5 1.4 copy.328
  606.0 1.3 multiply_subtract_fusion.5
  609.6 3.1 add_add_fusion.2
  612.6 1.3 copy.353
  615.0 1.3 copy.354
  (267 shorter events, 51.5 us)
Async XLA Ops:
  0.7 2.9 copy-start.19
  3.5 1.1 copy-start.30
  3.5 1.2 copy-start.57
  3.5 1.6 copy-start.38
  3.5 1.6 copy-start.48
  3.6 1.7 copy-start.55
  107.3 6.4 %copy-start.11 = (bf16[788,512]{1,0:T(8,128)(2,1)S(1)}, bf16[788,512]{1,0:T(8,128)(2,1)}, u32[]{:S(2)}) copy-start(bf16[788,512]{1,0:T(8,128)(2,1)} %param.17) | copy-start | bytes 2420740
  113.7 1.3 copy-start.53
  113.7 1.3 copy-start.62
  114.0 4.0 copy-start.42
  115.0 3.0 copy-start.46
  121.2 5.6 copy-start.17
  126.8 1.1 copy-start.15
  127.9 2.8 copy-start.2
  127.9 2.8 copy-start.28
  132.8 4.8 copy-start.25
  139.3 2.1 copy-start.32
  141.8 2.0 copy-start.52
  142.1 11.1 %copy-start.9 = (bf16[788,512]{1,0:T(8,128)(2,1)}, bf16[788,512]{1,0:T(8,128)(2,1)S(1)}, u32[]{:S(2)}) copy-start(bf16[788,512]{1,0:T(8,128)(2,1)S(1)} %add_convert_fusion.2) | copy-start | bytes 2420740
  155.9 44.7 %copy-start.1 = (s32[8]{0:T(128)}, s32[8]{0:T(128)S(1)}, u32[]{:S(2)}) copy-start(s32[8]{0:T(128)S(1)} %reshape.320.counts) | copy-start | bytes 100
  158.9 2.2 copy-start
  241.0 3.2 copy-start.4
  335.8 2.2 copy-start.24
  350.8 3.2 copy-start.6
  354.0 2.9 copy-start.13
  355.7 1.2 copy-start.7
  357.2 0.9 copy-start.34
  367.6 11.4 %slice-start = ((s8[6553600]{0:T(1024)(128)(4,1)}), s8[2359296]{0:T(1024)(128)(4,1)S(1)}, s32[]{:S(2)}) async-start(s8[6553600]{0:T(1024)(128)(4,1)} %bitcast.214), calls=%async_computation | async-start | bytes 4718592
  371.2 7.8 %slice-start.1 = ((s8[6553600]{0:T(1024)(128)(4,1)}), s8[4194304]{0:T(1024)(128)(4,1)S(1)}, s32[]{:S(2)}) async-start(s8[6553600]{0:T(1024)(128)(4,1)} %bitcast.214), calls=%async_computation.1 | async-start | bytes 8388608
  379.0 4.5 copy-start.18
  383.5 1.7 copy-start.3
  385.2 1.7 copy-start.16
  391.2 1.2 copy-start.26
  392.5 1.5 copy-start.23
  392.9 1.7 copy-start.12
  392.9 2.6 copy-start.27
  392.9 2.6 copy-start.43
  392.9 2.6 copy-start.54
  395.5 2.0 copy-start.45
  395.5 3.1 copy-start.47
  395.5 4.7 copy-start.5
  397.5 1.2 copy-start.22
  397.5 2.7 copy-start.60
  397.5 2.7 copy-start.59
  400.2 1.1 copy-start.63
  401.3 5.3 copy-start.33
  401.3 5.3 copy-start.35
  406.5 1.1 copy-start.10
  406.5 1.5 copy-start.50
  435.5 137.3 %copy-start.58 = (f32[2,11,64]{2,0,1:T(2,128)S(1)}, f32[2,11,64]{2,0,1:T(2,128)}, u32[]{:S(2)}) copy-start(f32[2,11,64]{2,0,1:T(2,128)} %param.33) | copy-start | bytes 16900
  435.5 137.5 %copy-start.49 = (f32[11,64]{1,0:T(8,128)S(1)}, f32[11,64]{1,0:T(8,128)}, u32[]{:S(2)}) copy-start(f32[11,64]{1,0:T(8,128)} %param.26) | copy-start | bytes 8452
  580.9 2.5 copy-start.36
  580.9 2.9 copy-start.51
  590.9 2.5 copy-start.61
  590.9 4.1 copy-start.37
  590.9 4.2 copy-start.39
  593.4 3.1 copy-start.29
  595.1 4.7 copy-start.40
  596.7 0.7 copy-start.31
  597.4 12.1 %copy-start.8 = (f32[788,512]{1,0:T(8,128)S(1)}, f32[788,512]{1,0:T(8,128)}, u32[]{:S(2)}) copy-start(f32[788,512]{1,0:T(8,128)} %copy-done.7) | copy-start | bytes 4841476
  597.4 12.1 %copy-start.14 = (bf16[788,512]{1,0:T(8,128)(2,1)S(1)}, bf16[788,512]{1,0:T(8,128)(2,1)}, u32[]{:S(2)}) copy-start(bf16[788,512]{1,0:T(8,128)(2,1)} %param.18) | copy-start | bytes 2420740
  606.0 6.6 %copy-start.56 = (f32[4,256]{1,0:T(4,128)}, f32[4,256]{1,0:T(4,128)S(1)}, u32[]{:S(2)}) copy-start(f32[4,256]{1,0:T(4,128)S(1)} %reshape.345) | copy-start | bytes 12292
  609.5 3.1 copy-start.21
  612.6 2.3 copy-start.20
  (2 other events, 1.2 us)

commit v6 on v5

--- a/solution.py
+++ b/solution.py
@@ -473,6 +473,7 @@
 
 
 TILE = 128
+TILE_B = 256
 CAPP = 512
 SQRT_HALF = float(np.sqrt(0.5))
 INV_SQRT_2PI = float(1.0 / np.sqrt(2.0 * np.pi))
@@ -532,14 +533,14 @@
     )(counts, table_in, w1, b1, w2, b2)
 
 
-def ffn_bwd_kernel(micro, counts, dy_ref, x_ref, hp_ref, h_ref, w1_ref, w2_ref, dt_ref, gu_ref, gd_ref, gb_ref):
+def ffn_bwd_kernel(micro, counts, dy_ref, x_ref, hp_ref, h_ref, w1_ref, w2_ref, dt_ref, gu_ref, gd_ref, gb_ref, gu_acc, gd_acc):
     e, m, t = pl.program_id(0), pl.program_id(1), pl.program_id(2)
-    active = t * TILE < counts[e * micro + m]
+    active = t * TILE_B < counts[e * micro + m]
 
     @pl.when((m == 0) & (t == 0))
     def _():
-        gu_ref[...] = jnp.zeros(gu_ref.shape, F32)
-        gd_ref[...] = jnp.zeros(gd_ref.shape, F32)
+        gu_acc[...] = jnp.zeros(gu_acc.shape, F32)
+        gd_acc[...] = jnp.zeros(gd_acc.shape, F32)
         gb_ref[...] = jnp.zeros(gb_ref.shape, F32)
 
     @pl.when(active)
@@ -550,17 +551,22 @@
         slope = 0.5 * (1.0 + lax.erf(hp * SQRT_HALF)) + hp * jnp.exp(-0.5 * hp * hp) * INV_SQRT_2PI
         d_pre = (d_hidden * slope).astype(BF16)
         dt_ref[0] = lax.dot_general(d_pre, w1_ref[0], (((1,), (1,)), ((), ())), preferred_element_type=F32)
-        gu_ref[0] += lax.dot_general(x_ref[0], d_pre, (((0,), (0,)), ((), ())), preferred_element_type=F32)
-        gd_ref[0] += lax.dot_general(h_ref[0], dy, (((0,), (0,)), ((), ())), preferred_element_type=F32)
+        gu_acc[...] += lax.dot_general(x_ref[0], d_pre, (((0,), (0,)), ((), ())), preferred_element_type=F32)
+        gd_acc[...] += lax.dot_general(h_ref[0], dy, (((0,), (0,)), ((), ())), preferred_element_type=F32)
         gb_ref[0] += jnp.sum(d_pre.astype(F32), 0, keepdims=True)
 
     @pl.when(jnp.logical_not(active))
     def _():
         dt_ref[0] = jnp.zeros(dt_ref.shape[1:], F32)
 
+    @pl.when((m == micro - 1) & (t == pl.num_programs(2) - 1))
+    def _():
+        gu_ref[0] = gu_acc[...].astype(BF16)
+        gd_ref[0] = gd_acc[...].astype(BF16)
+
 
 def ffn_backward(counts, d_expert, table_in, hp, h, w1, w2, micro):
-    tiles = CAPP // TILE
+    tiles = CAPP // TILE_B
     rows = table_in.shape[1]
     row_map = lambda e, m, t, c: (e, m * tiles + t, 0)
     w_map = lambda e, m, t, c: (e, 0, 0)
@@ -568,19 +574,20 @@
         num_scalar_prefetch=1,
         grid=(E, micro, tiles),
         in_specs=[
-            pl.BlockSpec((1, TILE, D), row_map),
-            pl.BlockSpec((1, TILE, D), row_map),
-            pl.BlockSpec((1, TILE, F), row_map),
-            pl.BlockSpec((1, TILE, F), row_map),
+            pl.BlockSpec((1, TILE_B, D), row_map),
+            pl.BlockSpec((1, TILE_B, D), row_map),
+            pl.BlockSpec((1, TILE_B, F), row_map),
+            pl.BlockSpec((1, TILE_B, F), row_map),
             pl.BlockSpec((1, D, F), w_map),
             pl.BlockSpec((1, F, D), w_map),
         ],
         out_specs=[
-            pl.BlockSpec((1, TILE, D), row_map),
+            pl.BlockSpec((1, TILE_B, D), row_map),
             pl.BlockSpec((1, D, F), w_map),
             pl.BlockSpec((1, F, D), w_map),
             pl.BlockSpec((1, 1, F), w_map),
         ],
+        scratch_shapes=[pltpu.VMEM((D, F), F32), pltpu.VMEM((F, D), F32)],
     )
     work = E * rows
     return pl.pallas_call(
@@ -588,16 +595,15 @@
         grid_spec=grid_spec,
         out_shape=[
             jax.ShapeDtypeStruct((E, rows, D), F32),
-            jax.ShapeDtypeStruct((E, D, F), F32),
-            jax.ShapeDtypeStruct((E, F, D), F32),
+            jax.ShapeDtypeStruct((E, D, F), BF16),
+            jax.ShapeDtypeStruct((E, F, D), BF16),
             jax.ShapeDtypeStruct((E, 1, F), F32),
         ],
-        compiler_params=pltpu.CompilerParams(vmem_limit_bytes=56 * 1024 * 1024),
+        compiler_params=pltpu.CompilerParams(vmem_limit_bytes=60 * 1024 * 1024),
         cost_estimate=pl.CostEstimate(
-            flops=8 * work * D * F // 2, bytes_accessed=work * (8 * D + 6 * F) // 2 + 32 * E * D * F, transcendentals=2 * work * F // 2
+            flops=8 * work * D * F // 2, bytes_accessed=work * (8 * D + 6 * F) // 2 + 16 * E * D * F, transcendentals=2 * work * F // 2
         ),
     )(counts, d_expert, table_in, hp, h, w1, w2)
-
 
 def layer_norm(value, gain, shift):
     center = value - jnp.mean(value, -1, keepdims=True)
@@ -817,7 +823,7 @@
     width = dense_g.shape[1]
     dense_g = jnp.pad(dense_g, ((0, 0), (0, DENSE_AG - width))).astype(BF16)
     x_pair = lax.axis_size("rx") == 2
-    r_up, r_down, r_dense = grad_reduce(g_up.astype(BF16), g_down.astype(BF16), dense_g, group_size, x_pair, 0)
+    r_up, r_down, r_dense = grad_reduce(g_up, g_down, dense_g, group_size, x_pair, 0)
     if not x_pair:
         r_up, r_down, r_dense = lax.psum((r_up, r_down, r_dense), "rx")
     r_qkv, r_out, r_router, r_table, r_ub = unpack_dense(r_dense[:, :width])

time: 628 us -> 583 us (0.928)
  Pallas kernels: 358 us -> 334 us
  other arithmetic: 92.1 us -> 73.7 us
    pallas_call x1, Pallas kernels: 80.6 us -> 58.2 us  [ffn_backward(): pl.pallas_call(functools.partial(ffn_bwd_kernel, micro), grid_spec=grid_s...]
    convert_element_type x2 -> x0, other arithmetic: 18 us -> none  [the longest x1 9.08 us: shards(): g_up.astype(BF16)]
    unnamed x145 -> x159, local copies, waits for them, and re-layouts: 23.1 us -> 22.4 us
where the time goes in v6:
time: 583 us; the launch traced here: 573 us
  Pallas kernels  334 us (57%)
  local copies, waits for them, and re-layouts  95 us (16%)
  other arithmetic  73.7 us (13%)
  matrix products  68.2 us (12%)
    pallas_call x1, Pallas kernels, grad_reduce(): pl.pallas_call(functools.partial(ring_rs2_kernel, groups, x_pair), out_sh...  136 us
    pallas_call x1, Pallas kernels, ring_all_gather(): pl.pallas_call(functools.partial(ring_ag_kernel, groups), out_shape=shape...  101 us
    pallas_call x1, Pallas kernels, ffn_backward(): pl.pallas_call(functools.partial(ffn_bwd_kernel, micro), grid_spec=grid_s...  58.2 us
    pallas_call x1, Pallas kernels, ffn_forward(): pl.pallas_call(functools.partial(ffn_fwd_kernel, micro), grid_spec=grid_s...  39.3 us
    another operation x15, other arithmetic, adamw(): return (weight - rate * (update + 0.1 * weight), jnp.stack([first, root]))  26 us
    unnamed x159, local copies, waits for them, and re-layouts  22.4 us
    dot_general x2, matrix products, pick_rows(): jnp.einsum('mnr,mrd->mnd', onehot, hi_lo(table), preferred_element_type=F32)  16.1 us
    convert_element_type x2, other arithmetic, hi_lo(): lo = (v - hi.astype(F32)).astype(BF16)  11.9 us

profile of v6, /device:TPU:1, one launch (start us, length us, event | category | flops | bytes accessed | tf_op | source)
XLA Modules:
  0.0 573.2 jit_solution(14450135535199763703)
XLA Ops:
  0.7 2.9 convert_element_type.126.refs_0_
  6.2 101.1 %shard_map.344 = (bf16[4,512,2048]{2,1,0:T(8,128)(2,1)}, bf16[4,2048,512]{2,1,0:T(8,128)(2,1)}, bf16[512,2560]{1,0:T(8,128)(2,1)}) custom-call(bf16[4,64,2048]{2,1,0:T(8,128)(2,1)} %convert_element_type.126.refs_0_, bf16[4,256,512]{2,1,0:T(8,128)(2,1)} %convert_element_type.127.refs_1_, bf16[64,2560]{1,0:T(8,128)(2,1)} %pad.14.refs_2_), custom_call_target="tpu_custom_call" | custom-call | bytes 19398656 | tf_op jit(solution)/shard_map/pallas_call | solution.py:271
  107.3 4.5 copy.278
  115.0 3.0 add_convert_fusion
  118.0 1.3 fusion.113
  121.2 3.5 reshape.353
  124.8 2.0 copy.283
  128.0 1.3 fusion.16
  129.3 1.5 copy-done.2
  131.6 1.2 copy.284
  132.8 4.8 fusion.57
  139.3 2.1 fusion.117
  142.2 1.4 fusion.118
  144.1 2.3 reduce-window.6
  147.3 5.9 %fusion.18 = bf16[2,2048,512]{2,1,0:T(8,128)(2,1)S(1)} fusion(s32[2,788]{1,0:T(2,128)S(1)} %multiply_add_fusion.6, bf16[2,394,512]{2,1,0:T(8,128)(2,1)S(1)} %reshape.321), kind=kOutput, calls=%fused_computation.33 | convolution fusion | flops 3313664000 | bytes 5007520 | tf_op jit(solution)/shard_map/mnr,mnd->mrd/dot_general | solution.py:776
  153.3 2.5 copy.288
  159.0 2.2 copy-done
  161.2 39.3 %shard_map.345 = (f32[4,1024,2048]{2,1,0:T(8,128)}, bf16[4,1024,2048]{2,1,0:T(8,128)(2,1)}, f32[4,1024,512]{2,1,0:T(8,128)}) custom-call(s32[8]{0:T(128)S(1)} %reshape.320.counts, bf16[4,1024,512]{2,1,0:T(8,128)(2,1)S(1)} %bitcast.213, bf16[4,512,2048]{2,1,0:T(8,128)(2,1)} %get-tuple-element.37.w1_ref, f32[4,1,2048]{2,1,0:T(1,128)S(1)} %reshape.350.b1_ref, ...), custom_call_target="tpu_custom_call" | custom-call | flops 8589934592 | bytes 31457280 | tf_op jit(solution)/shard_map/pallas_call | solution.py:521
  200.4 5.1 copy.292
  205.5 6.0 %fusion.12 = (bf16[2,2048,512]{2,1,0:T(8,128)(2,1)}, bf16[2,2048,512]{2,1,0:T(8,128)(2,1)}) fusion(f32[2,4,512,512]{3,2,1,0:T(8,128)S(1)} %copy.292), kind=kLoop, calls=%fused_computation.17 | loop fusion | flops 8388608 | bytes 16777216 | tf_op jit(solution)/shard_map/convert_element_type | solution.py:636
  211.5 9.4 %fusion.2 = f32[2,788,1024]{2,1,0:T(8,128)S(1)} fusion(bf16[2,2048,512]{2,1,0:T(8,128)(2,1)} %get-tuple-element.191, bf16[2,2048,512]{2,1,0:T(8,128)(2,1)} %get-tuple-element.192, s32[2,788]{1,0:T(2,128)S(1)} %multiply_add_fusion.6), kind=kOutput, calls=%fused_computation.3 | convolution fusion | flops 6630227968 | bytes 14850208 | tf_op jit(solution)/shard_map/mnr,mrd->mnd/dot_general | solution.py:641
  221.7 2.1 fusion.112
  223.8 1.6 reshape.326
  225.4 2.7 reshape.327
  228.2 2.1 multiply_reduce_fusion.5
  230.5 2.5 reshape.329
  233.0 1.7 multiply_convert_fusion.4
  234.7 6.0 %fusion.19 = bf16[2,2048,512]{2,1,0:T(8,128)(2,1)S(1)} fusion(s32[2,788]{1,0:T(2,128)S(1)} %multiply_add_fusion.6, bf16[2,394,512]{2,1,0:T(8,128)(2,1)S(1)} %get-tuple-element.205, bf16[2,394,512]{2,1,0:T(8,128)(2,1)S(1)} %get-tuple-element.204), kind=kOutput, calls=%fused_computation.34 | convolution fusion | flops 3313664000 | bytes 5814432 | tf_op jit(solution)/shard_map/mnr,mnd->mrd/dot_general | solution.py:792
  240.7 2.8 copy.293
  243.9 58.2 %shard_map.346 = (f32[4,1024,512]{2,1,0:T(8,128)}, bf16[4,512,2048]{2,1,0:T(8,128)(2,1)}, bf16[4,2048,512]{2,1,0:T(8,128)(2,1)}, f32[4,1,2048]{2,1,0:T(1,128)}) custom-call(s32[8]{0:T(128)} %copy-done.1, bf16[4,1024,512]{2,1,0:T(8,128)(2,1)} %bitcast.216, bf16[4,1024,512]{2,1,0:T(8,128)(2,1)} %bitcast.212, f32[4,1024,2048]{2,1,0:T(8,128)} %get-tuple-element.40.hp_ref, ...), custom_call_target="tpu_custom_call" | custom-call | flops 17179869184 | bytes 100663296 | tf_op jit(solution)/shard_map/pallas_call | solution.py:593
  302.1 5.1 copy.294
  307.2 5.8 %fusion.11 = (bf16[2,2048,512]{2,1,0:T(8,128)(2,1)}, bf16[2,2048,512]{2,1,0:T(8,128)(2,1)}) fusion(f32[2,4,512,512]{3,2,1,0:T(8,128)S(1)} %copy.294), kind=kLoop, calls=%fused_computation.14 | loop fusion | flops 8388608 | bytes 16777216 | tf_op jit(solution)/shard_map/convert_element_type | solution.py:636
  315.2 6.8 %fusion.7 = f32[2,394,1024]{2,1,0:T(8,128)} fusion(bf16[2,2048,512]{2,1,0:T(8,128)(2,1)S(1)} %copy-done.25, bf16[2,2048,512]{2,1,0:T(8,128)(2,1)} %get-tuple-element.190, bf16[2,788,2048]{2,1,0:T(8,128)(2,1)S(1)} %fusion.1), kind=kOutput, calls=%fused_computation.8 | convolution fusion | flops 3323502592 | bytes 18169856 | tf_op jit(solution)/shard_map/mnr,mrd->mnd/dot_general | solution.py:641
  322.0 3.4 slice_add_fusion.3
  325.4 2.8 reshape.334
  328.2 2.6 multiply_reduce_fusion.2
  330.9 1.7 fusion.111
  332.6 1.2 copy-done.7
  334.9 1.7 convolution_convert_fusion.1
  338.5 4.2 fusion.54
  342.7 1.8 copy.306
  344.4 3.6 reshape.338
  348.1 7.8 %multiply_reduce_fusion = (f32[4,8,197]{2,1,0:T(8,128)S(1)}, f32[4,8,197,197]{2,3,1,0:T(8,128)}) fusion(f32[4,8,197,197]{2,3,1,0:T(8,128)} %copy-done.2, f32[4,8,197]{2,1,0:T(8,128)S(1)} %log_add_fusion, bf16[4,197,8,64]{1,3,2,0:T(8,128)(2,1)S(1)} %copy.296, bf16[4,197,8,64]{1,3,2,0:T(8,128)(2,1)} %copy-done.26), kind=kOutput, calls=%fused_computation.19 | convolution fusion | flops 163922912 | bytes 11599360 | tf_op jit(solution)/shard_map/bqhd,bkhd->bhqk/dot_general | solution.py:702
  355.9 4.5 multiply_convert_fusion
  360.4 1.2 fusion.59
  363.7 2.7 fusion.58
  372.4 2.0 fusion.108
  374.4 1.5 fusion.38
  378.1 1.5 convolution_convert_fusion.2
  380.1 4.1 convolution_convert_fusion
  384.3 1.1 reshape_squeeze.4
  385.8 4.6 concatenate.54
  390.4 3.3 pad.16.refs_2_
  393.7 135.7 %shard_map.347 = (f32[4,64,2048]{2,1,0:T(8,128)}, f32[4,256,512]{2,1,0:T(8,128)}, f32[64,2560]{1,0:T(8,128)}) custom-call(bf16[4,512,2048]{2,1,0:T(8,128)(2,1)} %get-tuple-element.43.refs_0_, bf16[4,2048,512]{2,1,0:T(8,128)(2,1)} %get-tuple-element.44.refs_1_, bf16[512,2560]{1,0:T(8,128)(2,1)} %pad.16.refs_2_), custom_call_target="tpu_custom_call" | custom-call | flops 9699328 | bytes 19398656 | tf_op jit(solution)/shard_map/pallas_call | solution.py:462
  531.4 6.2 %fusion.62 = (f32[1,4,256,512]{3,2,1,0:T(8,128)S(1)}, f32[1,4,256,512]{3,2,1,0:T(8,128)S(1)}, f32[4,256,512]{2,1,0:T(8,128)}) fusion(f32[4,256,512]{2,1,0:T(8,128)} %get-tuple-element.275, f32[2,4,256,512]{3,2,1,0:T(8,128)} %param.32, f32[4,256,512]{2,1,0:T(8,128)} %param.25), kind=kLoop, calls=%fused_computation.112 | loop fusion | flops 6815744 | bytes 14680064 | tf_op jit(solution)/shard_map/stack | solution.py:723
  537.7 2.5 pad_maximum_fusion.1
  541.1 6.5 %fusion.61 = (f32[1,4,64,2048]{3,2,1,0:T(8,128)S(1)}, f32[1,4,64,2048]{3,2,1,0:T(8,128)S(1)}, f32[4,64,2048]{2,1,0:T(8,128)}) fusion(f32[4,64,2048]{2,1,0:T(8,128)} %get-tuple-element.273, f32[2,4,64,2048]{3,2,1,0:T(8,128)} %param.30, f32[4,64,2048]{2,1,0:T(8,128)} %param.23), kind=kLoop, calls=%fused_computation.111 | loop fusion | flops 6815744 | bytes 14680064 | tf_op jit(solution)/shard_map/stack | solution.py:723
  547.7 2.5 pad_maximum_fusion
  554.1 2.4 fusion.76
  561.2 1.4 copy.328
  562.8 1.3 multiply_subtract_fusion.5
  566.3 3.1 add_add_fusion.2
  569.4 1.3 copy.353
  571.7 1.3 copy.354
  (279 shorter events, 49.4 us)
Async XLA Ops:
  0.7 2.9 copy-start.19
  3.5 1.6 copy-start.41
  3.5 1.6 copy-start.58
  3.6 1.7 copy-start.65
  107.3 6.4 %copy-start.11 = (bf16[788,512]{1,0:T(8,128)(2,1)S(1)}, bf16[788,512]{1,0:T(8,128)(2,1)}, u32[]{:S(2)}) copy-start(bf16[788,512]{1,0:T(8,128)(2,1)} %param.17) | copy-start | bytes 2420740
  113.7 1.3 copy-start.63
  113.7 1.3 copy-start.70
  113.7 28.1 %copy-start.56 = (f32[1,512]{1,0:T(1,128)}, f32[1,512]{1,0:T(1,128)S(1)}, u32[]{:S(2)}) copy-start(f32[1,512]{1,0:T(1,128)S(1)} %get-tuple-element.218) | copy-start | bytes 6148
  114.0 4.0 copy-start.45
  115.0 3.0 copy-start.51
  121.2 5.6 copy-start.17
  127.9 2.8 copy-start.2
  128.0 2.8 copy-start.29
  132.8 4.8 copy-start.26
  139.3 2.1 copy-start.33
  141.8 2.0 copy-start.62
  142.2 11.1 %copy-start.9 = (bf16[788,512]{1,0:T(8,128)(2,1)}, bf16[788,512]{1,0:T(8,128)(2,1)S(1)}, u32[]{:S(2)}) copy-start(bf16[788,512]{1,0:T(8,128)(2,1)S(1)} %add_convert_fusion.2) | copy-start | bytes 2420740
  155.9 44.5 %copy-start.1 = (s32[8]{0:T(128)}, s32[8]{0:T(128)S(1)}, u32[]{:S(2)}) copy-start(s32[8]{0:T(128)S(1)} %reshape.320.counts) | copy-start | bytes 100
  159.0 2.2 copy-start
  240.7 3.3 copy-start.4
  313.0 2.2 copy-start.25
  325.4 2.8 copy-start.57
  328.2 2.6 copy-start.6
  330.8 2.9 copy-start.13
  332.6 1.5 copy-start.54
  344.4 11.4 %slice-start = ((s8[6553600]{0:T(1024)(128)(4,1)}), s8[2359296]{0:T(1024)(128)(4,1)S(1)}, s32[]{:S(2)}) async-start(s8[6553600]{0:T(1024)(128)(4,1)} %bitcast.214), calls=%async_computation | async-start | bytes 4718592
  348.1 7.8 %slice-start.1 = ((s8[6553600]{0:T(1024)(128)(4,1)}), s8[4194304]{0:T(1024)(128)(4,1)S(1)}, s32[]{:S(2)}) async-start(s8[6553600]{0:T(1024)(128)(4,1)} %bitcast.214), calls=%async_computation.1 | async-start | bytes 8388608
  355.9 4.5 copy-start.18
  360.4 1.7 copy-start.3
  362.1 1.7 copy-start.16
  368.1 1.2 copy-start.27
  369.4 1.5 copy-start.23
  369.8 1.7 copy-start.12
  369.8 2.6 copy-start.28
  369.8 2.6 copy-start.46
  369.8 2.6 copy-start.64
  372.4 2.0 copy-start.48
  372.4 2.0 copy-start.52
  372.4 3.6 copy-start.5
  374.3 1.6 copy-start.22
  374.4 1.5 copy-start.49
  375.9 2.2 copy-start.34
  376.0 2.2 copy-start.36
  378.1 2.0 copy-start.24
  380.1 4.1 copy-start.60
  380.1 5.7 copy-start.39
  380.1 5.7 copy-start.40
  393.7 135.7 %copy-start.68 = (f32[2,11,64]{2,0,1:T(2,128)S(1)}, f32[2,11,64]{2,0,1:T(2,128)}, u32[]{:S(2)}) copy-start(f32[2,11,64]{2,0,1:T(2,128)} %param.33) | copy-start | bytes 16900
  393.7 136.0 %copy-start.59 = (f32[11,64]{1,0:T(8,128)S(1)}, f32[11,64]{1,0:T(8,128)}, u32[]{:S(2)}) copy-start(f32[11,64]{1,0:T(8,128)} %param.26) | copy-start | bytes 8452
  537.7 2.5 copy-start.37
  537.7 2.9 copy-start.61
  547.6 2.5 copy-start.69
  547.6 4.1 copy-start.38
  547.7 4.2 copy-start.42
  550.2 3.1 copy-start.30
  551.8 4.8 copy-start.43
  554.1 12.2 %copy-start.8 = (f32[788,512]{1,0:T(8,128)S(1)}, f32[788,512]{1,0:T(8,128)}, u32[]{:S(2)}) copy-start(f32[788,512]{1,0:T(8,128)} %copy-done.7) | copy-start | bytes 4841476
  554.1 12.2 %copy-start.14 = (bf16[788,512]{1,0:T(8,128)(2,1)S(1)}, bf16[788,512]{1,0:T(8,128)(2,1)}, u32[]{:S(2)}) copy-start(bf16[788,512]{1,0:T(8,128)(2,1)} %param.18) | copy-start | bytes 2420740
  554.1 12.2 %copy-start.50 = (f32[788]{0:T(1024)S(1)}, f32[788]{0:T(1024)}, u32[]{:S(2)}) copy-start(f32[788]{0:T(1024)} %copy-done.49) | copy-start | bytes 9460
  554.1 12.2 %copy-start.53 = (f32[788]{0:T(1024)S(1)}, f32[788]{0:T(1024)}, u32[]{:S(2)}) copy-start(f32[788]{0:T(1024)} %copy-done.51) | copy-start | bytes 9460
  554.1 12.2 %copy-start.55 = (f32[788]{0:T(1024)S(1)}, f32[788]{0:T(1024)}, u32[]{:S(2)}) copy-start(f32[788]{0:T(1024)} %copy-done.54) | copy-start | bytes 9460
  562.8 6.6 %copy-start.66 = (f32[4,256]{1,0:T(4,128)}, f32[4,256]{1,0:T(4,128)S(1)}, u32[]{:S(2)}) copy-start(f32[4,256]{1,0:T(4,128)S(1)} %reshape.345) | copy-start | bytes 12292
  566.3 3.1 copy-start.21
  569.4 2.3 copy-start.20
  (9 other events, 8.6 us)
